TPU v7x, 128 devices: a whole 4x4x4 slice. The times are simulated.
128 devices in a mesh: row: 32 (over x_hi, z, y), ch: 4 (over x_lo, core).
Axes of the slice: x: 4 (x_hi: 2, x_lo: 2; x = x_hi * 2 + x_lo), y: 4, z: 4, core: 2. Of those that a mesh axis runs over, the one named last changes fastest.
Arguments:
- pair_rep: float32 [256, 256, 128], P(('row', 'ch')), may hold values from -6 to 6
- pair_mask: int32 [256, 256], P(('row', 'ch')), may hold values from 0 to 1, as said below
- ln_in_gain: float32 [128], replicated, may hold values from 0.5 to 1.5
- ln_in_bias: float32 [128], replicated, may hold values from -3 to 3
- w_in: float32 [128, 640], replicated, may hold values from -0.5 to 0.5
- b_in: float32 [640], replicated, may hold values from -3 to 3
- ln_out_gain: float32 [128], replicated, may hold values from 0.5 to 1.5
- ln_out_bias: float32 [128], replicated, may hold values from -3 to 3
- w_out: float32 [128, 128], replicated, may hold values from -0.5 to 0.5
- b_out: float32 [128], replicated, may hold values from -3 to 3
- cotangent: float32 [256, 256, 128], P(('row', 'ch')), may hold values from -6 to 6
Outputs:
- update: float32 [256, 256, 128], P(('row', 'ch'))
- grad_pair: float32 [256, 256, 128], P(('row', 'ch'))
- grad_w_in: float32 [128, 640], replicated
- grad_w_out: float32 [128, 128], replicated
Inputs may be any that keep to these rules, and one draw needn't show every extreme that they name: pair_mask[i, k] = m_i m_k, where m is 1 for the residues present in the crop and 0 otherwise.
All inputs are finite; a program needn't handle non-finite values.
Results may differ from a plain program's by a relative error of at most 0.00009.
Values sent between devices are 32-bit elements; how exact they have to be, the bound alone decides.
No kernel may reach another device: no remote copies, remote signals or barrier semaphores. Data moves between devices by JAX's collectives and lax.ppermute only.
A program may use at most 64 MiB of HBM per device.

v0:
```python
import jax
import jax.numpy as jnp
from jax import lax
from jax.sharding import PartitionSpec as P

epsilon = 1e-05


def side_by_side(arrays, axis, split_dim, concat_dim, along):
    ends, at = ([], 0)
    for a in arrays[:-1]:
        at += a.shape[along]
        ends.append(at)
    both = jnp.concatenate(arrays, axis=along)
    return tuple(
        jnp.split(
            lax.all_to_all(both, axis, split_axis=split_dim, concat_axis=concat_dim, tiled=True),
            ends,
            axis=along,
        )
    )


def prelude(field, keep_mask, norm_gain, norm_bias, weights, offsets):
    channels = field.shape[-1]
    hidden = (weights.shape[1] - channels) // 4
    center = jnp.mean(field, -1, keepdims=True)
    spread = jnp.mean((field - center) ** 2, -1, keepdims=True)
    normed = (field - center) * lax.rsqrt(spread + epsilon) * norm_gain + norm_bias
    pieces = jnp.einsum(
        "ikc,cf->fik", normed, weights[:, : 4 * hidden], precision=lax.Precision.HIGHEST
    )
    pieces = pieces + offsets[: 4 * hidden, None, None]
    gate = jax.nn.sigmoid(
        jnp.einsum("ikc,cf->ikf", normed, weights[:, 4 * hidden :], precision=lax.Precision.HIGHEST)
        + offsets[4 * hidden :]
    )
    keep = keep_mask.astype(field.dtype)[None]
    left = keep * jax.nn.sigmoid(pieces[:hidden]) * pieces[hidden : 2 * hidden]
    right = keep * jax.nn.sigmoid(pieces[2 * hidden : 3 * hidden]) * pieces[3 * hidden :]
    return (left, right, gate)


def epilogue(product, gate, norm_gain, norm_bias, weights, offset):
    center = jnp.mean(product, 0, keepdims=True)
    spread = jnp.mean((product - center) ** 2, 0, keepdims=True)
    normed = (product - center) * lax.rsqrt(spread + epsilon) * norm_gain[
        :, None, None
    ] + norm_bias[:, None, None]
    projected = jnp.einsum("hij,hc->ijc", normed, weights, precision=lax.Precision.HIGHEST) + offset
    return gate * projected


def on_device(
    pair_rep,
    pair_mask,
    ln_in_gain,
    ln_in_bias,
    w_in,
    b_in,
    ln_out_gain,
    ln_out_bias,
    w_out,
    b_out,
    cotangent,
):
    row_count = pair_rep.shape[0]
    length = pair_rep.shape[1]
    hidden = w_out.shape[0]
    per_device = hidden // (lax.axis_size("row") * lax.axis_size("ch"))

    def local_prelude(field, weights):
        return prelude(field, pair_mask, ln_in_gain, ln_in_bias, weights, b_in)

    (left_rows, right_rows, gate), prelude_back = jax.vjp(local_prelude, pair_rep, w_in)
    row_shape = (hidden, 1, row_count, length)
    left_cols, right_cols = side_by_side(
        (left_rows.reshape(row_shape), right_rows.reshape(row_shape)), ("row", "ch"), 0, 2, 1
    )
    left_cols = left_cols.reshape(per_device, length, length)
    right_cols = right_cols.reshape(per_device, length, length)
    product = jnp.einsum("hik,hjk->hij", left_cols, right_cols, precision=lax.Precision.HIGHEST)
    product_rows = lax.all_to_all(
        product.reshape(per_device, 1, length, length),
        ("row", "ch"),
        split_axis=2,
        concat_axis=0,
        tiled=True,
    )
    product_rows = product_rows.reshape(hidden, row_count, length)

    def local_epilogue(prod_part, gate_part, weights):
        return epilogue(prod_part, gate_part, ln_out_gain, ln_out_bias, weights, b_out)

    update, epilogue_back = jax.vjp(local_epilogue, product_rows, gate, w_out)
    d_product, d_gate, d_wout = epilogue_back(cotangent)
    d_cols = lax.all_to_all(
        d_product.reshape(row_shape), ("row", "ch"), split_axis=0, concat_axis=2, tiled=True
    )
    d_cols = d_cols.reshape(per_device, length, length)
    d_left = jnp.einsum("hij,hjk->hik", d_cols, right_cols, precision=lax.Precision.HIGHEST)
    d_right = jnp.einsum("hij,hik->hjk", d_cols, left_cols, precision=lax.Precision.HIGHEST)
    col_shape = (per_device, 1, length, length)
    d_left, d_right = side_by_side(
        (d_left.reshape(col_shape), d_right.reshape(col_shape)), ("row", "ch"), 2, 0, 1
    )
    d_left = d_left.reshape(hidden, row_count, length)
    d_right = d_right.reshape(hidden, row_count, length)
    grad_pair, d_win = prelude_back((d_left, d_right, d_gate))
    d_win, d_wout = lax.psum((d_win, d_wout), ("row", "ch"))
    return (update, grad_pair, d_win / length, d_wout / length)


def solution(mesh):
    placed = (
        P(("row", "ch"), None, None),
        P(("row", "ch"), None),
        P(),
        P(),
        P(),
        P(),
        P(),
        P(),
        P(),
        P(),
        P(("row", "ch"), None, None),
    )
    return jax.shard_map(
        on_device,
        mesh=mesh,
        in_specs=placed,
        out_specs=(P(("row", "ch"), None, None), P(("row", "ch"), None, None), P(), P()),
        check_vma=False,
    )
```

profile of v0, /device:TPU:1, one launch (start us, length us, event | category | flops | bytes accessed | tf_op | source)
XLA Modules:
  0.0 247.7 jit_solution(5997997700631045639)
XLA Ops:
  7.2 0.7 convert_element_type.3
  7.9 1.1 copy.48
  9.3 0.7 copy-done.3
  10.0 1.1 fusion
  11.6 24.7 %all_to_all.54 = f32[128,2,2,256]{3,2,1,0:T(2,128)S(1)} all-to-all(f32[128,2,2,256]{3,2,1,0:T(2,128)S(1)} %copy.51), channel_id=1, replica_groups=mesh['row'=32,'ch'=4] {'row','ch'}, dimensions={0} | all-to-all | bytes 1048576 | tf_op jit(solution)/shard_map/all_to_all | solution.py:17
  36.7 0.4 fusion.51
  37.1 0.4 convolution_bitcast_fusion.2
  37.5 1.0 copy.53
  38.5 4.9 %all-to-all-start.1 = ((f32[1,1,256,256]{3,1,0,2:T(1,128)}), f32[1,1,256,256]{3,1,0,2:T(1,128)S(1)}, u32[]{:S(2)}, u32[]{:S(2)}) async-start(f32[1,1,256,256]{3,1,0,2:T(1,128)} %copy.53), calls=%async_computation.1 | async-start | bytes 524288 | tf_op jit(solution)/shard_map/all_to_all | solution.py:83
  43.4 0.7 fusion.6
  44.1 10.3 %all-to-all-done.1 = f32[1,1,256,256]{3,1,0,2:T(1,128)S(1)} async-done(((f32[1,1,256,256]{3,1,0,2:T(1,128)}), f32[1,1,256,256]{3,1,0,2:T(1,128)S(1)}, u32[]{:S(2)}, u32[]{:S(2)}) %all-to-all-start.1) | async-done | bytes 262176 | tf_op jit(solution)/shard_map/all_to_all | solution.py:83
  54.3 0.6 reduce
  55.3 0.8 copy-done.1
  56.1 0.4 multiply_reduce_fusion.1
  56.9 15.3 %all_to_all.55 = f32[128,1,2,256]{3,2,1,0:T(2,128)S(1)} all-to-all(f32[128,1,2,256]{3,2,1,0:T(2,128)S(1)} %copy.56), channel_id=1, replica_groups=mesh['row'=32,'ch'=4] {'row','ch'}, dimensions={0} | all-to-all | bytes 524288 | tf_op jit(solution)/shard_map/all_to_all | solution.py:97
  72.4 0.6 convolution_bitcast_fusion
  73.0 0.4 convolution_bitcast_fusion.1
  73.4 1.2 copy.57
  74.6 4.5 %all-to-all-start.3 = ((f32[1,2,256,256]{3,1,0,2:T(2,128)}), f32[1,2,256,256]{3,1,0,2:T(2,128)S(1)}, u32[]{:S(2)}, u32[]{:S(2)}) async-start(f32[1,2,256,256]{3,1,0,2:T(2,128)} %copy.57), calls=%async_computation.3 | async-start | bytes 1048576 | tf_op jit(solution)/shard_map/all_to_all | solution.py:17
  79.4 1.1 convolution_bitcast_fusion.4
  80.4 1.4 fusion.52
  81.8 0.5 convolution_bitcast_fusion.5
  82.3 10.3 %all-to-all-done.3 = f32[1,2,256,256]{3,1,0,2:T(2,128)S(1)} async-done(((f32[1,2,256,256]{3,1,0,2:T(2,128)}), f32[1,2,256,256]{3,1,0,2:T(2,128)S(1)}, u32[]{:S(2)}, u32[]{:S(2)}) %all-to-all-start.3) | async-done | bytes 524320 | tf_op jit(solution)/shard_map/all_to_all | solution.py:17
  93.1 0.6 copy-done.8
  93.7 0.8 convolution_bitcast_fusion.3
  94.7 1.2 fusion.7
  95.9 0.5 multiply_reduce_fusion.5
  96.5 0.7 pad_add_fusion.3
  97.3 0.8 copy.61
  98.2 140.3 %all-reduce.9.cloned.1.call-done = (f32[128,640]{1,0:T(8,128)}, f32[128,128]{1,0:T(8,128)}) async-done(((f32[128,640]{1,0:T(8,128)}, f32[128,128]{1,0:T(8,128)}), (f32[128,640]{1,0:T(8,128)}, f32[128,128]{1,0:T(8,128)})) %all-reduce.9.cloned.1.call-update) | async-done | bytes 393232 | tf_op jit(solution)/shard_map/psum | solution.py:110
  238.4 1.8 broadcast_multiply_fusion
  240.2 0.6 broadcast_multiply_fusion.1
  (54 shorter events, 3.0 us)
Async XLA Ops:
  7.2 48.1 %copy-start = (f32[128,128]{1,0:T(8,128)S(1)}, f32[128,128]{1,0:T(8,128)}, u32[]{:S(2)}) copy-start(f32[128,128]{1,0:T(8,128)} %param.19) | copy-start | bytes 196612
  7.9 1.2 copy-start.2
  9.1 1.0 copy-start.3
  9.3 0.8 slice-start
  9.3 0.7 copy-start.7
  9.3 0.7 copy-start.10
  38.5 4.9 %copy-start.6 = (f32[640]{0:T(1024)S(1)}, f32[640]{0:T(1024)}, u32[]{:S(2)}) copy-start(f32[640]{0:T(1024)} %param.16) | copy-start | bytes 7684
  38.5 15.9 %all-to-all-start.1 = ((f32[1,1,256,256]{3,1,0,2:T(1,128)}), f32[1,1,256,256]{3,1,0,2:T(1,128)S(1)}, u32[]{:S(2)}, u32[]{:S(2)}) async-start(f32[1,1,256,256]{3,1,0,2:T(1,128)} %copy.53), calls=%async_computation.1 | async-start | bytes 524288 | tf_op jit(solution)/shard_map/all_to_all | solution.py:83
  55.1 1.0 copy-start.1
  55.3 0.8 copy-start.9
  74.6 4.8 %copy-start.12 = (f32[128]{0:T(128)S(1)}, f32[128]{0:T(128)}, u32[]{:S(2)}) copy-start(f32[128]{0:T(128)} %param.18) | copy-start | bytes 1540
  74.6 18.0 %all-to-all-start.3 = ((f32[1,2,256,256]{3,1,0,2:T(2,128)}), f32[1,2,256,256]{3,1,0,2:T(2,128)S(1)}, u32[]{:S(2)}, u32[]{:S(2)}) async-start(f32[1,2,256,256]{3,1,0,2:T(2,128)} %copy.57), calls=%async_computation.3 | async-start | bytes 1048576 | tf_op jit(solution)/shard_map/all_to_all | solution.py:17
  79.1 1.3 copy-start.13
  79.1 159.3 %all-reduce.9.cloned.1.call-start = ((), (), s32[]{:S(2)}) async-start(), calls=%async_computation.4 | async-start | bytes 786432 | tf_op jit(solution)/shard_map/psum | solution.py:110
  93.1 0.7 copy-start.8
  93.1 0.7 copy-start.11
  93.7 1.0 copy-start.4
  238.4 1.8 copy-start.5
Sparse Core Ops, SparseCore 0:
  97.4 141.0 all-reduce.8
where the time goes:
time: 248 us
  waiting for transfers between devices  161 us (65%)
  blocking collectives  40 us (16%)
  between operations  14.4 us (6%)
  starting transfers between devices  9.62 us (4%)
  matrix products  8.93 us (4%)
  local copies, waits for them, and re-layouts  8.28 us (3%)
  other arithmetic  5.56 us (2%)
    psum x1, waiting for transfers between devices, on_device(): d_win, d_wout = lax.psum((d_win, d_wout), ('row', 'ch'))  140 us
    all_to_all x1, blocking collectives, side_by_side(): lax.all_to_all(both, axis, split_axis=split_dim, concat_axis=concat_dim,...  24.7 us
    all_to_all x1, blocking collectives, on_device(): lax.all_to_all(d_product.reshape(row_shape), ('row', 'ch'), split_axis=0,...  15.3 us
    all_to_all x1, waiting for transfers between devices, side_by_side(): lax.all_to_all(both, axis, split_axis=split_dim, concat_axis=concat_dim,...  10.3 us
    all_to_all x1, waiting for transfers between devices, on_device(): lax.all_to_all(product.reshape(per_device, 1, length, length), ('row', 'c...  10.3 us
  transfers between devices with their start and end apart: 3, of which 3 were waited for; matrix products, arithmetic and copies ran while one was open for 2% of the time, Pallas kernels for 0%

commit v1 on v0

--- a/solution.py
+++ b/solution.py
@@ -107,8 +107,18 @@
     d_left = d_left.reshape(hidden, row_count, length)
     d_right = d_right.reshape(hidden, row_count, length)
     grad_pair, d_win = prelude_back((d_left, d_right, d_gate))
-    d_win, d_wout = lax.psum((d_win, d_wout), ("row", "ch"))
-    return (update, grad_pair, d_win / length, d_wout / length)
+    wide = w_in.shape[1]
+    terms = jnp.concatenate([d_win, d_wout], axis=1)
+    terms = lax.all_to_all(terms, ("row", "ch"), split_axis=0, concat_axis=0, tiled=True)
+    mine = jnp.sum(terms, 0, keepdims=True) / length
+    whole = lax.all_to_all(
+        jnp.broadcast_to(mine, terms.shape),
+        ("row", "ch"),
+        split_axis=0,
+        concat_axis=0,
+        tiled=True,
+    )
+    return (update, grad_pair, whole[:, :wide], whole[:, wide:])
 
 
 def solution(mesh):

time: 248 us -> 129 us (0.52)
  waiting for transfers between devices: 161 us -> 43 us
  between operations: 14.4 us -> 1.05 us
  starting transfers between devices: 9.62 us -> 19.1 us
  local copies, waits for them, and re-layouts: 8.28 us -> 12.2 us
  other arithmetic: 5.56 us -> 2.76 us
    psum x1 -> x0, waiting for transfers between devices: 140 us -> none  [on_device(): d_win, d_wout = lax.psum((d_win, d_wout), ('row', 'ch'))]
    all_to_all x0 -> x2, waiting for transfers between devices: none -> 22.6 us  [the longest x1 11.5 us: on_device(): lax.all_to_all(terms, ('row', 'ch'), split_axis=0, concat_axis=0, tiled=T...]
    all_to_all x0 -> x2, starting transfers between devices: none -> 9.72 us  [the longest x1 4.88 us: on_device(): lax.all_to_all(terms, ('row', 'ch'), split_axis=0, concat_axis=0, tiled=T...]
    unnamed x30 -> x31, local copies, waits for them, and re-layouts: 4.38 us -> 5 us
  transfers between devices with their start and end apart: 3 -> 4, of which waited for: 3 -> 4; matrix products, arithmetic and copies ran while one was open for 2% -> 4% of each run, Pallas kernels for 0% -> 0%
where the time goes in v1:
time: 129 us
  waiting for transfers between devices  43 us (33%)
  blocking collectives  40 us (31%)
  starting transfers between devices  19.1 us (15%)
  local copies, waits for them, and re-layouts  12.2 us (9%)
  matrix products  10.4 us (8%)
  other arithmetic  2.76 us (2%)
    all_to_all x1, blocking collectives, side_by_side(): lax.all_to_all(both, axis, split_axis=split_dim, concat_axis=concat_dim,...  24.7 us
    all_to_all x1, blocking collectives, on_device(): lax.all_to_all(d_product.reshape(row_shape), ('row', 'ch'), split_axis=0,...  15.3 us
    all_to_all x1, waiting for transfers between devices, on_device(): lax.all_to_all(terms, ('row', 'ch'), split_axis=0, concat_axis=0, tiled=T...  11.5 us
    all_to_all x1, waiting for transfers between devices, on_device(): lax.all_to_all(jnp.broadcast_to(mine, terms.shape), ('row', 'ch'), split_...  11.1 us
    all_to_all x1, waiting for transfers between devices, on_device(): lax.all_to_all(product.reshape(per_device, 1, length, length), ('row', 'c...  10.3 us
    all_to_all x1, waiting for transfers between devices, side_by_side(): lax.all_to_all(both, axis, split_axis=split_dim, concat_axis=concat_dim,...  10.1 us
    unnamed x31, local copies, waits for them, and re-layouts  5 us
    all_to_all x1, starting transfers between devices, on_device(): lax.all_to_all(product.reshape(per_device, 1, length, length), ('row', 'c...  4.88 us
  transfers between devices with their start and end apart: 4, of which 4 were waited for; matrix products, arithmetic and copies ran while one was open for 4% of the time, Pallas kernels for 0%

profile of v1, /device:TPU:1, one launch (start us, length us, event | category | flops | bytes accessed | tf_op | source)
XLA Modules:
  0.0 128.7 jit_solution(5223931275819464922)
XLA Ops:
  0.6 0.7 convert_element_type.3
  1.4 1.1 copy.61
  2.8 0.7 copy-done.3
  3.5 1.1 fusion
  5.1 24.7 %all_to_all.72 = f32[128,2,2,256]{3,2,1,0:T(2,128)S(1)} all-to-all(f32[128,2,2,256]{3,2,1,0:T(2,128)S(1)} %copy.64), channel_id=1, replica_groups=mesh['row'=32,'ch'=4] {'row','ch'}, dimensions={0} | all-to-all | bytes 1048576 | tf_op jit(solution)/shard_map/all_to_all | solution.py:17
  31.0 1.0 copy.66
  31.9 4.9 %all-to-all-start.1 = ((f32[1,1,256,256]{3,1,0,2:T(1,128)}), f32[1,1,256,256]{3,1,0,2:T(1,128)S(1)}, u32[]{:S(2)}, u32[]{:S(2)}) async-start(f32[1,1,256,256]{3,1,0,2:T(1,128)} %copy.66), calls=%async_computation.1 | async-start | bytes 524288 | tf_op jit(solution)/shard_map/all_to_all | solution.py:83
  36.8 0.7 fusion.6
  37.5 10.3 %all-to-all-done.1 = f32[1,1,256,256]{3,1,0,2:T(1,128)S(1)} async-done(((f32[1,1,256,256]{3,1,0,2:T(1,128)}), f32[1,1,256,256]{3,1,0,2:T(1,128)S(1)}, u32[]{:S(2)}, u32[]{:S(2)}) %all-to-all-start.1) | async-done | bytes 262176 | tf_op jit(solution)/shard_map/all_to_all | solution.py:83
  47.8 0.6 reduce.1
  48.8 0.8 copy-done.1
  50.3 15.3 %all_to_all.73 = f32[128,1,2,256]{3,2,1,0:T(2,128)S(1)} all-to-all(f32[128,1,2,256]{3,2,1,0:T(2,128)S(1)} %copy.69), channel_id=1, replica_groups=mesh['row'=32,'ch'=4] {'row','ch'}, dimensions={0} | all-to-all | bytes 524288 | tf_op jit(solution)/shard_map/all_to_all | solution.py:97
  65.8 0.6 convolution_bitcast_fusion
  66.9 1.2 copy.70
  68.1 4.5 %all-to-all-start.3 = ((f32[1,2,256,256]{3,1,0,2:T(2,128)}), f32[1,2,256,256]{3,1,0,2:T(2,128)S(1)}, u32[]{:S(2)}, u32[]{:S(2)}) async-start(f32[1,2,256,256]{3,1,0,2:T(2,128)} %copy.70), calls=%async_computation.3 | async-start | bytes 1048576 | tf_op jit(solution)/shard_map/all_to_all | solution.py:17
  72.6 1.3 convolution_bitcast_fusion.4
  73.9 1.4 %fusion.52 = (f32[2,256,128]{2,1,0:T(8,128)}, f32[2,256,128]{2,1,0:T(8,128)S(1)}) fusion(f32[2,256,128]{2,1,0:T(8,128)S(1)} %fusion.6, f32[128]{0:T(128)S(1)} %copy-done.13, f32[128,128]{1,0:T(8,128)S(1)} %copy-done, f32[128]{0:T(128)S(1)} %copy-done.12, f32[128]{0:T(128)S(1)} %copy-done.9, f32[2,256]{1,0:T(2,128)S(1)} %get-tuple-element.33, ...), kind=kOutput, calls=%fused_computation.98 | convolution fusion | flops 101056512 | bytes 1119744 | tf_op jit(solution)/shard_map/jvp(hij,hc->ijc)/dot_general | solution.py:50
  75.3 0.6 convolution_bitcast_fusion.5
  75.9 10.1 %all-to-all-done.3 = f32[1,2,256,256]{3,1,0,2:T(2,128)S(1)} async-done(((f32[1,2,256,256]{3,1,0,2:T(2,128)}), f32[1,2,256,256]{3,1,0,2:T(2,128)S(1)}, u32[]{:S(2)}, u32[]{:S(2)}) %all-to-all-start.3) | async-done | bytes 524320 | tf_op jit(solution)/shard_map/all_to_all | solution.py:17
  86.6 0.6 copy-done.8
  87.2 1.9 %convolution_bitcast_fusion.3 = f32[128,512]{0,1:T(8,128)S(1)} fusion(f32[128,2,256]{0,2,1:T(8,128)S(1)} %get-tuple-element.25, f32[128,2,256]{0,2,1:T(8,128)S(1)} %get-tuple-element.27, f32[128,2,256]{0,2,1:T(8,128)S(1)} %get-tuple-element.26, f32[128,2,256]{0,2,1:T(8,128)S(1)} %get-tuple-element.24, f32[2,256,128]{1,2,0:T(8,128)S(1)} %copy.61, ...), kind=kOutput, calls=%fused_computation.15 | convolution fusion | flops 403701760 | bytes 1577984 | tf_op jit(solution)/shard_map/transpose(jvp(ikc,cf->fik))/dot_general | solution.py:30
  89.1 1.2 fusion.7
  90.3 0.8 copy-done.5
  91.2 1.0 copy.78
  92.2 4.9 %all-to-all-start.4 = ((f32[128,1,768]{2,1,0:T(1,128)}), f32[128,1,768]{2,1,0:T(1,128)S(1)}, u32[]{:S(2)}, u32[]{:S(2)}) async-start(f32[128,1,768]{2,1,0:T(1,128)} %copy.78), calls=%async_computation.4 | async-start | bytes 786432 | tf_op jit(solution)/shard_map/all_to_all | solution.py:112
  97.6 11.5 %all-to-all-done.4 = f32[128,1,768]{2,1,0:T(1,128)S(1)} async-done(((f32[128,1,768]{2,1,0:T(1,128)}), f32[128,1,768]{2,1,0:T(1,128)S(1)}, u32[]{:S(2)}, u32[]{:S(2)}) %all-to-all-start.4) | async-done | bytes 393248 | tf_op jit(solution)/shard_map/all_to_all | solution.py:112
  109.4 0.9 broadcast_in_dim.8
  110.4 4.8 %all-to-all-start.5 = ((f32[128,1,768]{2,1,0:T(1,128)}), f32[128,1,768]{2,1,0:T(1,128)S(1)}, u32[]{:S(2)}, u32[]{:S(2)}) async-start(f32[128,1,768]{2,1,0:T(1,128)} %broadcast_in_dim.8), calls=%async_computation.5 | async-start | bytes 786432 | tf_op jit(solution)/shard_map/all_to_all | solution.py:114
  115.3 0.8 copy.79
  116.1 11.1 %all-to-all-done.5 = f32[128,1,768]{2,1,0:T(1,128)S(1)} async-done(((f32[128,1,768]{2,1,0:T(1,128)}), f32[128,1,768]{2,1,0:T(1,128)S(1)}, u32[]{:S(2)}, u32[]{:S(2)}) %all-to-all-start.5) | async-done | bytes 393248 | tf_op jit(solution)/shard_map/all_to_all | solution.py:114
  127.3 0.6 slice.45
  127.9 0.7 slice.44
  (61 shorter events, 5.0 us)
Async XLA Ops:
  0.6 48.1 %copy-start = (f32[128,128]{1,0:T(8,128)S(1)}, f32[128,128]{1,0:T(8,128)}, u32[]{:S(2)}) copy-start(f32[128,128]{1,0:T(8,128)} %param.19) | copy-start | bytes 196612
  1.4 1.2 copy-start.2
  2.5 1.0 copy-start.3
  2.8 0.8 slice-start
  2.8 0.7 copy-start.7
  2.8 0.7 copy-start.10
  31.9 4.9 %copy-start.6 = (f32[640]{0:T(1024)S(1)}, f32[640]{0:T(1024)}, u32[]{:S(2)}) copy-start(f32[640]{0:T(1024)} %param.16) | copy-start | bytes 7684
  31.9 15.9 %all-to-all-start.1 = ((f32[1,1,256,256]{3,1,0,2:T(1,128)}), f32[1,1,256,256]{3,1,0,2:T(1,128)S(1)}, u32[]{:S(2)}, u32[]{:S(2)}) async-start(f32[1,1,256,256]{3,1,0,2:T(1,128)} %copy.66), calls=%async_computation.1 | async-start | bytes 524288 | tf_op jit(solution)/shard_map/all_to_all | solution.py:83
  48.6 1.0 copy-start.1
  48.7 0.8 copy-start.9
  68.0 4.5 %copy-start.12 = (f32[128]{0:T(128)S(1)}, f32[128]{0:T(128)}, u32[]{:S(2)}) copy-start(f32[128]{0:T(128)} %param.18) | copy-start | bytes 1540
  68.1 18.0 %all-to-all-start.3 = ((f32[1,2,256,256]{3,1,0,2:T(2,128)}), f32[1,2,256,256]{3,1,0,2:T(2,128)S(1)}, u32[]{:S(2)}, u32[]{:S(2)}) async-start(f32[1,2,256,256]{3,1,0,2:T(2,128)} %copy.70), calls=%async_computation.3 | async-start | bytes 1048576 | tf_op jit(solution)/shard_map/all_to_all | solution.py:17
  72.6 1.3 %copy-start.13 = (f32[128]{0:T(128)S(1)}, f32[128]{0:T(128)}, u32[]{:S(2)}) copy-start(f32[128]{0:T(128)} %param.20) | copy-start | bytes 1540
  86.5 0.7 copy-start.8
  86.5 0.7 copy-start.11
  87.2 1.9 %copy-start.4 = (f32[128,640]{1,0:T(8,128)S(1)}, f32[128,640]{1,0:T(8,128)}, u32[]{:S(2)}) copy-start(f32[128,640]{1,0:T(8,128)} %param.15) | copy-start | bytes 983044
  90.3 0.8 copy-start.5
  92.2 16.9 %all-to-all-start.4 = ((f32[128,1,768]{2,1,0:T(1,128)}), f32[128,1,768]{2,1,0:T(1,128)S(1)}, u32[]{:S(2)}, u32[]{:S(2)}) async-start(f32[128,1,768]{2,1,0:T(1,128)} %copy.78), calls=%async_computation.4 | async-start | bytes 786432 | tf_op jit(solution)/shard_map/all_to_all | solution.py:112
  110.4 16.9 %all-to-all-start.5 = ((f32[128,1,768]{2,1,0:T(1,128)}), f32[128,1,768]{2,1,0:T(1,128)S(1)}, u32[]{:S(2)}, u32[]{:S(2)}) async-start(f32[128,1,768]{2,1,0:T(1,128)} %broadcast_in_dim.8), calls=%async_computation.5 | async-start | bytes 786432 | tf_op jit(solution)/shard_map/all_to_all | solution.py:114

commit v2 on v0

v2 whole, which is shorter than its diff:
```python
import functools

import jax
import jax.numpy as jnp
from jax import lax
from jax.experimental import pallas as pl
from jax.experimental.pallas import tpu as pltpu
from jax.sharding import PartitionSpec as P

epsilon = 1e-05
LANES = 128
AXES = ("row", "ch")
F32 = jnp.float32
NN = (((1,), (0,)), ((), ()))
NT = (((1,), (1,)), ((), ()))
TN = (((0,), (0,)), ((), ()))


def mm(a, b, dims):
    return lax.dot_general(
        a, b, dims, precision=lax.Precision.HIGHEST, preferred_element_type=F32
    )


def every(start, step):
    return pl.ds(start, LANES, stride=step)


def block(b):
    return slice(b * LANES, (b + 1) * LANES)


def column(row):
    return jnp.transpose(jnp.broadcast_to(row, (LANES, LANES)))


def norm_rows(x):
    center = x - jnp.mean(x, -1, keepdims=True)
    scale = lax.rsqrt(jnp.mean(center * center, -1, keepdims=True) + epsilon)
    return center * scale, scale


def norm_cols(x):
    center = x - jnp.mean(x, 0, keepdims=True)
    scale = lax.rsqrt(jnp.mean(center * center, 0, keepdims=True) + epsilon)
    return center * scale, scale


def project(normed, w_ref, b_ref, part):
    return mm(jnp.transpose(w_ref[:, block(part)]), normed, NT) + jnp.tile(
        column(b_ref[pl.ds(part * LANES, LANES)][None]), (1, normed.shape[0] // LANES)
    )


def cell_mask(mask_ref):
    mask = mask_ref[...].astype(F32)
    return jnp.concatenate([mask[0:1], mask[1:2]], axis=1)


def first_kernel(*refs):
    arrays, out_ref, held, sems = refs[:6], refs[6], refs[7:13], refs[13]
    copies = [pltpu.make_async_copy(a, h, sems.at[n]) for n, (a, h) in enumerate(zip(arrays, held))]
    for copy in copies:
        copy.start()
    x_ref, mask_ref, g_ref, b_ref, w_ref, bin_ref = held
    for n in (0, 1, 2, 3, 5, 4):
        copies[n].wait()
    hat, _ = norm_rows(x_ref[...])
    normed = hat * g_ref[...] + b_ref[...]
    mask = cell_mask(mask_ref)
    for side in range(2):
        value = (
            mask
            * jax.nn.sigmoid(project(normed, w_ref, bin_ref, 2 * side))
            * project(normed, w_ref, bin_ref, 2 * side + 1)
        )
        for b in range(4):
            out_ref[every(4 * side + b, 8), :] = value[:, block(b)]


def side_kernel(
    x_ref, mask_ref, g_ref, b_ref, w_ref, bin_ref, cot_ref, wout_ref, gout_ref,
    normed_ref, factor_ref, gate_ref, back_ref, cg_ref,
):
    hat, _ = norm_rows(x_ref[...])
    normed = hat * g_ref[...] + b_ref[...]
    normed_ref[...] = normed
    mask = cell_mask(mask_ref)
    for side in range(2):
        sig = jax.nn.sigmoid(project(normed, w_ref, bin_ref, 2 * side))
        value = project(normed, w_ref, bin_ref, 2 * side + 1)
        open_part = mask * sig
        factor_ref[block(2 * side), :] = open_part * (1.0 - sig) * value
        factor_ref[block(2 * side + 1), :] = open_part
    gate = jax.nn.sigmoid(mm(normed, w_ref[:, block(4)], NN) + bin_ref[pl.ds(4 * LANES, LANES)][None])
    gate_ref[...] = gate
    cg_ref[...] = gate * cot_ref[...]
    gain = column(gout_ref[...])
    for q in range(4):
        part = cg_ref[every((q // 2) * 256 + q % 2, 2), :]
        back_ref[:, block(q)] = gain * mm(wout_ref[...], part, NT)


def gather_sides(in_ref):
    sides = []
    for side in range(2):
        rows = [
            jnp.concatenate([in_ref[every(4 * side + 2 * r + h, 8), :] for h in range(2)], axis=1)
            for r in range(2)
        ]
        sides.append(jnp.concatenate(rows, axis=0))
    return sides


def product_kernel(in_ref, out_ref):
    left, right = gather_sides(in_ref)
    product = mm(left, right, NT)
    for q in range(4):
        out_ref[every(q, 4), :] = product[block(q // 2), block(q % 2)]


def middle_kernel(in_ref, back_ref, out_ref):
    for q in range(4):
        hat, scale = norm_cols(in_ref[every(q, 4), :])
        back = back_ref[:, block(q)]
        first = jnp.mean(back, 0, keepdims=True)
        second = jnp.mean(back * hat, 0, keepdims=True)
        out_ref[every(q, 4), :] = scale * (back - first - hat * second)


def update_kernel(
    in_ref, gate_ref, cot_ref, cg_ref, normed_ref, wout_ref, gout_ref, bout_ref, boff_ref, w_ref,
    update_ref, grads_ref, dnorm_ref,
):
    gain, bias = column(gout_ref[...]), column(boff_ref[...])
    d_wout = jnp.zeros((LANES, LANES), F32)
    d_gate_w = jnp.zeros((LANES, LANES), F32)
    for q in range(4):
        cells = every((q // 2) * 256 + q % 2, 2)
        hat, _ = norm_cols(in_ref[every(q, 4), :])
        normed_product = hat * gain + bias
        projected = mm(normed_product, wout_ref[...], TN) + bout_ref[...]
        gate = gate_ref[cells, :]
        update_ref[cells, :] = gate * projected
        d_wout += mm(normed_product, cg_ref[cells, :], NN)
        d_open = cot_ref[cells, :] * projected * gate * (1.0 - gate)
        d_gate_w += mm(normed_ref[cells, :], d_open, TN)
        dnorm_ref[cells, :] = mm(d_open, w_ref[:, block(4)], NT)
    grads_ref[block(0), :] = d_wout
    grads_ref[block(1), :] = d_gate_w


def back_product_kernel(grad_ref, in_ref, out_ref):
    left, right = gather_sides(in_ref)
    grad = jnp.concatenate(
        [
            jnp.concatenate([grad_ref[every(2 * r + c, 4), :] for c in range(2)], axis=1)
            for r in range(2)
        ],
        axis=0,
    )
    sides = (mm(grad, right, NN), mm(grad, left, TN))
    for side in range(2):
        for b in range(4):
            out_ref[every(4 * side + b, 8), :] = sides[side][block(b // 2), block(b % 2)]


def piece_grads(in_ref, factor_ref):
    parts = []
    for side in range(2):
        grad = jnp.concatenate([in_ref[every(4 * side + b, 8), :] for b in range(4)], axis=1)
        parts += [grad * factor_ref[block(2 * side + m), :] for m in range(2)]
    return jnp.concatenate(parts, axis=0)


def weight_kernel(in_ref, factor_ref, normed_ref, extra_ref, out_ref):
    terms = mm(piece_grads(in_ref, factor_ref), normed_ref[...], NN)
    for part in range(4):
        out_ref[every(part, 6), :] = terms[block(part), :]
    for part in range(2):
        out_ref[every(4 + part, 6), :] = extra_ref[block(part), :]


def pair_kernel(in_ref, factor_ref, dnorm_ref, x_ref, g_ref, w_ref, out_ref):
    grads = piece_grads(in_ref, factor_ref)
    d_normed = jnp.transpose(mm(w_ref[:, : 4 * LANES], grads, NN)) + dnorm_ref[...]
    hat, scale = norm_rows(x_ref[...])
    d_hat = d_normed * g_ref[...]
    first = jnp.mean(d_hat, -1, keepdims=True)
    second = jnp.mean(d_hat * hat, -1, keepdims=True)
    out_ref[...] = scale * (d_hat - first - hat * second)


def sum_kernel(length, in_ref, out_ref):
    terms = in_ref[...]
    total = jnp.sum(terms.reshape(LANES // 4, 24, LANES), 0)
    mine = (total[0:6] + total[6:12]) + (total[12:18] + total[18:24])
    mine = jnp.concatenate([mine] * 4, axis=0) * (1.0 / length)
    out_ref[...] = jnp.broadcast_to(mine[None], (LANES // 4, 24, LANES)).reshape(terms.shape)


def last_kernel(in_ref, win_ref, wout_ref):
    for part in range(4):
        win_ref[:, block(part)] = jnp.transpose(in_ref[every(part, 6), :])
    wout_ref[...] = in_ref[every(4, 6), :]
    win_ref[:, block(4)] = in_ref[every(5, 6), :]


def call(kernel, outs, *args):
    many = isinstance(outs, list)
    shapes = [jax.ShapeDtypeStruct(s, F32) for s in (outs if many else [outs])]
    spec = pl.BlockSpec(memory_space=pltpu.VMEM)
    return pl.pallas_call(
        kernel,
        out_shape=shapes if many else shapes[0],
        in_specs=[spec] * len(args),
        out_specs=[spec] * len(shapes) if many else spec,
        compiler_params=pltpu.CompilerParams(vmem_limit_bytes=24 * 2**20),
    )(*args)


def exchange(x):
    return lax.all_to_all(x, AXES, split_axis=0, concat_axis=0, tiled=True)


def exchange_pairs(x):
    return exchange(x.reshape(-1, 2, LANES)).reshape(x.shape)


def on_device(
    pair_rep,
    pair_mask,
    ln_in_gain,
    ln_in_bias,
    w_in,
    b_in,
    ln_out_gain,
    ln_out_bias,
    w_out,
    b_out,
    cotangent,
):
    length = pair_rep.shape[1]
    cells = pair_rep.shape[0] * length
    x = pair_rep.reshape(cells, LANES)
    cot = cotangent.reshape(cells, LANES)
    g_in, o_in = ln_in_gain[None], ln_in_bias[None]
    g_out, o_out = ln_out_gain[None], ln_out_bias[None]
    bias_out = b_out[None]

    inputs = (x, pair_mask, g_in, o_in, w_in, b_in)
    sent = pl.pallas_call(
        first_kernel,
        out_shape=jax.ShapeDtypeStruct((8 * LANES, LANES), F32),
        in_specs=[pl.BlockSpec(memory_space=pltpu.HBM)] * len(inputs),
        out_specs=pl.BlockSpec(memory_space=pltpu.VMEM),
        scratch_shapes=[pltpu.VMEM(a.shape, a.dtype) for a in inputs]
        + [pltpu.SemaphoreType.DMA((len(inputs),))],
        compiler_params=pltpu.CompilerParams(vmem_limit_bytes=24 * 2**20),
    )(*[pltpu.with_memory_space_constraint(a, pltpu.HBM) for a in inputs])
    sides = exchange(sent)
    normed, factor, gate, back, cg = call(
        side_kernel,
        [(cells, LANES), (4 * LANES, cells), (cells, LANES), (LANES, cells), (cells, LANES)],
        *inputs,
        cot,
        w_out,
        g_out,
    )
    product = exchange(call(product_kernel, (4 * LANES, LANES), sides))
    d_product = exchange(call(middle_kernel, (4 * LANES, LANES), product, back))
    update, extra, d_norm = call(
        update_kernel,
        [(cells, LANES), (2 * LANES, LANES), (cells, LANES)],
        product,
        gate,
        cot,
        cg,
        normed,
        w_out,
        g_out,
        bias_out,
        o_out,
        w_in,
    )
    d_sides = exchange(call(back_product_kernel, (8 * LANES, LANES), d_product, sides))
    terms = exchange_pairs(
        call(weight_kernel, (6 * LANES, LANES), d_sides, factor, normed, extra)
    )
    grad_pair = call(
        pair_kernel, (cells, LANES), d_sides, factor, d_norm, x, g_in, w_in
    )
    whole = exchange_pairs(
        call(functools.partial(sum_kernel, length), (6 * LANES, LANES), terms)
    )
    d_win, d_wout = call(last_kernel, [w_in.shape, w_out.shape], whole)
    return (update.reshape(pair_rep.shape), grad_pair.reshape(pair_rep.shape), d_win, d_wout)


def solution(mesh):
    placed = (
        P(("row", "ch"), None, None),
        P(("row", "ch"), None),
        P(),
        P(),
        P(),
        P(),
        P(),
        P(),
        P(),
        P(),
        P(("row", "ch"), None, None),
    )
    return jax.shard_map(
        on_device,
        mesh=mesh,
        in_specs=placed,
        out_specs=(P(("row", "ch"), None, None), P(("row", "ch"), None, None), P(), P()),
        check_vma=False,
    )
```

time: 248 us -> 118 us (0.48)
  waiting for transfers between devices: 161 us -> 26.8 us
  blocking collectives: 40 us -> 56.8 us
  Pallas kernels: 0 us -> 14 us
  between operations: 14.4 us -> 0.79 us
  matrix products: 8.93 us -> 0 us
  other arithmetic: 5.56 us -> 0 us
  starting transfers between devices: 9.62 us -> 14.2 us
  local copies, waits for them, and re-layouts: 8.28 us -> 4.5 us
    psum x1 -> x0, waiting for transfers between devices: 140 us -> none  [on_device(): d_win, d_wout = lax.psum((d_win, d_wout), ('row', 'ch'))]
    all_to_all x2 -> x3, blocking collectives: 40 us -> 56.8 us  [exchange(): return lax.all_to_all(x, AXES, split_axis=0, concat_axis=0, tiled=True)]
    pallas_call x0 -> x10, Pallas kernels: none -> 14 us  [the longest x9 11.6 us: call(): pl.pallas_call(kernel, out_shape=shapes if many else shapes[0], in_specs=...]
    dot_general x12 -> x0, matrix products: 8.93 us -> none  [the longest x3 3.05 us: prelude(): jnp.einsum('ikc,cf->fik', normed, weights[:, :4 * hidden], precision=lax....]
    all_to_all x2 -> x3, waiting for transfers between devices: 20.6 us -> 26.8 us  [exchange(): return lax.all_to_all(x, AXES, split_axis=0, concat_axis=0, tiled=True)]
    all_to_all x2 -> x3, starting transfers between devices: 9.4 us -> 14.2 us  [exchange(): return lax.all_to_all(x, AXES, split_axis=0, concat_axis=0, tiled=True)]
  transfers between devices with their start and end apart: 3 -> 3, of which waited for: 3 -> 3; matrix products, arithmetic and copies ran while one was open for 2% -> 0% of each run, Pallas kernels for 0% -> 5%
where the time goes in v2:
time: 118 us; the launch traced here: 117 us
  blocking collectives  56.8 us (48%)
  waiting for transfers between devices  26.8 us (23%)
  starting transfers between devices  14.2 us (12%)
  Pallas kernels  14 us (12%)
  local copies, waits for them, and re-layouts  4.5 us (4%)
    all_to_all x3, blocking collectives, exchange(): return lax.all_to_all(x, AXES, split_axis=0, concat_axis=0, tiled=True)  56.8 us
    all_to_all x3, waiting for transfers between devices, exchange(): return lax.all_to_all(x, AXES, split_axis=0, concat_axis=0, tiled=True)  26.8 us
    all_to_all x3, starting transfers between devices, exchange(): return lax.all_to_all(x, AXES, split_axis=0, concat_axis=0, tiled=True)  14.2 us
    pallas_call x9, Pallas kernels, call(): pl.pallas_call(kernel, out_shape=shapes if many else shapes[0], in_specs=...  11.6 us
    unnamed x30, local copies, waits for them, and re-layouts  4.5 us
    pallas_call x1, Pallas kernels, on_device(): pl.pallas_call(first_kernel, out_shape=jax.ShapeDtypeStruct((8 * LANES, L...  2.38 us
  transfers between devices with their start and end apart: 3, of which 3 were waited for; matrix products, arithmetic and copies ran while one was open for 0% of the time, Pallas kernels for 5%

profile of v2, /device:TPU:1, one launch (start us, length us, event | category | flops | bytes accessed | tf_op | source)
XLA Modules:
  0.0 117.1 jit_solution(3759683008484220947)
XLA Ops:
  0.6 2.4 %shard_map.138 = f32[1024,128]{1,0:T(8,128)S(1)} custom-call(f32[512,128]{1,0:T(8,128)} %bitcast.25, s32[2,256]{1,0:T(2,128)} %mask_ref.1, f32[1,128]{1,0:T(1,128)} %bitcast.38, f32[1,128]{1,0:T(1,128)} %bitcast.41, f32[128,640]{1,0:T(8,128)} %w_ref.5, f32[640]{0:T(1024)} %bin_ref.1), custom_call_target="tpu_custom_call" | custom-call | tf_op jit(solution)/shard_map/pallas_call | solution.py:252
  3.0 24.7 %all_to_all.54 = f32[128,8,128]{2,1,0:T(8,128)S(1)} all-to-all(f32[128,8,128]{2,1,0:T(8,128)S(1)} %bitcast.30), channel_id=1, replica_groups=mesh['row'=32,'ch'=4] {'row','ch'}, dimensions={0} | all-to-all | bytes 1048576 | tf_op jit(solution)/shard_map/all_to_all | solution.py:223
  27.8 1.1 shard_map.139
  28.9 4.9 %all-to-all-start.1 = ((f32[128,4,128]{2,1,0:T(4,128)}), f32[128,4,128]{2,1,0:T(4,128)S(1)}, u32[]{:S(2)}, u32[]{:S(2)}) async-start(f32[128,4,128]{2,1,0:T(4,128)} %bitcast.5), calls=%async_computation.1 | async-start | bytes 524288 | tf_op jit(solution)/shard_map/all_to_all | solution.py:223
  33.8 0.0 copy-start.9
  33.8 0.0 copy-start.10
  33.8 0.0 copy-start.12
  33.9 0.6 copy-done.9
  34.5 0.0 copy-done.12
  34.5 2.3 %shard_map.140 = (f32[512,128]{1,0:T(8,128)S(1)}, f32[512,512]{1,0:T(8,128)S(1)}, f32[512,128]{1,0:T(8,128)S(1)}, f32[128,512]{1,0:T(8,128)S(1)}, f32[512,128]{1,0:T(8,128)S(1)}) custom-call(f32[512,128]{1,0:T(8,128)S(1)} %bitcast.26, s32[2,256]{1,0:T(2,128)S(1)} %copy-done.9, f32[1,128]{1,0:T(1,128)S(1)} %bitcast.39, f32[1,128]{1,0:T(1,128)S(1)} %bitcast.42, ...), custom_call_target="tpu_custom_call" | custom-call | tf_op jit(solution)/shard_map/pallas_call | solution.py:213
  36.9 0.0 copy-start.4
  36.9 0.7 copy-done.4
  37.6 7.2 %all-to-all-done.1 = f32[128,4,128]{2,1,0:T(4,128)S(1)} async-done(((f32[128,4,128]{2,1,0:T(4,128)}), f32[128,4,128]{2,1,0:T(4,128)S(1)}, u32[]{:S(2)}, u32[]{:S(2)}) %all-to-all-start.1) | async-done | bytes 262176 | tf_op jit(solution)/shard_map/all_to_all | solution.py:223
  44.8 0.2 shard_map.142
  44.9 15.3 %all_to_all.55 = f32[128,4,128]{2,1,0:T(4,128)S(1)} all-to-all(f32[128,4,128]{2,1,0:T(4,128)S(1)} %bitcast.35), channel_id=1, replica_groups=mesh['row'=32,'ch'=4] {'row','ch'}, dimensions={0} | all-to-all | bytes 524288 | tf_op jit(solution)/shard_map/all_to_all | solution.py:223
  60.3 1.5 %shard_map.143 = f32[1024,128]{1,0:T(8,128)} custom-call(f32[512,128]{1,0:T(8,128)S(1)} %bitcast.34, f32[1024,128]{1,0:T(8,128)S(1)} %bitcast.22), custom_call_target="tpu_custom_call" | custom-call | tf_op jit(solution)/shard_map/pallas_call | solution.py:213
  61.8 4.5 %all-to-all-start.3 = ((f32[128,8,128]{2,1,0:T(8,128)}), f32[128,8,128]{2,1,0:T(8,128)S(1)}, u32[]{:S(2)}, u32[]{:S(2)}) async-start(f32[128,8,128]{2,1,0:T(8,128)} %bitcast.14), calls=%async_computation.3 | async-start | bytes 1048576 | tf_op jit(solution)/shard_map/all_to_all | solution.py:223
  66.3 0.0 copy-start.13
  66.3 0.6 copy-done.13
  67.0 0.0 copy-done.14
  67.0 0.9 copy-done.5
  67.9 1.8 %shard_map.141 = (f32[512,128]{1,0:T(8,128)}, f32[256,128]{1,0:T(8,128)S(1)}, f32[512,128]{1,0:T(8,128)S(1)}) custom-call(f32[512,128]{1,0:T(8,128)S(1)} %bitcast.29, f32[512,128]{1,0:T(8,128)S(1)} %get-tuple-element.14.gate_ref, f32[512,128]{1,0:T(8,128)S(1)} %bitcast.37, f32[512,128]{1,0:T(8,128)S(1)} %copy-done.5, ...), custom_call_target="tpu_custom_call" | custom-call | tf_op jit(solution)/shard_map/pallas_call | solution.py:213
  69.8 0.7 copy-done.6
  70.4 9.3 %all-to-all-done.3 = f32[128,8,128]{2,1,0:T(8,128)S(1)} async-done(((f32[128,8,128]{2,1,0:T(8,128)}), f32[128,8,128]{2,1,0:T(8,128)S(1)}, u32[]{:S(2)}, u32[]{:S(2)}) %all-to-all-start.3) | async-done | bytes 524320 | tf_op jit(solution)/shard_map/all_to_all | solution.py:223
  79.8 0.9 copy-done.7
  80.7 1.1 shard_map.145
  81.8 16.7 %all_to_all.56 = f32[384,2,128]{2,1,0:T(2,128)S(1)} all-to-all(f32[384,2,128]{2,1,0:T(2,128)S(1)} %bitcast.32), channel_id=1, replica_groups=mesh['row'=32,'ch'=4] {'row','ch'}, dimensions={0} | all-to-all | bytes 786432 | tf_op jit(solution)/shard_map/all_to_all | solution.py:223
  98.5 0.8 shard_map.146
  99.3 4.8 %all-to-all-start.5 = ((f32[384,2,128]{2,1,0:T(2,128)}), f32[384,2,128]{2,1,0:T(2,128)S(1)}, u32[]{:S(2)}, u32[]{:S(2)}) async-start(f32[384,2,128]{2,1,0:T(2,128)} %bitcast.19), calls=%async_computation.5 | async-start | bytes 786432 | tf_op jit(solution)/shard_map/all_to_all | solution.py:223
  104.2 1.8 %shard_map.144 = f32[512,128]{1,0:T(8,128)} custom-call(f32[1024,128]{1,0:T(8,128)S(1)} %bitcast.24, f32[512,512]{1,0:T(8,128)S(1)} %get-tuple-element.19.factor_ref, f32[512,128]{1,0:T(8,128)S(1)} %get-tuple-element.20.dnorm_ref, f32[512,128]{1,0:T(8,128)S(1)} %bitcast.27, f32[1,128]{1,0:T(1,128)S(1)} %bitcast.40, f32[128,640]{1,0:T(8,128)S(1)} %copy-done), custom_call_target="tpu_custom_call" | custom-call | tf_op jit(solution)/shard_map/pallas_call | solution.py:213
  106.0 10.3 %all-to-all-done.5 = f32[384,2,128]{2,1,0:T(2,128)S(1)} async-done(((f32[384,2,128]{2,1,0:T(2,128)}), f32[384,2,128]{2,1,0:T(2,128)S(1)}, u32[]{:S(2)}, u32[]{:S(2)}) %all-to-all-start.5) | async-done | bytes 393248 | tf_op jit(solution)/shard_map/all_to_all | solution.py:223
  116.2 0.9 shard_map.147
  (17 shorter events, 0.0 us)
Async XLA Ops:
  27.8 6.1 %copy-start.1 = (f32[2,256,128]{2,1,0:T(8,128)S(1)}, f32[2,256,128]{2,1,0:T(8,128)}, u32[]{:S(2)}) copy-start(f32[2,256,128]{2,1,0:T(8,128)} %param.11) | copy-start | bytes 786436
  27.8 6.1 %copy-start.2 = (f32[2,256,128]{2,1,0:T(8,128)S(1)}, f32[2,256,128]{2,1,0:T(8,128)}, u32[]{:S(2)}) copy-start(f32[2,256,128]{2,1,0:T(8,128)} %param.21) | copy-start | bytes 786436
  28.9 5.0 %copy-start = (f32[128,640]{1,0:T(8,128)S(1)}, f32[128,640]{1,0:T(8,128)}, u32[]{:S(2)}) copy-start(f32[128,640]{1,0:T(8,128)} %w_ref.5) | copy-start | bytes 983044
  28.9 5.0 %copy-start.3 = (f32[128,128]{1,0:T(8,128)S(1)}, f32[128,128]{1,0:T(8,128)}, u32[]{:S(2)}) copy-start(f32[128,128]{1,0:T(8,128)} %wout_ref.3) | copy-start | bytes 196612
  28.9 5.0 %copy-start.8 = (f32[640]{0:T(1024)S(1)}, f32[640]{0:T(1024)}, u32[]{:S(2)}) copy-start(f32[640]{0:T(1024)} %bin_ref.1) | copy-start | bytes 7684
  28.9 15.9 %all-to-all-start.1 = ((f32[128,4,128]{2,1,0:T(4,128)}), f32[128,4,128]{2,1,0:T(4,128)S(1)}, u32[]{:S(2)}, u32[]{:S(2)}) async-start(f32[128,4,128]{2,1,0:T(4,128)} %bitcast.5), calls=%async_computation.1 | async-start | bytes 524288 | tf_op jit(solution)/shard_map/all_to_all | solution.py:223
  33.8 0.7 copy-start.9
  33.8 0.7 copy-start.10
  33.8 0.7 copy-start.11
  33.8 0.7 copy-start.12
  36.9 0.7 copy-start.4
  61.8 18.0 %all-to-all-start.3 = ((f32[128,8,128]{2,1,0:T(8,128)}), f32[128,8,128]{2,1,0:T(8,128)S(1)}, u32[]{:S(2)}, u32[]{:S(2)}) async-start(f32[128,8,128]{2,1,0:T(8,128)} %bitcast.14), calls=%async_computation.3 | async-start | bytes 1048576 | tf_op jit(solution)/shard_map/all_to_all | solution.py:223
  66.3 0.7 copy-start.13
  66.3 0.7 copy-start.14
  67.0 0.9 copy-start.5
  69.8 0.7 copy-start.6
  79.8 0.9 copy-start.7
  99.3 16.9 %all-to-all-start.5 = ((f32[384,2,128]{2,1,0:T(2,128)}), f32[384,2,128]{2,1,0:T(2,128)S(1)}, u32[]{:S(2)}, u32[]{:S(2)}) async-start(f32[384,2,128]{2,1,0:T(2,128)} %bitcast.19), calls=%async_computation.5 | async-start | bytes 786432 | tf_op jit(solution)/shard_map/all_to_all | solution.py:223

commit v3 on v2

--- a/solution.py
+++ b/solution.py
@@ -9,7 +9,9 @@
 
 epsilon = 1e-05
 LANES = 128
-AXES = ("row", "ch")
+PARTS = ("x_high", "z", "y", "x_low", "core")
+SIZES = (2, 4, 4, 2, 2)
+AXES = ("x_low", "core", "x_high", "y", "z")
 F32 = jnp.float32
 NN = (((1,), (0,)), ((), ()))
 NT = (((1,), (1,)), ((), ()))
@@ -22,6 +24,22 @@
     )
 
 
+def halves(x):
+    high = x.astype(jnp.bfloat16)
+    return high, (x - high.astype(F32)).astype(jnp.bfloat16)
+
+
+def mm3(a, b, dims):
+    (a_high, a_low), (b_high, b_low) = halves(a), halves(b)
+    ((a_dim,), (b_dim,)), _ = dims
+    return lax.dot_general(
+        jnp.concatenate([a_high, a_low, a_high], axis=a_dim),
+        jnp.concatenate([b_high, b_high, b_low], axis=b_dim),
+        dims,
+        preferred_element_type=F32,
+    )
+
+
 def every(start, step):
     return pl.ds(start, LANES, stride=step)
 
@@ -46,8 +64,15 @@
     return center * scale, scale
 
 
-def project(normed, w_ref, b_ref, part):
-    return mm(jnp.transpose(w_ref[:, block(part)]), normed, NT) + jnp.tile(
+def places():
+    s = lax.broadcasted_iota(jnp.int32, (LANES, LANES), 0)
+    d = lax.broadcasted_iota(jnp.int32, (LANES, LANES), 1)
+    x_low_core, x_high, y, z = s // 32, (s // 16) % 2, (s // 4) % 4, s % 4
+    return (d == x_high * 64 + z * 16 + y * 4 + x_low_core).astype(F32)
+
+
+def project(normed, w_ref, b_ref, part, mul=mm):
+    return mul(jnp.transpose(w_ref[:, block(part)]), normed, NT) + jnp.tile(
         column(b_ref[pl.ds(part * LANES, LANES)][None]), (1, normed.shape[0] // LANES)
     )
 
@@ -71,34 +96,31 @@
     for side in range(2):
         value = (
             mask
-            * jax.nn.sigmoid(project(normed, w_ref, bin_ref, 2 * side))
-            * project(normed, w_ref, bin_ref, 2 * side + 1)
+            * jax.nn.sigmoid(project(normed, w_ref, bin_ref, 2 * side, mm3))
+            * project(normed, w_ref, bin_ref, 2 * side + 1, mm3)
         )
         for b in range(4):
             out_ref[every(4 * side + b, 8), :] = value[:, block(b)]
 
 
 def side_kernel(
-    x_ref, mask_ref, g_ref, b_ref, w_ref, bin_ref, cot_ref, wout_ref, gout_ref,
-    normed_ref, factor_ref, gate_ref, back_ref, cg_ref,
+    x_ref, g_ref, b_ref, w_ref, bin_ref, cot_ref, wout_ref, gout_ref, back_ref, cg_ref, held_ref,
 ):
     hat, _ = norm_rows(x_ref[...])
     normed = hat * g_ref[...] + b_ref[...]
-    normed_ref[...] = normed
-    mask = cell_mask(mask_ref)
-    for side in range(2):
-        sig = jax.nn.sigmoid(project(normed, w_ref, bin_ref, 2 * side))
-        value = project(normed, w_ref, bin_ref, 2 * side + 1)
-        open_part = mask * sig
-        factor_ref[block(2 * side), :] = open_part * (1.0 - sig) * value
-        factor_ref[block(2 * side + 1), :] = open_part
-    gate = jax.nn.sigmoid(mm(normed, w_ref[:, block(4)], NN) + bin_ref[pl.ds(4 * LANES, LANES)][None])
-    gate_ref[...] = gate
-    cg_ref[...] = gate * cot_ref[...]
+    held_ref[...] = cot_ref[...] * gate_of(normed, w_ref, bin_ref)
     gain = column(gout_ref[...])
+    place = places()
     for q in range(4):
-        part = cg_ref[every((q // 2) * 256 + q % 2, 2), :]
+        part = mm(place, held_ref[every((q // 2) * 256 + q % 2, 2), :], NN)
+        cg_ref[block(q), :] = part
         back_ref[:, block(q)] = gain * mm(wout_ref[...], part, NT)
+
+
+def gate_of(normed, w_ref, bin_ref):
+    return jax.nn.sigmoid(
+        mm(normed, w_ref[:, block(4)], NN) + bin_ref[pl.ds(4 * LANES, LANES)][None]
+    )
 
 
 def gather_sides(in_ref):
@@ -114,7 +136,7 @@
 
 def product_kernel(in_ref, out_ref):
     left, right = gather_sides(in_ref)
-    product = mm(left, right, NT)
+    product = mm3(left, right, NT)
     for q in range(4):
         out_ref[every(q, 4), :] = product[block(q // 2), block(q % 2)]
 
@@ -129,25 +151,38 @@
 
 
 def update_kernel(
-    in_ref, gate_ref, cot_ref, cg_ref, normed_ref, wout_ref, gout_ref, bout_ref, boff_ref, w_ref,
-    update_ref, grads_ref, dnorm_ref,
+    in_ref, x_ref, mask_ref, g_ref, b_ref, w_ref, bin_ref, cot_ref, cg_ref,
+    wout_ref, gout_ref, boff_ref, bout_ref,
+    update_ref, dnorm_ref, kept_ref, factor_ref, gate_ref,
 ):
+    hat, _ = norm_rows(x_ref[...])
+    normed = hat * g_ref[...] + b_ref[...]
+    kept_ref[0 : normed.shape[0], :] = normed
+    gate_ref[...] = gate_of(normed, w_ref, bin_ref)
+    mask = cell_mask(mask_ref)
+    for side in range(2):
+        sig = jax.nn.sigmoid(project(normed, w_ref, bin_ref, 2 * side))
+        value = project(normed, w_ref, bin_ref, 2 * side + 1)
+        open_part = mask * sig
+        factor_ref[block(2 * side), :] = open_part * (1.0 - sig) * value
+        factor_ref[block(2 * side + 1), :] = open_part
     gain, bias = column(gout_ref[...]), column(boff_ref[...])
+    place = places()
     d_wout = jnp.zeros((LANES, LANES), F32)
     d_gate_w = jnp.zeros((LANES, LANES), F32)
     for q in range(4):
         cells = every((q // 2) * 256 + q % 2, 2)
         hat, _ = norm_cols(in_ref[every(q, 4), :])
         normed_product = hat * gain + bias
-        projected = mm(normed_product, wout_ref[...], TN) + bout_ref[...]
+        d_wout += mm(normed_product, cg_ref[block(q), :], NN)
+        projected = mm(place, mm(normed_product, wout_ref[...], TN), TN) + bout_ref[...]
         gate = gate_ref[cells, :]
         update_ref[cells, :] = gate * projected
-        d_wout += mm(normed_product, cg_ref[cells, :], NN)
         d_open = cot_ref[cells, :] * projected * gate * (1.0 - gate)
-        d_gate_w += mm(normed_ref[cells, :], d_open, TN)
+        d_gate_w += mm(kept_ref[cells, :], d_open, TN)
         dnorm_ref[cells, :] = mm(d_open, w_ref[:, block(4)], NT)
-    grads_ref[block(0), :] = d_wout
-    grads_ref[block(1), :] = d_gate_w
+    kept_ref[block(4), :] = d_wout
+    kept_ref[block(5), :] = d_gate_w
 
 
 def back_product_kernel(grad_ref, in_ref, out_ref):
@@ -159,7 +194,7 @@
         ],
         axis=0,
     )
-    sides = (mm(grad, right, NN), mm(grad, left, TN))
+    sides = (mm3(grad, right, NN), mm3(jnp.transpose(grad), left, NN))
     for side in range(2):
         for b in range(4):
             out_ref[every(4 * side + b, 8), :] = sides[side][block(b // 2), block(b % 2)]
@@ -173,12 +208,12 @@
     return jnp.concatenate(parts, axis=0)
 
 
-def weight_kernel(in_ref, factor_ref, normed_ref, extra_ref, out_ref):
-    terms = mm(piece_grads(in_ref, factor_ref), normed_ref[...], NN)
+def weight_kernel(in_ref, factor_ref, kept_ref, out_ref):
+    terms = mm3(piece_grads(in_ref, factor_ref), kept_ref[0 : 4 * LANES, :], NN)
     for part in range(4):
         out_ref[every(part, 6), :] = terms[block(part), :]
     for part in range(2):
-        out_ref[every(4 + part, 6), :] = extra_ref[block(part), :]
+        out_ref[every(4 + part, 6), :] = kept_ref[block(4 + part), :]
 
 
 def pair_kernel(in_ref, factor_ref, dnorm_ref, x_ref, g_ref, w_ref, out_ref):
@@ -206,7 +241,7 @@
     win_ref[:, block(4)] = in_ref[every(5, 6), :]
 
 
-def call(kernel, outs, *args):
+def call(kernel, outs, *args, scratch=()):
     many = isinstance(outs, list)
     shapes = [jax.ShapeDtypeStruct(s, F32) for s in (outs if many else [outs])]
     spec = pl.BlockSpec(memory_space=pltpu.VMEM)
@@ -215,6 +250,7 @@
         out_shape=shapes if many else shapes[0],
         in_specs=[spec] * len(args),
         out_specs=[spec] * len(shapes) if many else spec,
+        scratch_shapes=[pltpu.VMEM(s, F32) for s in scratch],
         compiler_params=pltpu.CompilerParams(vmem_limit_bytes=24 * 2**20),
     )(*args)
 
@@ -259,33 +295,42 @@
         compiler_params=pltpu.CompilerParams(vmem_limit_bytes=24 * 2**20),
     )(*[pltpu.with_memory_space_constraint(a, pltpu.HBM) for a in inputs])
     sides = exchange(sent)
-    normed, factor, gate, back, cg = call(
+    back, cg = call(
         side_kernel,
-        [(cells, LANES), (4 * LANES, cells), (cells, LANES), (LANES, cells), (cells, LANES)],
-        *inputs,
+        [(LANES, cells), (cells, LANES)],
+        x,
+        g_in,
+        o_in,
+        w_in,
+        b_in,
         cot,
         w_out,
         g_out,
+        scratch=[(cells, LANES)],
     )
     product = exchange(call(product_kernel, (4 * LANES, LANES), sides))
     d_product = exchange(call(middle_kernel, (4 * LANES, LANES), product, back))
-    update, extra, d_norm = call(
+    d_sides = exchange(call(back_product_kernel, (8 * LANES, LANES), d_product, sides))
+    update, d_norm, kept, factor = call(
         update_kernel,
-        [(cells, LANES), (2 * LANES, LANES), (cells, LANES)],
+        [
+            (cells, LANES),
+            (cells, LANES),
+            (6 * LANES, LANES),
+            (4 * LANES, cells),
+        ],
         product,
-        gate,
+        *inputs,
         cot,
         cg,
-        normed,
         w_out,
         g_out,
+        o_out,
         bias_out,
-        o_out,
-        w_in,
-    )
-    d_sides = exchange(call(back_product_kernel, (8 * LANES, LANES), d_product, sides))
+        scratch=[(cells, LANES)],
+    )
     terms = exchange_pairs(
-        call(weight_kernel, (6 * LANES, LANES), d_sides, factor, normed, extra)
+        call(weight_kernel, (6 * LANES, LANES), d_sides, factor, kept)
     )
     grad_pair = call(
         pair_kernel, (cells, LANES), d_sides, factor, d_norm, x, g_in, w_in
@@ -298,23 +343,12 @@
 
 
 def solution(mesh):
-    placed = (
-        P(("row", "ch"), None, None),
-        P(("row", "ch"), None),
-        P(),
-        P(),
-        P(),
-        P(),
-        P(),
-        P(),
-        P(),
-        P(),
-        P(("row", "ch"), None, None),
-    )
+    whole = P(PARTS, None, None)
+    placed = (whole, P(PARTS, None)) + (P(),) * 8 + (whole,)
     return jax.shard_map(
         on_device,
-        mesh=mesh,
+        mesh=jax.sharding.Mesh(mesh.devices.reshape(SIZES), PARTS),
         in_specs=placed,
-        out_specs=(P(("row", "ch"), None, None), P(("row", "ch"), None, None), P(), P()),
+        out_specs=(whole, whole, P(), P()),
         check_vma=False,
     )

time: 118 us -> 113 us (0.958)
  starting transfers between devices: 14.2 us -> 12.1 us
  local copies, waits for them, and re-layouts: 4.5 us -> 2.95 us
    all_to_all x3, starting transfers between devices: 14.2 us -> 12.1 us  [exchange(): return lax.all_to_all(x, AXES, split_axis=0, concat_axis=0, tiled=True)]
    unnamed x30 -> x26, local copies, waits for them, and re-layouts: 4.5 us -> 2.95 us
    pallas_call x9, Pallas kernels: 11.6 us -> 12.9 us  [call(): pl.pallas_call(kernel, out_shape=shapes if many else shapes[0], in_specs=...]
  transfers between devices with their start and end apart: 3 -> 3, of which waited for: 3 -> 3; matrix products, arithmetic and copies ran while one was open for 0% -> 0% of each run, Pallas kernels for 5% -> 7%
where the time goes in v3:
time: 113 us
  blocking collectives  56.1 us (50%)
  waiting for transfers between devices  26.1 us (23%)
  Pallas kernels  14.9 us (13%)
  starting transfers between devices  12.1 us (11%)
  local copies, waits for them, and re-layouts  2.95 us (3%)
    all_to_all x3, blocking collectives, exchange(): return lax.all_to_all(x, AXES, split_axis=0, concat_axis=0, tiled=True)  56.1 us
    all_to_all x3, waiting for transfers between devices, exchange(): return lax.all_to_all(x, AXES, split_axis=0, concat_axis=0, tiled=True)  26.1 us
    pallas_call x9, Pallas kernels, call(): pl.pallas_call(kernel, out_shape=shapes if many else shapes[0], in_specs=...  12.9 us
    all_to_all x3, starting transfers between devices, exchange(): return lax.all_to_all(x, AXES, split_axis=0, concat_axis=0, tiled=True)  12.1 us
    unnamed x26, local copies, waits for them, and re-layouts  2.95 us
  transfers between devices with their start and end apart: 3, of which 3 were waited for; matrix products, arithmetic and copies ran while one was open for 0% of the time, Pallas kernels for 7%

profile of v3, /device:TPU:1, one launch (start us, length us, event | category | flops | bytes accessed | tf_op | source)
XLA Modules:
  0.0 112.9 jit_solution(2309099911303153997)
XLA Ops:
  0.6 2.0 %shard_map.138 = f32[1024,128]{1,0:T(8,128)S(1)} custom-call(f32[512,128]{1,0:T(8,128)} %bitcast.25, s32[2,256]{1,0:T(2,128)} %mask_ref.1, f32[1,128]{1,0:T(1,128)} %bitcast.39, f32[1,128]{1,0:T(1,128)} %bitcast.43, f32[128,640]{1,0:T(8,128)} %w_ref.5, f32[640]{0:T(1024)} %bin_ref.3), custom_call_target="tpu_custom_call" | custom-call | tf_op jit(solution)/shard_map/pallas_call | solution.py:288
  2.7 24.8 %all_to_all.54 = f32[128,8,128]{2,1,0:T(8,128)S(1)} all-to-all(f32[128,8,128]{2,1,0:T(8,128)S(1)} %bitcast.31), channel_id=1, replica_groups=mesh['x_high'=2,'z'=4,'y'=4,'x_low'=2,'core'=2] {'x_low','core','x_high'..., dimensions={0} | all-to-all | bytes 1048576 | tf_op jit(solution)/shard_map/all_to_all | solution.py:259
  27.5 1.0 shard_map.139
  28.5 4.3 %all-to-all-start.1 = ((f32[128,4,128]{2,1,0:T(4,128)}), f32[128,4,128]{2,1,0:T(4,128)S(1)}, u32[]{:S(2)}, u32[]{:S(2)}) async-start(f32[128,4,128]{2,1,0:T(4,128)} %bitcast.5), calls=%async_computation.1 | async-start | bytes 524288 | tf_op jit(solution)/shard_map/all_to_all | solution.py:259
  32.8 0.0 copy-start.7
  32.8 0.0 copy-start.9
  32.8 0.0 copy-start.10
  32.9 0.6 copy-done.7
  33.4 0.0 copy-done.9
  33.5 0.0 copy-done.10
  33.5 2.1 %shard_map.140 = (f32[128,512]{1,0:T(8,128)S(1)}, f32[512,128]{1,0:T(8,128)S(1)}) custom-call(f32[512,128]{1,0:T(8,128)S(1)} %bitcast.26, f32[1,128]{1,0:T(1,128)S(1)} %bitcast.40, f32[1,128]{1,0:T(1,128)S(1)} %bitcast.44, f32[128,640]{1,0:T(8,128)S(1)} %copy-done, f32[640]{0:T(1024)S(1)} %copy-done.6, f32[512,128]{1,0:T(8,128)S(1)} %bitcast.37, ...), custom_call_target="tpu_custom_call" | custom-call | tf_op jit(solution)/shard_map/pallas_call | solution.py:248
  35.5 0.0 copy-start.3
  35.6 0.7 copy-done.3
  36.2 7.7 %all-to-all-done.1 = f32[128,4,128]{2,1,0:T(4,128)S(1)} async-done(((f32[128,4,128]{2,1,0:T(4,128)}), f32[128,4,128]{2,1,0:T(4,128)S(1)}, u32[]{:S(2)}, u32[]{:S(2)}) %all-to-all-start.1) | async-done | bytes 262176 | tf_op jit(solution)/shard_map/all_to_all | solution.py:259
  44.0 0.2 shard_map.142
  44.2 14.8 %all_to_all.55 = f32[128,4,128]{2,1,0:T(4,128)S(1)} all-to-all(f32[128,4,128]{2,1,0:T(4,128)S(1)} %bitcast.36), channel_id=1, replica_groups=mesh['x_high'=2,'z'=4,'y'=4,'x_low'=2,'core'=2] {'x_low','core','x_high'..., dimensions={0} | all-to-all | bytes 524288 | tf_op jit(solution)/shard_map/all_to_all | solution.py:259
  58.9 1.3 %shard_map.143 = f32[1024,128]{1,0:T(8,128)} custom-call(f32[512,128]{1,0:T(8,128)S(1)} %bitcast.35, f32[1024,128]{1,0:T(8,128)S(1)} %bitcast.22), custom_call_target="tpu_custom_call" | custom-call | tf_op jit(solution)/shard_map/pallas_call | solution.py:248
  60.2 3.9 %all-to-all-start.3 = ((f32[128,8,128]{2,1,0:T(8,128)}), f32[128,8,128]{2,1,0:T(8,128)S(1)}, u32[]{:S(2)}, u32[]{:S(2)}) async-start(f32[128,8,128]{2,1,0:T(8,128)} %bitcast.14), calls=%async_computation.3 | async-start | bytes 1048576 | tf_op jit(solution)/shard_map/all_to_all | solution.py:259
  64.1 0.0 copy-start.8
  64.1 0.0 copy-start.11
  64.1 0.0 copy-start.12
  64.1 0.6 copy-done.8
  64.8 0.9 copy-done.4
  65.7 4.3 %shard_map.141 = (f32[512,128]{1,0:T(8,128)}, f32[512,128]{1,0:T(8,128)S(1)}, f32[768,128]{1,0:T(8,128)S(1)}, f32[512,512]{1,0:T(8,128)S(1)}) custom-call(f32[512,128]{1,0:T(8,128)S(1)} %bitcast.30, f32[512,128]{1,0:T(8,128)S(1)} %bitcast.27, s32[2,256]{1,0:T(2,128)S(1)} %copy-done.8, f32[1,128]{1,0:T(1,128)S(1)} %bitcast.41, f32[1,128]{1,0:T(1,128)S(1)} %bitcast.45, ...), custom_call_target="tpu_custom_call" | custom-call | tf_op jit(solution)/shard_map/pallas_call | solution.py:248
  70.0 7.7 %all-to-all-done.3 = f32[128,8,128]{2,1,0:T(8,128)S(1)} async-done(((f32[128,8,128]{2,1,0:T(8,128)}), f32[128,8,128]{2,1,0:T(8,128)S(1)}, u32[]{:S(2)}, u32[]{:S(2)}) %all-to-all-start.3) | async-done | bytes 524320 | tf_op jit(solution)/shard_map/all_to_all | solution.py:259
  77.7 0.6 shard_map.145
  78.3 16.5 %all_to_all.56 = f32[384,2,128]{2,1,0:T(2,128)S(1)} all-to-all(f32[384,2,128]{2,1,0:T(2,128)S(1)} %bitcast.33), channel_id=1, replica_groups=mesh['x_high'=2,'z'=4,'y'=4,'x_low'=2,'core'=2] {'x_low','core','x_high'..., dimensions={0} | all-to-all | bytes 786432 | tf_op jit(solution)/shard_map/all_to_all | solution.py:259
  94.8 0.8 shard_map.146
  95.6 4.0 %all-to-all-start.5 = ((f32[384,2,128]{2,1,0:T(2,128)}), f32[384,2,128]{2,1,0:T(2,128)S(1)}, u32[]{:S(2)}, u32[]{:S(2)}) async-start(f32[384,2,128]{2,1,0:T(2,128)} %bitcast.19), calls=%async_computation.5 | async-start | bytes 786432 | tf_op jit(solution)/shard_map/all_to_all | solution.py:259
  99.6 1.8 %shard_map.144 = f32[512,128]{1,0:T(8,128)} custom-call(f32[1024,128]{1,0:T(8,128)S(1)} %bitcast.24, f32[512,512]{1,0:T(8,128)S(1)} %get-tuple-element.15.factor_ref, f32[512,128]{1,0:T(8,128)S(1)} %get-tuple-element.16.dnorm_ref, f32[512,128]{1,0:T(8,128)S(1)} %bitcast.28, f32[1,128]{1,0:T(1,128)S(1)} %bitcast.42, f32[128,640]{1,0:T(8,128)S(1)} %copy-done), custom_call_target="tpu_custom_call" | custom-call | tf_op jit(solution)/shard_map/pallas_call | solution.py:248
  101.4 10.6 %all-to-all-done.5 = f32[384,2,128]{2,1,0:T(2,128)S(1)} async-done(((f32[384,2,128]{2,1,0:T(2,128)}), f32[384,2,128]{2,1,0:T(2,128)S(1)}, u32[]{:S(2)}, u32[]{:S(2)}) %all-to-all-start.5) | async-done | bytes 393248 | tf_op jit(solution)/shard_map/all_to_all | solution.py:259
  112.0 0.9 shard_map.147
  (13 shorter events, 0.0 us)
Async XLA Ops:
  27.5 5.4 %copy-start.1 = (f32[2,256,128]{2,1,0:T(8,128)S(1)}, f32[2,256,128]{2,1,0:T(8,128)}, u32[]{:S(2)}) copy-start(f32[2,256,128]{2,1,0:T(8,128)} %param.11) | copy-start | bytes 786436
  27.5 5.4 %copy-start.2 = (f32[2,256,128]{2,1,0:T(8,128)S(1)}, f32[2,256,128]{2,1,0:T(8,128)}, u32[]{:S(2)}) copy-start(f32[2,256,128]{2,1,0:T(8,128)} %param.21) | copy-start | bytes 786436
  28.5 4.4 %copy-start = (f32[128,640]{1,0:T(8,128)S(1)}, f32[128,640]{1,0:T(8,128)}, u32[]{:S(2)}) copy-start(f32[128,640]{1,0:T(8,128)} %w_ref.5) | copy-start | bytes 983044
  28.5 4.4 %copy-start.5 = (f32[128,128]{1,0:T(8,128)S(1)}, f32[128,128]{1,0:T(8,128)}, u32[]{:S(2)}) copy-start(f32[128,128]{1,0:T(8,128)} %wout_ref.3) | copy-start | bytes 196612
  28.5 4.4 %copy-start.6 = (f32[640]{0:T(1024)S(1)}, f32[640]{0:T(1024)}, u32[]{:S(2)}) copy-start(f32[640]{0:T(1024)} %bin_ref.3) | copy-start | bytes 7684
  28.5 15.5 %all-to-all-start.1 = ((f32[128,4,128]{2,1,0:T(4,128)}), f32[128,4,128]{2,1,0:T(4,128)S(1)}, u32[]{:S(2)}, u32[]{:S(2)}) async-start(f32[128,4,128]{2,1,0:T(4,128)} %bitcast.5), calls=%async_computation.1 | async-start | bytes 524288 | tf_op jit(solution)/shard_map/all_to_all | solution.py:259
  32.8 0.7 copy-start.7
  32.8 0.7 copy-start.9
  32.8 0.7 copy-start.10
  35.5 0.7 copy-start.3
  60.2 17.5 %all-to-all-start.3 = ((f32[128,8,128]{2,1,0:T(8,128)}), f32[128,8,128]{2,1,0:T(8,128)S(1)}, u32[]{:S(2)}, u32[]{:S(2)}) async-start(f32[128,8,128]{2,1,0:T(8,128)} %bitcast.14), calls=%async_computation.3 | async-start | bytes 1048576 | tf_op jit(solution)/shard_map/all_to_all | solution.py:259
  64.1 0.7 copy-start.8
  64.1 0.7 copy-start.11
  64.1 0.7 copy-start.12
  64.8 1.0 copy-start.4
  95.6 16.4 %all-to-all-start.5 = ((f32[384,2,128]{2,1,0:T(2,128)}), f32[384,2,128]{2,1,0:T(2,128)S(1)}, u32[]{:S(2)}, u32[]{:S(2)}) async-start(f32[384,2,128]{2,1,0:T(2,128)} %bitcast.19), calls=%async_computation.5 | async-start | bytes 786432 | tf_op jit(solution)/shard_map/all_to_all | solution.py:259

commit v4 on v3

v4 whole, which is shorter than its diff:
```python
import functools

import jax
import jax.numpy as jnp
from jax import lax
from jax.experimental import pallas as pl
from jax.experimental.pallas import tpu as pltpu
from jax.sharding import PartitionSpec as P

epsilon = 1e-05
LANES = 128
PARTS = ("x_high", "z", "y", "x_low", "core")
SIZES = (2, 4, 4, 2, 2)
AXES = ("x_low", "core", "x_high", "z", "y")
PLANE = AXES[:4]
LINE = "y"
MEMBERS = 4
SHARE = LANES // MEMBERS
F32 = jnp.float32
NN = (((1,), (0,)), ((), ()))
NT = (((1,), (1,)), ((), ()))
TN = (((0,), (0,)), ((), ()))


def mm(a, b, dims):
    return lax.dot_general(
        a, b, dims, precision=lax.Precision.HIGHEST, preferred_element_type=F32
    )


def halves(x):
    high = x.astype(jnp.bfloat16)
    return high, (x - high.astype(F32)).astype(jnp.bfloat16)


def mm3(a, b, dims):
    (a_high, a_low), (b_high, b_low) = halves(a), halves(b)
    ((a_dim,), (b_dim,)), _ = dims
    return lax.dot_general(
        jnp.concatenate([a_high, a_low, a_high], axis=a_dim),
        jnp.concatenate([b_high, b_high, b_low], axis=b_dim),
        dims,
        preferred_element_type=F32,
    )


def every(start, step):
    return pl.ds(start, LANES, stride=step)


def block(b):
    return slice(b * LANES, (b + 1) * LANES)


def column(row):
    return jnp.transpose(jnp.broadcast_to(row, (LANES, LANES)))


def norm_rows(x):
    center = x - jnp.mean(x, -1, keepdims=True)
    scale = lax.rsqrt(jnp.mean(center * center, -1, keepdims=True) + epsilon)
    return center * scale, scale


def norm_cols(x):
    center = x - jnp.mean(x, 0, keepdims=True)
    scale = lax.rsqrt(jnp.mean(center * center, 0, keepdims=True) + epsilon)
    return center * scale, scale


def places():
    s = lax.broadcasted_iota(jnp.int32, (LANES, LANES), 0)
    d = lax.broadcasted_iota(jnp.int32, (LANES, LANES), 1)
    x_low_core, x_high, z, y = s // 32, (s // 16) % 2, (s // 4) % 4, s % 4
    return (d == x_high * 64 + z * 16 + y * 4 + x_low_core).astype(F32)


def project(normed, w_ref, b_ref, part, mul=mm):
    return mul(jnp.transpose(w_ref[:, block(part)]), normed, NT) + jnp.tile(
        column(b_ref[pl.ds(part * LANES, LANES)][None]), (1, normed.shape[0] // LANES)
    )


def cell_mask(mask_ref):
    mask = mask_ref[...].astype(F32)
    return jnp.concatenate([mask[0:1], mask[1:2]], axis=1)


def first_kernel(x_ref, mask_ref, g_ref, b_ref, w_ref, bin_ref, out_ref, pack_ref):
    hat, _ = norm_rows(x_ref[...])
    normed = hat * g_ref[...] + b_ref[...]
    mask = cell_mask(mask_ref)
    for side in range(2):
        value = (
            mask
            * jax.nn.sigmoid(project(normed, w_ref, bin_ref, 2 * side, mm3))
            * project(normed, w_ref, bin_ref, 2 * side + 1, mm3)
        )
        for b in range(4):
            out_ref[every(4 * side + b, 8), :] = value[:, block(b)]
    pack_ref[0 : 4 * LANES, :] = x_ref[...]
    pack_ref[4 * LANES : 4 * LANES + 8, :] = jnp.concatenate(
        [mask[:, block(b)] for b in range(4)] + [jnp.zeros((4, LANES), F32)], axis=0
    )


def side_kernel(
    x_ref, g_ref, b_ref, w_ref, bin_ref, cot_ref, wout_ref, gout_ref, back_ref, cg_ref, held_ref,
):
    hat, _ = norm_rows(x_ref[...])
    normed = hat * g_ref[...] + b_ref[...]
    held_ref[...] = cot_ref[...] * gate_of(normed, w_ref, bin_ref)
    cg = mm(places(), in_quarters(held_ref), NN)
    for q in range(4):
        cg_ref[block(q), :] = cg[:, block(q)]
    back_ref[...] = jnp.tile(column(gout_ref[...]), (1, 4)) * mm3(wout_ref[...], cg_ref[...], NT)


def quarter(q):
    return every((q // 2) * 256 + q % 2, 2)


def in_quarters(ref):
    return jnp.concatenate([ref[quarter(q), :] for q in range(4)], axis=1)


def gate_of(normed, w_ref, bin_ref):
    return jax.nn.sigmoid(
        mm3(normed, w_ref[:, block(4)], NN) + bin_ref[pl.ds(4 * LANES, LANES)][None]
    )


def gather_sides(in_ref):
    sides = []
    for side in range(2):
        rows = [
            jnp.concatenate([in_ref[every(4 * side + 2 * r + h, 8), :] for h in range(2)], axis=1)
            for r in range(2)
        ]
        sides.append(jnp.concatenate(rows, axis=0))
    return sides


def product_kernel(in_ref, out_ref):
    left, right = gather_sides(in_ref)
    product = mm3(left, right, NT)
    for q in range(4):
        out_ref[every(q, 4), :] = product[block(q // 2), block(q % 2)]


def middle_kernel(in_ref, back_ref, out_ref):
    for q in range(4):
        hat, scale = norm_cols(in_ref[every(q, 4), :])
        back = back_ref[:, block(q)]
        first = jnp.mean(back, 0, keepdims=True)
        second = jnp.mean(back * hat, 0, keepdims=True)
        out_ref[every(q, 4), :] = scale * (back - first - hat * second)


def update_kernel(
    x_ref, g_ref, b_ref, w_ref, bin_ref, cot_ref, wout_ref, gout_ref, boff_ref, bout_ref,
    in_ref, cg_ref,
    update_ref, dnorm_ref, *rest,
):
    extra_refs, (open_ref, gate_ref, grads_ref, held_ref) = rest[:MEMBERS], rest[MEMBERS:]
    hat, _ = norm_rows(x_ref[...])
    normed = hat * g_ref[...] + b_ref[...]
    gate_ref[...] = gate_of(normed, w_ref, bin_ref)
    gain, bias = column(gout_ref[...]), column(boff_ref[...])
    normed_product = jnp.concatenate(
        [norm_cols(in_ref[every(q, 4), :])[0] * gain + bias for q in range(4)], axis=1
    )
    grads_ref[block(0), :] = mm3(normed_product, cg_ref[...], NN)
    projected = mm3(jnp.transpose(normed_product), wout_ref[...], NN)
    projected = jnp.concatenate([projected[block(q), :] for q in range(4)], axis=1)
    projected = mm(places(), projected, TN)
    for q in range(4):
        open_ref[quarter(q), :] = projected[:, block(q)] + bout_ref[...]
    gate = gate_ref[...]
    projected = open_ref[...]
    update_ref[...] = gate * projected
    d_open = cot_ref[...] * projected * gate * (1.0 - gate)
    grads_ref[block(1), :] = mm3(jnp.transpose(normed), d_open, NN)
    dnorm_ref[...] = mm3(d_open, w_ref[:, block(4)], NT)
    for member in range(MEMBERS):
        for part in range(2):
            held_ref[share(2 * member + part), :] = grads_ref[
                pl.ds(part * LANES + member, SHARE, stride=MEMBERS), :
            ]
    for turn in range(MEMBERS):
        extra_refs[turn][...] = held_ref[pl.ds(member_at(turn) * 2 * SHARE, 2 * SHARE), :]


def member_at(turn):
    return lax.rem(lax.axis_index(LINE) + turn, MEMBERS)


def share(n):
    return slice(n * SHARE, (n + 1) * SHARE)


def mine():
    u = lax.broadcasted_iota(jnp.int32, (SHARE, LANES), 0)
    f = lax.broadcasted_iota(jnp.int32, (SHARE, LANES), 1)
    return (f == u * MEMBERS + lax.axis_index(LINE)).astype(F32)


def my_weights(pick, w_ref):
    return jnp.concatenate([mm(pick, w_ref[:, block(p)], NT) for p in range(4)], axis=0)


def factor_kernel(*refs):
    packs, refs = refs[:MEMBERS], refs[MEMBERS:]
    g_ref, b_ref, w_ref, bin_ref, high_ref, low_ref, factor_ref, weights_ref, bias_ref = refs
    pick = mine()
    weights_ref[...] = my_weights(pick, w_ref)
    for p in range(4):
        row = bin_ref[pl.ds(p * LANES, LANES)][None]
        bias_ref[share(p), :] = jnp.broadcast_to(
            jnp.sum(pick * row, axis=1, keepdims=True), (SHARE, LANES)
        )
    for turn in range(MEMBERS):
        pack = packs[turn]
        hat, _ = norm_rows(pack[0 : 4 * LANES, :])
        normed = hat * g_ref[...] + b_ref[...]
        member = member_at(turn)
        rows = pl.ds(pl.multiple_of(member * 4 * LANES, 4 * LANES), 4 * LANES)
        high_ref[rows, :], low_ref[rows, :] = halves(normed)
        pieces = mm3(weights_ref[...], normed, NT) + jnp.tile(bias_ref[...], (1, 4))
        mask = jnp.concatenate([pack[4 * LANES + b : 4 * LANES + b + 1, :] for b in range(4)], axis=1)
        parts = []
        for side in range(2):
            sig = jax.nn.sigmoid(pieces[share(2 * side)])
            open_part = mask * sig
            parts += [open_part * (1.0 - sig) * pieces[share(2 * side + 1)], open_part]
        factor_ref[pl.ds(member * LANES, LANES), :] = jnp.concatenate(parts, axis=0)


def back_product_kernel(grad_ref, in_ref, out_ref):
    left, right = gather_sides(in_ref)
    grad = jnp.concatenate(
        [
            jnp.concatenate([grad_ref[every(2 * r + c, 4), :] for c in range(2)], axis=1)
            for r in range(2)
        ],
        axis=0,
    )
    sides = (mm3(grad, right, NN), mm3(jnp.transpose(grad), left, NN))
    for side in range(2):
        for b in range(4):
            out_ref[every(4 * side + b, 8), :] = sides[side][block(b // 2), block(b % 2)]


def piece_grads(in_ref, factor_ref, member):
    parts = []
    for side in range(2):
        grad = jnp.concatenate(
            [
                in_ref[pl.ds(member * 8 + 4 * side + b, SHARE, stride=8 * MEMBERS), :]
                for b in range(4)
            ],
            axis=1,
        )
        parts += [grad * factor_ref[share(4 * member + 2 * side + m), :] for m in range(2)]
    return jnp.concatenate(parts, axis=0)


def weight_kernel(in_ref, factor_ref, high_ref, low_ref, *refs):
    extras, out_ref = refs[:MEMBERS], refs[MEMBERS]
    grads = jnp.concatenate([piece_grads(in_ref, factor_ref, m) for m in range(MEMBERS)], axis=1)
    high, low = halves(grads)
    terms = sum(
        lax.dot_general(a, b[...], NN, preferred_element_type=F32)
        for a, b in ((high, high_ref), (low, high_ref), (high, low_ref))
    )
    extra = (extras[0][...] + extras[1][...]) + (extras[2][...] + extras[3][...])
    for part in range(4):
        out_ref[pl.ds(part, SHARE, stride=6), :] = terms[share(part), :]
    for part in range(2):
        out_ref[pl.ds(4 + part, SHARE, stride=6), :] = extra[share(part), :]


def cut_kernel(in_ref, *outs):
    for turn in range(MEMBERS):
        first = pl.multiple_of(member_at(turn) * 8, 8)
        rows = in_ref[:, pl.ds(first, 8), :]
        outs[turn][...] = rows.reshape(outs[turn].shape)


def own_kernel(x_ref, mask_ref, g_ref, b_ref, w_ref, bin_ref, hat_ref, scale_ref, factor_ref):
    hat, scale = norm_rows(x_ref[...])
    hat_ref[...] = hat
    scale_ref[...] = jnp.broadcast_to(scale, hat.shape)
    normed = hat * g_ref[...] + b_ref[...]
    mask = cell_mask(mask_ref)
    for side in range(2):
        sig = jax.nn.sigmoid(project(normed, w_ref, bin_ref, 2 * side, mm3))
        value = project(normed, w_ref, bin_ref, 2 * side + 1, mm3)
        open_part = mask * sig
        factor_ref[block(2 * side), :] = open_part * (1.0 - sig) * value
        factor_ref[block(2 * side + 1), :] = open_part


def pair_kernel(
    g_ref, w_ref, dnorm_ref, hat_ref, scale_ref, factor_ref, *refs
):
    cuts, (out_ref, held_ref, sides_ref) = refs[:MEMBERS], refs[MEMBERS:]
    size = 8 * SHARE
    for turn in range(MEMBERS):
        held_ref[pl.ds(member_at(MEMBERS - turn) * size, size), :] = cuts[turn][...]
    for member in range(MEMBERS):
        for n in range(8):
            sides_ref[pl.ds(n * LANES + member, SHARE, stride=MEMBERS), :] = held_ref[
                pl.ds(member * size + n, SHARE, stride=8), :
            ]
    parts = []
    for side in range(2):
        grad = jnp.concatenate([sides_ref[block(4 * side + b), :] for b in range(4)], axis=1)
        parts += [grad * factor_ref[block(2 * side + m), :] for m in range(2)]
    d_normed = mm3(w_ref[:, : 4 * LANES], jnp.concatenate(parts, axis=0), NN)
    d_normed = jnp.transpose(d_normed) + dnorm_ref[...]
    hat = hat_ref[...]
    d_hat = d_normed * g_ref[...]
    first = jnp.mean(d_hat, -1, keepdims=True)
    second = jnp.mean(d_hat * hat, -1, keepdims=True)
    out_ref[...] = scale_ref[...] * (d_hat - first - hat * second)


def sum_kernel(length, in_ref, out_ref):
    terms = in_ref[...]
    total = jnp.sum(terms.reshape(SHARE // 4, 24, LANES), 0)
    mine = (total[0:6] + total[6:12]) + (total[12:18] + total[18:24])
    mine = jnp.concatenate([mine] * 4, axis=0) * (1.0 / length)
    out_ref[...] = jnp.broadcast_to(mine[None], (LANES // 4, 24, LANES)).reshape(out_ref.shape)


def last_kernel(in_ref, win_ref, wout_ref):
    for part in range(4):
        win_ref[:, block(part)] = jnp.transpose(in_ref[every(part, 6), :])
    wout_ref[...] = in_ref[every(4, 6), :]
    win_ref[:, block(4)] = in_ref[every(5, 6), :]


def call(kernel, outs, *args, scratch=(), far=0, work=0):
    many = isinstance(outs, list)
    shapes = [
        jax.ShapeDtypeStruct(s, F32) if isinstance(s, tuple) else s
        for s in (outs if many else [outs])
    ]
    near = pl.BlockSpec(memory_space=pltpu.VMEM)
    held = [pltpu.VMEM(a.shape, a.dtype) for a in args[:far]]

    def body(*refs):
        end = len(args) + len(shapes)
        places = refs[end : end + far]
        copies = [
            pltpu.make_async_copy(refs[n], places[n], refs[-1].at[n]) for n in range(far)
        ]
        for copy in copies:
            copy.start()
        for copy in copies:
            copy.wait()
        kernel(*places, *refs[far:end], *refs[end + far : len(refs) - 1])

    return pl.pallas_call(
        body if far else kernel,
        out_shape=shapes if many else shapes[0],
        in_specs=[pl.BlockSpec(memory_space=pltpu.HBM)] * far + [near] * (len(args) - far),
        out_specs=[near] * len(shapes) if many else near,
        scratch_shapes=held
        + [pltpu.VMEM(s, F32) for s in scratch]
        + ([pltpu.SemaphoreType.DMA((far,))] if far else []),
        cost_estimate=pl.CostEstimate(flops=1000 * work, transcendentals=0, bytes_accessed=work)
        if work
        else None,
        compiler_params=pltpu.CompilerParams(vmem_limit_bytes=24 * 2**20),
    )(*[pltpu.with_memory_space_constraint(a, pltpu.HBM) for a in args[:far]], *args[far:])


def exchange(x, axes=AXES):
    return lax.all_to_all(x, axes, split_axis=0, concat_axis=0, tiled=True)


def exchange_pairs(x, axes=AXES):
    return exchange(x.reshape(-1, 2, LANES), axes).reshape(x.shape)


def fetch(x, turn):
    return lax.ppermute(x, LINE, [((n + turn) % MEMBERS, n) for n in range(MEMBERS)])


def hand(x, turn):
    return lax.ppermute(x, LINE, [(n, (n + turn) % MEMBERS) for n in range(MEMBERS)])


def on_device(
    pair_rep,
    pair_mask,
    ln_in_gain,
    ln_in_bias,
    w_in,
    b_in,
    ln_out_gain,
    ln_out_bias,
    w_out,
    b_out,
    cotangent,
):
    length = pair_rep.shape[1]
    cells = pair_rep.shape[0] * length
    x = pair_rep.reshape(cells, LANES)
    cot = cotangent.reshape(cells, LANES)
    g_in, o_in = ln_in_gain[None], ln_in_bias[None]
    g_out, o_out = ln_out_gain[None], ln_out_bias[None]
    bias_out = b_out[None]

    inputs = (x, pair_mask, g_in, o_in, w_in, b_in)
    sent, pack = call(
        first_kernel, [(8 * LANES, LANES), (cells + 8, LANES)], *inputs, far=len(inputs)
    )
    sides = exchange(sent)
    sides, x_late, pack = lax.optimization_barrier((sides, x, pack))
    back, cg = call(
        side_kernel,
        [(LANES, cells), (cells, LANES)],
        x_late,
        *inputs[2:],
        cot,
        w_out,
        g_out,
        scratch=[(cells, LANES)],
        far=8,
    )
    product = exchange(call(product_kernel, (4 * LANES, LANES), sides))
    packs = [pack] + [fetch(pack, turn) for turn in range(1, MEMBERS)]
    d_product = exchange(call(middle_kernel, (4 * LANES, LANES), product, back))
    update, d_norm, *extras = call(
        update_kernel,
        [(cells, LANES), (cells, LANES)] + [(2 * SHARE, LANES)] * MEMBERS,
        x,
        *inputs[2:],
        cot,
        w_out,
        g_out,
        o_out,
        bias_out,
        product,
        cg,
        far=10,
        scratch=[(cells, LANES), (cells, LANES), (2 * LANES, LANES), (2 * LANES, LANES)],
    )
    high, low, factor = call(
        factor_kernel,
        [jax.ShapeDtypeStruct((MEMBERS * cells, LANES), jnp.bfloat16)] * 2
        + [(MEMBERS * LANES, cells)],
        *packs,
        g_in,
        o_in,
        w_in,
        b_in,
        scratch=[(LANES, LANES), (LANES, LANES)],
        far=8,
    )
    d_product, high, low, factor, extras = lax.optimization_barrier(
        (d_product, high, low, factor, extras)
    )
    extras = [extras[0]] + [hand(extras[turn], turn) for turn in range(1, MEMBERS)]
    d_sides = exchange(call(back_product_kernel, (8 * LANES, LANES), d_product, sides), PLANE)
    terms = call(weight_kernel, (6 * SHARE, LANES), d_sides, factor, high, low, *extras)
    terms, d_sides = lax.optimization_barrier((terms, d_sides))
    terms = exchange_pairs(terms, PLANE)
    cuts = call(
        cut_kernel,
        [(8 * SHARE, LANES)] * MEMBERS,
        d_sides.reshape(SHARE, 8 * MEMBERS, LANES),
    )
    terms, inputs = lax.optimization_barrier((terms, inputs))
    own = call(
        own_kernel, [(cells, LANES), (cells, LANES), (4 * LANES, cells)], *inputs, far=6, work=10**7,
    )
    cuts = [cuts[0]] + [hand(cuts[turn], turn) for turn in range(1, MEMBERS)]
    grad_pair = call(
        pair_kernel,
        (cells, LANES),
        g_in,
        w_in,
        d_norm,
        *own,
        *cuts,
        scratch=[(8 * LANES, LANES), (8 * LANES, LANES)],
        far=3,
    )
    whole = exchange_pairs(
        call(functools.partial(sum_kernel, length), (6 * LANES, LANES), terms)
    )
    d_win, d_wout = call(last_kernel, [w_in.shape, w_out.shape], whole)
    return (update.reshape(pair_rep.shape), grad_pair.reshape(pair_rep.shape), d_win, d_wout)


def solution(mesh):
    whole = P(PARTS, None, None)
    placed = (whole, P(PARTS, None)) + (P(),) * 8 + (whole,)
    return jax.shard_map(
        on_device,
        mesh=jax.sharding.Mesh(mesh.devices.reshape(SIZES), PARTS),
        in_specs=placed,
        out_specs=(whole, whole, P(), P()),
        check_vma=False,
    )
```

time: 113 us -> 112 us (level)
  blocking collectives: 56.1 us -> 25 us
  starting transfers between devices: 12.1 us -> 38 us
  Pallas kernels: 14.9 us -> 21.2 us
  waiting for transfers between devices: 26.1 us -> 24 us
    all_to_all x3 -> x1, blocking collectives: 56.1 us -> 25 us  [exchange(): return lax.all_to_all(x, axes, split_axis=0, concat_axis=0, tiled=True)]
    ppermute x0 -> x9, starting transfers between devices: none -> 13.7 us  [the longest x6 9.9 us: hand(): lax.ppermute(x, LINE, [(n, (n + turn) % MEMBERS) for n in range(MEMBERS)])]
    all_to_all x3 -> x5, starting transfers between devices: 12.1 us -> 24.2 us  [exchange(): return lax.all_to_all(x, axes, split_axis=0, concat_axis=0, tiled=True)]
    pallas_call x10 -> x13, Pallas kernels: 14.9 us -> 21.2 us  [call(): pl.pallas_call(body if far else kernel, out_shape=shapes if many else sha...]
    all_to_all x3 -> x5, waiting for transfers between devices: 26.1 us -> 22.1 us  [exchange(): return lax.all_to_all(x, axes, split_axis=0, concat_axis=0, tiled=True)]
    ppermute x0 -> x9, waiting for transfers between devices: none -> 1.97 us  [the longest x6 1.96 us: hand(): lax.ppermute(x, LINE, [(n, (n + turn) % MEMBERS) for n in range(MEMBERS)])]
    unnamed x26 -> x8, local copies, waits for them, and re-layouts: 2.95 us -> 2.13 us
  transfers between devices with their start and end apart: 3 -> 14, of which waited for: 3 -> 7; matrix products, arithmetic and copies ran while one was open for 0% -> 0% of each run, Pallas kernels for 7% -> 13%
where the time goes in v4:
time: 112 us; the launch traced here: 111 us
  starting transfers between devices  38 us (34%)
  blocking collectives  25 us (22%)
  waiting for transfers between devices  24 us (21%)
  Pallas kernels  21.2 us (19%)
  local copies, waits for them, and re-layouts  2.13 us (2%)
    all_to_all x1, blocking collectives, exchange(): return lax.all_to_all(x, axes, split_axis=0, concat_axis=0, tiled=True)  25 us
    all_to_all x5, starting transfers between devices, exchange(): return lax.all_to_all(x, axes, split_axis=0, concat_axis=0, tiled=True)  24.2 us
    all_to_all x5, waiting for transfers between devices, exchange(): return lax.all_to_all(x, axes, split_axis=0, concat_axis=0, tiled=True)  22.1 us
    pallas_call x13, Pallas kernels, call(): pl.pallas_call(body if far else kernel, out_shape=shapes if many else sha...  21.2 us
    ppermute x6, starting transfers between devices, hand(): lax.ppermute(x, LINE, [(n, (n + turn) % MEMBERS) for n in range(MEMBERS)])  9.9 us
    ppermute x3, starting transfers between devices, fetch(): lax.ppermute(x, LINE, [((n + turn) % MEMBERS, n) for n in range(MEMBERS)])  3.83 us
  transfers between devices with their start and end apart: 14, of which 7 were waited for; matrix products, arithmetic and copies ran while one was open for 0% of the time, Pallas kernels for 13%

profile of v4, /device:TPU:1, one launch (start us, length us, event | category | flops | bytes accessed | tf_op | source)
XLA Modules:
  0.0 111.1 jit_solution(7034008613105159000)
XLA Ops:
  0.6 2.1 %shard_map.138 = (f32[1024,128]{1,0:T(8,128)S(1)}, f32[520,128]{1,0:T(8,128)S(1)}) custom-call(f32[512,128]{1,0:T(8,128)} %bitcast.31, s32[2,256]{1,0:T(2,128)} %refs_1_.3, f32[1,128]{1,0:T(1,128)} %bitcast.38, f32[1,128]{1,0:T(1,128)} %bitcast.44, f32[128,640]{1,0:T(8,128)} %refs_1_.4, f32[640]{0:T(1024)} %refs_5_.2), custom_call_target="tpu_custom_call" | custom-call | tf_op jit(solution)/shard_map/pallas_call | solution.py:365
  2.7 25.0 %all_to_all.56 = f32[128,8,128]{2,1,0:T(8,128)S(1)} all-to-all(f32[128,8,128]{2,1,0:T(8,128)S(1)} %bitcast.29), channel_id=1, replica_groups=mesh['x_high'=2,'z'=4,'y'=4,'x_low'=2,'core'=2] {'x_low','core','x_high'..., dimensions={0} | all-to-all | bytes 1048576 | tf_op jit(solution)/shard_map/all_to_all | solution.py:381
  27.7 1.0 shard_map.139
  28.7 3.9 %all-to-all-start.1 = ((f32[128,4,128]{2,1,0:T(4,128)}), f32[128,4,128]{2,1,0:T(4,128)S(1)}, u32[]{:S(2)}, u32[]{:S(2)}) async-start(f32[128,4,128]{2,1,0:T(4,128)} %bitcast.9), calls=%async_computation.1 | async-start | bytes 524288 | tf_op jit(solution)/shard_map/all_to_all | solution.py:381
  32.6 2.7 %collective-permute-start = (f32[520,128]{1,0:T(8,128)S(1)}, f32[520,128]{1,0:T(8,128)S(1)}, u32[]{:S(2)}, u32[]{:S(2)}) collective-permute-start(f32[520,128]{1,0:T(8,128)S(1)} %get-tuple-element.54.refs_0_), channel_id=1, source_target_pairs={{4,0},{8,4},{12,8},{0,12},{5,1},{9,5},{13,9},{1,13},{6,2},{10,6},{... | collective-permute-start | bytes 798728 | tf_op jit(solution)/shard_map/ppermute | solution.py:389
  36.5 2.3 %shard_map.140 = (f32[128,512]{1,0:T(8,128)S(1)}, f32[512,128]{1,0:T(8,128)S(1)}) custom-call(f32[512,128]{1,0:T(8,128)} %bitcast.32, f32[1,128]{1,0:T(1,128)} %bitcast.39, f32[1,128]{1,0:T(1,128)} %bitcast.45, f32[128,640]{1,0:T(8,128)} %refs_1_.4, f32[640]{0:T(1024)} %refs_5_.2, f32[512,128]{1,0:T(8,128)} %bitcast.35, f32[128,128]{1,0:T(8,128)} %refs_6_.4, ...), custom_call_target="tpu_custom_call" | custom-call | tf_op jit(solution)/shard_map/pallas_call | solution.py:365
  38.8 5.1 %all-to-all-done.1 = f32[128,4,128]{2,1,0:T(4,128)S(1)} async-done(((f32[128,4,128]{2,1,0:T(4,128)}), f32[128,4,128]{2,1,0:T(4,128)S(1)}, u32[]{:S(2)}, u32[]{:S(2)}) %all-to-all-start.1) | async-done | bytes 262176 | tf_op jit(solution)/shard_map/all_to_all | solution.py:381
  43.9 0.9 shard_map.142
  44.8 4.6 %all-to-all-start.2 = ((f32[128,4,128]{2,1,0:T(4,128)}), f32[128,4,128]{2,1,0:T(4,128)S(1)}, u32[]{:S(2)}, u32[]{:S(2)}) async-start(f32[128,4,128]{2,1,0:T(4,128)} %bitcast.12), calls=%async_computation.2 | async-start | bytes 524288 | tf_op jit(solution)/shard_map/all_to_all | solution.py:381
  49.4 3.1 %shard_map.141 = (f32[512,128]{1,0:T(8,128)}, f32[512,128]{1,0:T(8,128)S(1)}, f32[64,128]{1,0:T(8,128)S(1)}, f32[64,128]{1,0:T(8,128)S(1)}, f32[64,128]{1,0:T(8,128)S(1)}, /*index=5*/f32[64,128]{1,0:T(8,128)S(1)}) custom-call(f32[512,128]{1,0:T(8,128)} %bitcast.33, f32[1,128]{1,0:T(1,128)} %bitcast.40, f32[1,128]{1,0:T(1,128)} %bitcast.46, ...), custom_call_target="tpu_custom_call" | custom-call | tf_op jit(solution)/shard_map/pallas_call | solution.py:365
  54.7 2.7 %shard_map.143 = (bf16[2048,128]{1,0:T(8,128)(2,1)S(1)}, bf16[2048,128]{1,0:T(8,128)(2,1)S(1)}, f32[512,512]{1,0:T(8,128)S(1)}) custom-call(f32[520,128]{1,0:T(8,128)} %copy-done, f32[520,128]{1,0:T(8,128)} %copy-done.2, f32[520,128]{1,0:T(8,128)} %copy-done.3, f32[520,128]{1,0:T(8,128)} %collective-permute-done.2.refs_3_, f32[1,128]{1,0:T(1,128)} %bitcast.41, ...), custom_call_target="tpu_custom_call" | custom-call | tf_op jit(solution)/shard_map/pallas_call | solution.py:365
  57.3 3.4 %all-to-all-done.2 = f32[128,4,128]{2,1,0:T(4,128)S(1)} async-done(((f32[128,4,128]{2,1,0:T(4,128)}), f32[128,4,128]{2,1,0:T(4,128)S(1)}, u32[]{:S(2)}, u32[]{:S(2)}) %all-to-all-start.2) | async-done | bytes 262176 | tf_op jit(solution)/shard_map/all_to_all | solution.py:381
  60.7 1.3 %shard_map.144 = f32[1024,128]{1,0:T(8,128)} custom-call(f32[512,128]{1,0:T(8,128)S(1)} %bitcast.28, f32[1024,128]{1,0:T(8,128)S(1)} %bitcast.23), custom_call_target="tpu_custom_call" | custom-call | tf_op jit(solution)/shard_map/pallas_call | solution.py:365
  61.9 4.4 %all-to-all-start.3 = ((f32[32,32,128]{2,1,0:T(8,128)}), f32[32,32,128]{2,1,0:T(8,128)S(1)}, u32[]{:S(2)}, u32[]{:S(2)}) async-start(f32[32,32,128]{2,1,0:T(8,128)} %bitcast.14), calls=%async_computation.3 | async-start | bytes 1048576 | tf_op jit(solution)/shard_map/all_to_all | solution.py:381
  66.4 1.3 %collective-permute-start.3 = (f32[64,128]{1,0:T(8,128)S(1)}, f32[64,128]{1,0:T(8,128)S(1)}, u32[]{:S(2)}, u32[]{:S(2)}) collective-permute-start(f32[64,128]{1,0:T(8,128)S(1)} %get-tuple-element.67), channel_id=1, source_target_pairs={{0,4},{4,8},{8,12},{12,0},{1,5},{5,9},{9,13},{13,1},{2,6},{6,10},{... | collective-permute-start | bytes 98312 | tf_op jit(solution)/shard_map/ppermute | solution.py:393
  67.7 2.5 %collective-permute-start.4 = (f32[64,128]{1,0:T(8,128)S(1)}, f32[64,128]{1,0:T(8,128)S(1)}, u32[]{:S(2)}, u32[]{:S(2)}) collective-permute-start(f32[64,128]{1,0:T(8,128)S(1)} %get-tuple-element.68), channel_id=1, source_target_pairs={{0,8},{4,12},{8,0},{12,4},{1,9},{5,13},{9,1},{13,5},{2,10},{6,14},... | collective-permute-start | bytes 98312 | tf_op jit(solution)/shard_map/ppermute | solution.py:393
  70.2 1.1 collective-permute-start.5
  71.3 1.0 collective-permute-done.4.refs_2_
  72.4 0.9 collective-permute-done.5.refs_3_
  73.3 3.6 %all-to-all-done.3 = f32[32,32,128]{2,1,0:T(8,128)S(1)} async-done(((f32[32,32,128]{2,1,0:T(8,128)}), f32[32,32,128]{2,1,0:T(8,128)S(1)}, u32[]{:S(2)}, u32[]{:S(2)}) %all-to-all-start.3) | async-done | bytes 524320 | tf_op jit(solution)/shard_map/all_to_all | solution.py:381
  76.9 1.5 %shard_map.145 = f32[192,128]{1,0:T(8,128)} custom-call(f32[1024,128]{1,0:T(8,128)S(1)} %bitcast.24, f32[512,512]{1,0:T(8,128)S(1)} %get-tuple-element.63.factor_ref, bf16[2048,128]{1,0:T(8,128)(2,1)S(1)} %get-tuple-element.64.high_ref, bf16[2048,128]{1,0:T(8,128)(2,1)S(1)} %get-tuple-element.65.low_ref, f32[64,128]{1,0:T(8,128)S(1)} %get-tuple-element.66.refs_0_, ...), custom_call_target="tpu_custom_call" | custom-call | tf_op jit(solution)/shard_map/pallas_call | solution.py:365
  78.4 5.4 %all-to-all-start.4 = ((f32[96,2,128]{2,1,0:T(2,128)}), f32[96,2,128]{2,1,0:T(2,128)S(1)}, u32[]{:S(2)}, u32[]{:S(2)}) async-start(f32[96,2,128]{2,1,0:T(2,128)} %bitcast.16), calls=%async_computation.4 | async-start | bytes 196608 | tf_op jit(solution)/shard_map/all_to_all | solution.py:381
  83.9 1.3 %collective-permute-start.6 = (f32[256,128]{1,0:T(8,128)S(1)}, f32[256,128]{1,0:T(8,128)S(1)}, u32[]{:S(2)}, u32[]{:S(2)}) collective-permute-start(f32[256,128]{1,0:T(8,128)S(1)} %get-tuple-element.82), channel_id=1, source_target_pairs={{0,4},{4,8},{8,12},{12,0},{1,5},{5,9},{9,13},{13,1},{2,6},{6,10},{... | collective-permute-start | bytes 393224 | tf_op jit(solution)/shard_map/ppermute | solution.py:393
  85.2 2.5 %collective-permute-start.7 = (f32[256,128]{1,0:T(8,128)S(1)}, f32[256,128]{1,0:T(8,128)S(1)}, u32[]{:S(2)}, u32[]{:S(2)}) collective-permute-start(f32[256,128]{1,0:T(8,128)S(1)} %get-tuple-element.83), channel_id=1, source_target_pairs={{0,8},{4,12},{8,0},{12,4},{1,9},{5,13},{9,1},{13,5},{2,10},{6,14},... | collective-permute-start | bytes 393224 | tf_op jit(solution)/shard_map/ppermute | solution.py:393
  87.7 1.1 collective-permute-start.8
  88.8 2.4 %all-to-all-done.4 = f32[96,2,128]{2,1,0:T(2,128)S(1)} async-done(((f32[96,2,128]{2,1,0:T(2,128)}), f32[96,2,128]{2,1,0:T(2,128)S(1)}, u32[]{:S(2)}, u32[]{:S(2)}) %all-to-all-start.4) | async-done | bytes 98336 | tf_op jit(solution)/shard_map/all_to_all | solution.py:381
  91.2 0.8 shard_map.149
  91.9 5.9 %all-to-all-start.5 = ((f32[384,2,128]{2,1,0:T(2,128)}), f32[384,2,128]{2,1,0:T(2,128)S(1)}, u32[]{:S(2)}, u32[]{:S(2)}) async-start(f32[384,2,128]{2,1,0:T(2,128)} %bitcast.20), calls=%async_computation.5 | async-start | bytes 786432 | tf_op jit(solution)/shard_map/all_to_all | solution.py:381
  97.9 2.0 %shard_map.146 = (f32[512,128]{1,0:T(8,128)S(1)}, f32[512,128]{1,0:T(8,128)S(1)}, f32[512,512]{1,0:T(8,128)S(1)}) custom-call(f32[512,128]{1,0:T(8,128)} %bitcast.34, s32[2,256]{1,0:T(2,128)} %refs_1_.3, f32[1,128]{1,0:T(1,128)} %bitcast.42, f32[1,128]{1,0:T(1,128)} %bitcast.48, f32[128,640]{1,0:T(8,128)} %refs_1_.4, f32[640]{0:T(1024)} %refs_5_.2), custom_call_target="tpu_custom_call" | custom-call | flops 10000000000 | bytes 10000000 | tf_op jit(solution)/shard_map/pallas_call | solution.py:365
  99.9 2.7 %shard_map.148 = f32[512,128]{1,0:T(8,128)} custom-call(f32[1,128]{1,0:T(1,128)} %bitcast.43, f32[128,640]{1,0:T(8,128)} %refs_1_.4, f32[512,128]{1,0:T(8,128)} %copy-done.1, f32[512,128]{1,0:T(8,128)S(1)} %get-tuple-element.77.refs_3_, f32[512,128]{1,0:T(8,128)S(1)} %get-tuple-element.78.refs_4_, f32[512,512]{1,0:T(8,128)S(1)} %get-tuple-element.79.refs_5_, ...), custom_call_target="tpu_custom_call" | custom-call | tf_op jit(solution)/shard_map/pallas_call | solution.py:365
  102.6 7.6 %all-to-all-done.5 = f32[384,2,128]{2,1,0:T(2,128)S(1)} async-done(((f32[384,2,128]{2,1,0:T(2,128)}), f32[384,2,128]{2,1,0:T(2,128)S(1)}, u32[]{:S(2)}, u32[]{:S(2)}) %all-to-all-start.5) | async-done | bytes 393248 | tf_op jit(solution)/shard_map/all_to_all | solution.py:381
  110.3 0.9 shard_map.150
  (18 shorter events, 3.3 us)
Async XLA Ops:
  2.7 33.2 %copy-start = (f32[520,128]{1,0:T(8,128)}, f32[520,128]{1,0:T(8,128)S(1)}, u32[]{:S(2)}) copy-start(f32[520,128]{1,0:T(8,128)S(1)} %get-tuple-element.54.refs_0_) | copy-start | bytes 798724
  28.7 15.2 %all-to-all-start.1 = ((f32[128,4,128]{2,1,0:T(4,128)}), f32[128,4,128]{2,1,0:T(4,128)S(1)}, u32[]{:S(2)}, u32[]{:S(2)}) async-start(f32[128,4,128]{2,1,0:T(4,128)} %bitcast.9), calls=%async_computation.1 | async-start | bytes 524288 | tf_op jit(solution)/shard_map/all_to_all | solution.py:381
  32.6 20.6 %collective-permute-start = (f32[520,128]{1,0:T(8,128)S(1)}, f32[520,128]{1,0:T(8,128)S(1)}, u32[]{:S(2)}, u32[]{:S(2)}) collective-permute-start(f32[520,128]{1,0:T(8,128)S(1)} %get-tuple-element.54.refs_0_), channel_id=1, source_target_pairs={{4,0},{8,4},{12,8},{0,12},{5,1},{9,5},{13,9},{1,13},{6,2},{10,6},{... | collective-permute-start | bytes 798728 | tf_op jit(solution)/shard_map/ppermute | solution.py:389
  35.4 17.9 %collective-permute-start.1 = (f32[520,128]{1,0:T(8,128)S(1)}, f32[520,128]{1,0:T(8,128)S(1)}, u32[]{:S(2)}, u32[]{:S(2)}) collective-permute-start(f32[520,128]{1,0:T(8,128)S(1)} %get-tuple-element.54.refs_0_), channel_id=1, source_target_pairs={{8,0},{12,4},{0,8},{4,12},{9,1},{13,5},{1,9},{5,13},{10,2},{14,6},... | collective-permute-start | bytes 798728 | tf_op jit(solution)/shard_map/ppermute | solution.py:389
  35.9 18.8 %collective-permute-start.2 = (f32[520,128]{1,0:T(8,128)S(1)}, f32[520,128]{1,0:T(8,128)}, u32[]{:S(2)}, u32[]{:S(2)}) collective-permute-start(f32[520,128]{1,0:T(8,128)S(1)} %get-tuple-element.54.refs_0_), channel_id=1, source_target_pairs={{12,0},{0,4},{4,8},{8,12},{13,1},{1,5},{5,9},{9,13},{14,2},{2,6},{... | collective-permute-start | bytes 798728 | tf_op jit(solution)/shard_map/ppermute | solution.py:389
  44.8 15.9 %all-to-all-start.2 = ((f32[128,4,128]{2,1,0:T(4,128)}), f32[128,4,128]{2,1,0:T(4,128)S(1)}, u32[]{:S(2)}, u32[]{:S(2)}) async-start(f32[128,4,128]{2,1,0:T(4,128)} %bitcast.12), calls=%async_computation.2 | async-start | bytes 524288 | tf_op jit(solution)/shard_map/all_to_all | solution.py:381
  52.5 0.7 copy-start.1
  53.2 0.7 copy-start.2
  53.9 0.7 copy-start.3
  61.9 14.9 %all-to-all-start.3 = ((f32[32,32,128]{2,1,0:T(8,128)}), f32[32,32,128]{2,1,0:T(8,128)S(1)}, u32[]{:S(2)}, u32[]{:S(2)}) async-start(f32[32,32,128]{2,1,0:T(8,128)} %bitcast.14), calls=%async_computation.3 | async-start | bytes 1048576 | tf_op jit(solution)/shard_map/all_to_all | solution.py:381
  66.4 5.0 %collective-permute-start.3 = (f32[64,128]{1,0:T(8,128)S(1)}, f32[64,128]{1,0:T(8,128)S(1)}, u32[]{:S(2)}, u32[]{:S(2)}) collective-permute-start(f32[64,128]{1,0:T(8,128)S(1)} %get-tuple-element.67), channel_id=1, source_target_pairs={{0,4},{4,8},{8,12},{12,0},{1,5},{5,9},{9,13},{13,1},{2,6},{6,10},{... | collective-permute-start | bytes 98312 | tf_op jit(solution)/shard_map/ppermute | solution.py:393
  67.7 4.7 %collective-permute-start.4 = (f32[64,128]{1,0:T(8,128)S(1)}, f32[64,128]{1,0:T(8,128)S(1)}, u32[]{:S(2)}, u32[]{:S(2)}) collective-permute-start(f32[64,128]{1,0:T(8,128)S(1)} %get-tuple-element.68), channel_id=1, source_target_pairs={{0,8},{4,12},{8,0},{12,4},{1,9},{5,13},{9,1},{13,5},{2,10},{6,14},... | collective-permute-start | bytes 98312 | tf_op jit(solution)/shard_map/ppermute | solution.py:393
  70.2 3.1 %collective-permute-start.5 = (f32[64,128]{1,0:T(8,128)S(1)}, f32[64,128]{1,0:T(8,128)S(1)}, u32[]{:S(2)}, u32[]{:S(2)}) collective-permute-start(f32[64,128]{1,0:T(8,128)S(1)} %get-tuple-element.69), channel_id=1, source_target_pairs={{0,12},{4,0},{8,4},{12,8},{1,13},{5,1},{9,5},{13,9},{2,14},{6,2},{... | collective-permute-start | bytes 98312 | tf_op jit(solution)/shard_map/ppermute | solution.py:393
  78.4 12.8 %all-to-all-start.4 = ((f32[96,2,128]{2,1,0:T(2,128)}), f32[96,2,128]{2,1,0:T(2,128)S(1)}, u32[]{:S(2)}, u32[]{:S(2)}) async-start(f32[96,2,128]{2,1,0:T(2,128)} %bitcast.16), calls=%async_computation.4 | async-start | bytes 196608 | tf_op jit(solution)/shard_map/all_to_all | solution.py:381
  83.9 16.0 %collective-permute-start.6 = (f32[256,128]{1,0:T(8,128)S(1)}, f32[256,128]{1,0:T(8,128)S(1)}, u32[]{:S(2)}, u32[]{:S(2)}) collective-permute-start(f32[256,128]{1,0:T(8,128)S(1)} %get-tuple-element.82), channel_id=1, source_target_pairs={{0,4},{4,8},{8,12},{12,0},{1,5},{5,9},{9,13},{13,1},{2,6},{6,10},{... | collective-permute-start | bytes 393224 | tf_op jit(solution)/shard_map/ppermute | solution.py:393
  85.2 14.7 %collective-permute-start.7 = (f32[256,128]{1,0:T(8,128)S(1)}, f32[256,128]{1,0:T(8,128)S(1)}, u32[]{:S(2)}, u32[]{:S(2)}) collective-permute-start(f32[256,128]{1,0:T(8,128)S(1)} %get-tuple-element.83), channel_id=1, source_target_pairs={{0,8},{4,12},{8,0},{12,4},{1,9},{5,13},{9,1},{13,5},{2,10},{6,14},... | collective-permute-start | bytes 393224 | tf_op jit(solution)/shard_map/ppermute | solution.py:393
  87.7 12.2 %collective-permute-start.8 = (f32[256,128]{1,0:T(8,128)S(1)}, f32[256,128]{1,0:T(8,128)S(1)}, u32[]{:S(2)}, u32[]{:S(2)}) collective-permute-start(f32[256,128]{1,0:T(8,128)S(1)} %get-tuple-element.84), channel_id=1, source_target_pairs={{0,12},{4,0},{8,4},{12,8},{1,13},{5,1},{9,5},{13,9},{2,14},{6,2},{... | collective-permute-start | bytes 393224 | tf_op jit(solution)/shard_map/ppermute | solution.py:393
  91.9 18.3 %all-to-all-start.5 = ((f32[384,2,128]{2,1,0:T(2,128)}), f32[384,2,128]{2,1,0:T(2,128)S(1)}, u32[]{:S(2)}, u32[]{:S(2)}) async-start(f32[384,2,128]{2,1,0:T(2,128)} %bitcast.20), calls=%async_computation.5 | async-start | bytes 786432 | tf_op jit(solution)/shard_map/all_to_all | solution.py:381

commit v5 on v4

--- a/solution.py
+++ b/solution.py
@@ -90,12 +90,13 @@
     hat, _ = norm_rows(x_ref[...])
     normed = hat * g_ref[...] + b_ref[...]
     mask = cell_mask(mask_ref)
+    weights = jnp.concatenate([jnp.transpose(w_ref[:, block(p)]) for p in range(4)], axis=0)
+    bias = jnp.concatenate(
+        [column(bin_ref[pl.ds(p * LANES, LANES)][None]) for p in range(4)], axis=0
+    )
+    pieces = mm3(weights, normed, NT) + jnp.tile(bias, (1, 4))
     for side in range(2):
-        value = (
-            mask
-            * jax.nn.sigmoid(project(normed, w_ref, bin_ref, 2 * side, mm3))
-            * project(normed, w_ref, bin_ref, 2 * side + 1, mm3)
-        )
+        value = mask * jax.nn.sigmoid(pieces[block(2 * side)]) * pieces[block(2 * side + 1)]
         for b in range(4):
             out_ref[every(4 * side + b, 8), :] = value[:, block(b)]
     pack_ref[0 : 4 * LANES, :] = x_ref[...]
@@ -209,9 +210,8 @@
     return jnp.concatenate([mm(pick, w_ref[:, block(p)], NT) for p in range(4)], axis=0)
 
 
-def factor_kernel(*refs):
-    packs, refs = refs[:MEMBERS], refs[MEMBERS:]
-    g_ref, b_ref, w_ref, bin_ref, high_ref, low_ref, factor_ref, weights_ref, bias_ref = refs
+def factor_kernel(turns, g_ref, b_ref, w_ref, bin_ref, *refs):
+    packs, (high_ref, low_ref, factor_ref, weights_ref, bias_ref) = refs[: len(turns)], refs[-5:]
     pick = mine()
     weights_ref[...] = my_weights(pick, w_ref)
     for p in range(4):
@@ -219,8 +219,7 @@
         bias_ref[share(p), :] = jnp.broadcast_to(
             jnp.sum(pick * row, axis=1, keepdims=True), (SHARE, LANES)
         )
-    for turn in range(MEMBERS):
-        pack = packs[turn]
+    for pack, turn in zip(packs, turns):
         hat, _ = norm_rows(pack[0 : 4 * LANES, :])
         normed = hat * g_ref[...] + b_ref[...]
         member = member_at(turn)
@@ -341,7 +340,8 @@
     win_ref[:, block(4)] = in_ref[every(5, 6), :]
 
 
-def call(kernel, outs, *args, scratch=(), far=0, work=0):
+def call(kernel, outs, *given, args=(), scratch=(), far=0, work=0, aliases={}):
+    args = (*given, *args)
     many = isinstance(outs, list)
     shapes = [
         jax.ShapeDtypeStruct(s, F32) if isinstance(s, tuple) else s
@@ -370,6 +370,7 @@
         scratch_shapes=held
         + [pltpu.VMEM(s, F32) for s in scratch]
         + ([pltpu.SemaphoreType.DMA((far,))] if far else []),
+        input_output_aliases=aliases,
         cost_estimate=pl.CostEstimate(flops=1000 * work, transcendentals=0, bytes_accessed=work)
         if work
         else None,
@@ -432,7 +433,8 @@
         far=8,
     )
     product = exchange(call(product_kernel, (4 * LANES, LANES), sides))
-    packs = [pack] + [fetch(pack, turn) for turn in range(1, MEMBERS)]
+    packs = [pack, fetch(pack, 1), fetch(pack, 3)]
+    across = fetch(packs[1], 1)
     d_product = exchange(call(middle_kernel, (4 * LANES, LANES), product, back))
     update, d_norm, *extras = call(
         update_kernel,
@@ -449,20 +451,24 @@
         far=10,
         scratch=[(cells, LANES), (cells, LANES), (2 * LANES, LANES), (2 * LANES, LANES)],
     )
-    high, low, factor = call(
-        factor_kernel,
-        [jax.ShapeDtypeStruct((MEMBERS * cells, LANES), jnp.bfloat16)] * 2
+    factors = functools.partial(
+        call,
+        outs=[jax.ShapeDtypeStruct((MEMBERS * cells, LANES), jnp.bfloat16)] * 2
         + [(MEMBERS * LANES, cells)],
-        *packs,
-        g_in,
-        o_in,
-        w_in,
-        b_in,
         scratch=[(LANES, LANES), (LANES, LANES)],
-        far=8,
-    )
-    d_product, high, low, factor, extras = lax.optimization_barrier(
-        (d_product, high, low, factor, extras)
+    )
+    prelude = (g_in, o_in, w_in, b_in)
+    high, low, factor = factors(
+        functools.partial(factor_kernel, (0, 1, 3)), args=(*prelude, *packs), far=7
+    )
+    d_product, high, low, factor, extras, across = lax.optimization_barrier(
+        (d_product, high, low, factor, extras, across)
+    )
+    high, low, factor = factors(
+        functools.partial(factor_kernel, (2,)),
+        args=(*prelude, across, high, low, factor),
+        far=5,
+        aliases={5: 0, 6: 1, 7: 2},
     )
     extras = [extras[0]] + [hand(extras[turn], turn) for turn in range(1, MEMBERS)]
     d_sides = exchange(call(back_product_kernel, (8 * LANES, LANES), d_product, sides), PLANE)

time: 112 us -> 111 us (level)
  starting transfers between devices: 38 us -> 33.9 us
  waiting for transfers between devices: 24 us -> 27.7 us
  local copies, waits for them, and re-layouts: 2.13 us -> 0.7 us
  Pallas kernels: 21.2 us -> 22.6 us
    all_to_all x5, waiting for transfers between devices: 22.1 us -> 27.6 us  [exchange(): return lax.all_to_all(x, axes, split_axis=0, concat_axis=0, tiled=True)]
    ppermute x6, starting transfers between devices: 9.9 us -> 7.29 us  [hand(): lax.ppermute(x, LINE, [(n, (n + turn) % MEMBERS) for n in range(MEMBERS)])]
    ppermute x6, waiting for transfers between devices: 1.96 us -> 0.07 us  [hand(): lax.ppermute(x, LINE, [(n, (n + turn) % MEMBERS) for n in range(MEMBERS)])]
    unnamed x8 -> x6, local copies, waits for them, and re-layouts: 2.13 us -> 0.7 us
    all_to_all x5, starting transfers between devices: 24.2 us -> 22.9 us  [exchange(): return lax.all_to_all(x, axes, split_axis=0, concat_axis=0, tiled=True)]
    pallas_call x13 -> x14, Pallas kernels: 21.2 us -> 22.6 us  [call(): pl.pallas_call(body if far else kernel, out_shape=shapes if many else sha...]
  transfers between devices with their start and end apart: 14 -> 14, of which waited for: 7 -> 6; matrix products, arithmetic and copies ran while one was open for 0% -> 0% of each run, Pallas kernels for 13% -> 15%
where the time goes in v5:
time: 111 us
  starting transfers between devices  33.9 us (31%)
  waiting for transfers between devices  27.7 us (25%)
  blocking collectives  25 us (23%)
  Pallas kernels  22.6 us (20%)
    all_to_all x5, waiting for transfers between devices, exchange(): return lax.all_to_all(x, axes, split_axis=0, concat_axis=0, tiled=True)  27.6 us
    all_to_all x1, blocking collectives, exchange(): return lax.all_to_all(x, axes, split_axis=0, concat_axis=0, tiled=True)  25 us
    all_to_all x5, starting transfers between devices, exchange(): return lax.all_to_all(x, axes, split_axis=0, concat_axis=0, tiled=True)  22.9 us
    pallas_call x14, Pallas kernels, call(): pl.pallas_call(body if far else kernel, out_shape=shapes if many else sha...  22.6 us
    ppermute x6, starting transfers between devices, hand(): lax.ppermute(x, LINE, [(n, (n + turn) % MEMBERS) for n in range(MEMBERS)])  7.29 us
    ppermute x3, starting transfers between devices, fetch(): lax.ppermute(x, LINE, [((n + turn) % MEMBERS, n) for n in range(MEMBERS)])  3.7 us
  transfers between devices with their start and end apart: 14, of which 6 were waited for; matrix products, arithmetic and copies ran while one was open for 0% of the time, Pallas kernels for 15%

profile of v5, /device:TPU:1, one launch (start us, length us, event | category | flops | bytes accessed | tf_op | source)
XLA Modules:
  0.0 110.7 jit_solution(7526719790688754987)
XLA Ops:
  0.6 1.9 %shard_map.138 = (f32[1024,128]{1,0:T(8,128)S(1)}, f32[520,128]{1,0:T(8,128)S(1)}) custom-call(f32[512,128]{1,0:T(8,128)} %bitcast.31, s32[2,256]{1,0:T(2,128)} %refs_1_.3, f32[1,128]{1,0:T(1,128)} %bitcast.38, f32[1,128]{1,0:T(1,128)} %bitcast.45, f32[128,640]{1,0:T(8,128)} %refs_1_.4, f32[640]{0:T(1024)} %refs_5_.2), custom_call_target="tpu_custom_call" | custom-call | tf_op jit(solution)/shard_map/pallas_call | solution.py:365
  2.5 25.0 %all_to_all.56 = f32[128,8,128]{2,1,0:T(8,128)S(1)} all-to-all(f32[128,8,128]{2,1,0:T(8,128)S(1)} %bitcast.29), channel_id=1, replica_groups=mesh['x_high'=2,'z'=4,'y'=4,'x_low'=2,'core'=2] {'x_low','core','x_high'..., dimensions={0} | all-to-all | bytes 1048576 | tf_op jit(solution)/shard_map/all_to_all | solution.py:382
  27.5 0.8 collective-permute-start
  28.3 1.0 shard_map.139
  29.4 4.7 %all-to-all-start.1 = ((f32[128,4,128]{2,1,0:T(4,128)}), f32[128,4,128]{2,1,0:T(4,128)S(1)}, u32[]{:S(2)}, u32[]{:S(2)}) async-start(f32[128,4,128]{2,1,0:T(4,128)} %bitcast.9), calls=%async_computation.1 | async-start | bytes 524288 | tf_op jit(solution)/shard_map/all_to_all | solution.py:382
  34.1 1.5 %collective-permute-start.1 = (f32[520,128]{1,0:T(8,128)S(1)}, f32[520,128]{1,0:T(8,128)}, u32[]{:S(2)}, u32[]{:S(2)}) collective-permute-start(f32[520,128]{1,0:T(8,128)S(1)} %get-tuple-element.58.refs_4_), channel_id=1, source_target_pairs={{12,0},{0,4},{4,8},{8,12},{13,1},{1,5},{5,9},{9,13},{14,2},{2,6},{... | collective-permute-start | bytes 798728 | tf_op jit(solution)/shard_map/ppermute | solution.py:390
  35.5 1.5 %collective-permute-start.2 = (f32[520,128]{1,0:T(8,128)}, f32[520,128]{1,0:T(8,128)S(1)}, u32[]{:S(2)}, u32[]{:S(2)}) collective-permute-start(f32[520,128]{1,0:T(8,128)} %collective-permute-done.refs_5_), channel_id=1, source_target_pairs={{4,0},{8,4},{12,8},{0,12},{5,1},{9,5},{13,9},{1,13},{6,2},{10,6},{... | collective-permute-start | bytes 798728 | tf_op jit(solution)/shard_map/ppermute | solution.py:390
  37.0 2.3 %shard_map.140 = (f32[128,512]{1,0:T(8,128)S(1)}, f32[512,128]{1,0:T(8,128)S(1)}) custom-call(f32[512,128]{1,0:T(8,128)} %bitcast.32, f32[1,128]{1,0:T(1,128)} %bitcast.39, f32[1,128]{1,0:T(1,128)} %bitcast.46, f32[128,640]{1,0:T(8,128)} %refs_1_.4, f32[640]{0:T(1024)} %refs_5_.2, f32[512,128]{1,0:T(8,128)} %bitcast.35, f32[128,128]{1,0:T(8,128)} %refs_6_.3, ...), custom_call_target="tpu_custom_call" | custom-call | tf_op jit(solution)/shard_map/pallas_call | solution.py:365
  39.3 6.0 %all-to-all-done.1 = f32[128,4,128]{2,1,0:T(4,128)S(1)} async-done(((f32[128,4,128]{2,1,0:T(4,128)}), f32[128,4,128]{2,1,0:T(4,128)S(1)}, u32[]{:S(2)}, u32[]{:S(2)}) %all-to-all-start.1) | async-done | bytes 262176 | tf_op jit(solution)/shard_map/all_to_all | solution.py:382
  45.3 0.9 shard_map.142
  46.2 3.9 %all-to-all-start.2 = ((f32[128,4,128]{2,1,0:T(4,128)}), f32[128,4,128]{2,1,0:T(4,128)S(1)}, u32[]{:S(2)}, u32[]{:S(2)}) async-start(f32[128,4,128]{2,1,0:T(4,128)} %bitcast.12), calls=%async_computation.2 | async-start | bytes 524288 | tf_op jit(solution)/shard_map/all_to_all | solution.py:382
  50.1 3.1 %shard_map.141 = (f32[512,128]{1,0:T(8,128)}, f32[512,128]{1,0:T(8,128)S(1)}, f32[64,128]{1,0:T(8,128)S(1)}, f32[64,128]{1,0:T(8,128)S(1)}, f32[64,128]{1,0:T(8,128)S(1)}, /*index=5*/f32[64,128]{1,0:T(8,128)S(1)}) custom-call(f32[512,128]{1,0:T(8,128)} %bitcast.33, f32[1,128]{1,0:T(1,128)} %bitcast.40, f32[1,128]{1,0:T(1,128)} %bitcast.47, ...), custom_call_target="tpu_custom_call" | custom-call | tf_op jit(solution)/shard_map/pallas_call | solution.py:365
  53.2 0.7 copy-done.1
  53.9 2.3 %shard_map.143 = (bf16[2048,128]{1,0:T(8,128)(2,1)S(1)}, bf16[2048,128]{1,0:T(8,128)(2,1)S(1)}, f32[512,512]{1,0:T(8,128)S(1)}) custom-call(f32[1,128]{1,0:T(1,128)} %bitcast.41, f32[1,128]{1,0:T(1,128)} %bitcast.48, f32[128,640]{1,0:T(8,128)} %refs_1_.4, f32[640]{0:T(1024)} %refs_5_.2, f32[520,128]{1,0:T(8,128)} %copy-done, ...), custom_call_target="tpu_custom_call" | custom-call | tf_op jit(solution)/shard_map/pallas_call | solution.py:365
  56.3 5.2 %all-to-all-done.2 = f32[128,4,128]{2,1,0:T(4,128)S(1)} async-done(((f32[128,4,128]{2,1,0:T(4,128)}), f32[128,4,128]{2,1,0:T(4,128)S(1)}, u32[]{:S(2)}, u32[]{:S(2)}) %all-to-all-start.2) | async-done | bytes 262176 | tf_op jit(solution)/shard_map/all_to_all | solution.py:382
  61.4 1.3 %shard_map.144 = f32[1024,128]{1,0:T(8,128)} custom-call(f32[512,128]{1,0:T(8,128)S(1)} %bitcast.28, f32[1024,128]{1,0:T(8,128)S(1)} %bitcast.23), custom_call_target="tpu_custom_call" | custom-call | tf_op jit(solution)/shard_map/pallas_call | solution.py:365
  62.7 4.0 %all-to-all-start.3 = ((f32[32,32,128]{2,1,0:T(8,128)}), f32[32,32,128]{2,1,0:T(8,128)S(1)}, u32[]{:S(2)}, u32[]{:S(2)}) async-start(f32[32,32,128]{2,1,0:T(8,128)} %bitcast.14), calls=%async_computation.3 | async-start | bytes 1048576 | tf_op jit(solution)/shard_map/all_to_all | solution.py:382
  67.1 2.1 %collective-permute-start.4 = (f32[64,128]{1,0:T(8,128)S(1)}, f32[64,128]{1,0:T(8,128)S(1)}, u32[]{:S(2)}, u32[]{:S(2)}) collective-permute-start(f32[64,128]{1,0:T(8,128)S(1)} %get-tuple-element.76), channel_id=1, source_target_pairs={{0,8},{4,12},{8,0},{12,4},{1,9},{5,13},{9,1},{13,5},{2,10},{6,14},... | collective-permute-start | bytes 98312 | tf_op jit(solution)/shard_map/ppermute | solution.py:394
  69.2 1.1 %collective-permute-start.5 = (f32[64,128]{1,0:T(8,128)S(1)}, f32[64,128]{1,0:T(8,128)S(1)}, u32[]{:S(2)}, u32[]{:S(2)}) collective-permute-start(f32[64,128]{1,0:T(8,128)S(1)} %get-tuple-element.77), channel_id=1, source_target_pairs={{0,12},{4,0},{8,4},{12,8},{1,13},{5,1},{9,5},{13,9},{2,14},{6,2},{... | collective-permute-start | bytes 98312 | tf_op jit(solution)/shard_map/ppermute | solution.py:394
  70.3 1.9 %shard_map.145 = (bf16[2048,128]{1,0:T(8,128)(2,1)S(1)}, bf16[2048,128]{1,0:T(8,128)(2,1)S(1)}, f32[512,512]{1,0:T(8,128)S(1)}) custom-call(f32[1,128]{1,0:T(1,128)} %bitcast.42, f32[1,128]{1,0:T(1,128)} %bitcast.49, f32[128,640]{1,0:T(8,128)} %refs_1_.4, f32[640]{0:T(1024)} %refs_5_.2, ...), custom_call_target="tpu_custom_call", output_to_operand_aliasing={{0}: (5, {}), {1}: (6, {}), {2}: (7, {})} | custom-call | tf_op jit(solution)/shard_map/pallas_call | solution.py:365
  72.3 5.1 %all-to-all-done.3 = f32[32,32,128]{2,1,0:T(8,128)S(1)} async-done(((f32[32,32,128]{2,1,0:T(8,128)}), f32[32,32,128]{2,1,0:T(8,128)S(1)}, u32[]{:S(2)}, u32[]{:S(2)}) %all-to-all-start.3) | async-done | bytes 524320 | tf_op jit(solution)/shard_map/all_to_all | solution.py:382
  77.4 1.5 %shard_map.146 = f32[192,128]{1,0:T(8,128)} custom-call(f32[1024,128]{1,0:T(8,128)S(1)} %bitcast.24, f32[512,512]{1,0:T(8,128)S(1)} %get-tuple-element.71.factor_ref, bf16[2048,128]{1,0:T(8,128)(2,1)S(1)} %get-tuple-element.72.high_ref, bf16[2048,128]{1,0:T(8,128)(2,1)S(1)} %get-tuple-element.73.low_ref, f32[64,128]{1,0:T(8,128)S(1)} %get-tuple-element.74.refs_0_, ...), custom_call_target="tpu_custom_call" | custom-call | tf_op jit(solution)/shard_map/pallas_call | solution.py:365
  78.9 5.1 %all-to-all-start.4 = ((f32[96,2,128]{2,1,0:T(2,128)}), f32[96,2,128]{2,1,0:T(2,128)S(1)}, u32[]{:S(2)}, u32[]{:S(2)}) async-start(f32[96,2,128]{2,1,0:T(2,128)} %bitcast.16), calls=%async_computation.4 | async-start | bytes 196608 | tf_op jit(solution)/shard_map/all_to_all | solution.py:382
  84.6 2.1 %collective-permute-start.7 = (f32[256,128]{1,0:T(8,128)S(1)}, f32[256,128]{1,0:T(8,128)S(1)}, u32[]{:S(2)}, u32[]{:S(2)}) collective-permute-start(f32[256,128]{1,0:T(8,128)S(1)} %get-tuple-element.91), channel_id=1, source_target_pairs={{0,8},{4,12},{8,0},{12,4},{1,9},{5,13},{9,1},{13,5},{2,10},{6,14},... | collective-permute-start | bytes 393224 | tf_op jit(solution)/shard_map/ppermute | solution.py:394
  86.7 1.1 %collective-permute-start.8 = (f32[256,128]{1,0:T(8,128)S(1)}, f32[256,128]{1,0:T(8,128)S(1)}, u32[]{:S(2)}, u32[]{:S(2)}) collective-permute-start(f32[256,128]{1,0:T(8,128)S(1)} %get-tuple-element.92), channel_id=1, source_target_pairs={{0,12},{4,0},{8,4},{12,8},{1,13},{5,1},{9,5},{13,9},{2,14},{6,2},{... | collective-permute-start | bytes 393224 | tf_op jit(solution)/shard_map/ppermute | solution.py:394
  87.8 3.7 %all-to-all-done.4 = f32[96,2,128]{2,1,0:T(2,128)S(1)} async-done(((f32[96,2,128]{2,1,0:T(2,128)}), f32[96,2,128]{2,1,0:T(2,128)S(1)}, u32[]{:S(2)}, u32[]{:S(2)}) %all-to-all-start.4) | async-done | bytes 98336 | tf_op jit(solution)/shard_map/all_to_all | solution.py:382
  91.5 0.8 shard_map.150
  92.2 5.2 %all-to-all-start.5 = ((f32[384,2,128]{2,1,0:T(2,128)}), f32[384,2,128]{2,1,0:T(2,128)S(1)}, u32[]{:S(2)}, u32[]{:S(2)}) async-start(f32[384,2,128]{2,1,0:T(2,128)} %bitcast.20), calls=%async_computation.5 | async-start | bytes 786432 | tf_op jit(solution)/shard_map/all_to_all | solution.py:382
  97.4 2.0 %shard_map.147 = (f32[512,128]{1,0:T(8,128)S(1)}, f32[512,128]{1,0:T(8,128)S(1)}, f32[512,512]{1,0:T(8,128)S(1)}) custom-call(f32[512,128]{1,0:T(8,128)} %bitcast.34, s32[2,256]{1,0:T(2,128)} %refs_1_.3, f32[1,128]{1,0:T(1,128)} %bitcast.43, f32[1,128]{1,0:T(1,128)} %bitcast.50, f32[128,640]{1,0:T(8,128)} %refs_1_.4, f32[640]{0:T(1024)} %refs_5_.2), custom_call_target="tpu_custom_call" | custom-call | flops 10000000000 | bytes 10000000 | tf_op jit(solution)/shard_map/pallas_call | solution.py:365
  99.5 2.7 %shard_map.149 = f32[512,128]{1,0:T(8,128)} custom-call(f32[1,128]{1,0:T(1,128)} %bitcast.44, f32[128,640]{1,0:T(8,128)} %refs_1_.4, f32[512,128]{1,0:T(8,128)} %copy-done.1, f32[512,128]{1,0:T(8,128)S(1)} %get-tuple-element.85.refs_3_, f32[512,128]{1,0:T(8,128)S(1)} %get-tuple-element.86.refs_4_, f32[512,512]{1,0:T(8,128)S(1)} %get-tuple-element.87.refs_5_, ...), custom_call_target="tpu_custom_call" | custom-call | tf_op jit(solution)/shard_map/pallas_call | solution.py:365
  102.2 7.6 %all-to-all-done.5 = f32[384,2,128]{2,1,0:T(2,128)S(1)} async-done(((f32[384,2,128]{2,1,0:T(2,128)}), f32[384,2,128]{2,1,0:T(2,128)S(1)}, u32[]{:S(2)}, u32[]{:S(2)}) %all-to-all-start.5) | async-done | bytes 393248 | tf_op jit(solution)/shard_map/all_to_all | solution.py:382
  109.8 0.9 shard_map.151
  (17 shorter events, 1.0 us)
Async XLA Ops:
  2.5 31.5 %copy-start = (f32[520,128]{1,0:T(8,128)}, f32[520,128]{1,0:T(8,128)S(1)}, u32[]{:S(2)}) copy-start(f32[520,128]{1,0:T(8,128)S(1)} %get-tuple-element.58.refs_4_) | copy-start | bytes 798724
  27.5 8.0 %collective-permute-start = (f32[520,128]{1,0:T(8,128)S(1)}, f32[520,128]{1,0:T(8,128)}, u32[]{:S(2)}, u32[]{:S(2)}) collective-permute-start(f32[520,128]{1,0:T(8,128)S(1)} %get-tuple-element.58.refs_4_), channel_id=1, source_target_pairs={{4,0},{8,4},{12,8},{0,12},{5,1},{9,5},{13,9},{1,13},{6,2},{10,6},{... | collective-permute-start | bytes 798728 | tf_op jit(solution)/shard_map/ppermute | solution.py:390
  29.4 16.0 %all-to-all-start.1 = ((f32[128,4,128]{2,1,0:T(4,128)}), f32[128,4,128]{2,1,0:T(4,128)S(1)}, u32[]{:S(2)}, u32[]{:S(2)}) async-start(f32[128,4,128]{2,1,0:T(4,128)} %bitcast.9), calls=%async_computation.1 | async-start | bytes 524288 | tf_op jit(solution)/shard_map/all_to_all | solution.py:382
  34.1 19.9 %collective-permute-start.1 = (f32[520,128]{1,0:T(8,128)S(1)}, f32[520,128]{1,0:T(8,128)}, u32[]{:S(2)}, u32[]{:S(2)}) collective-permute-start(f32[520,128]{1,0:T(8,128)S(1)} %get-tuple-element.58.refs_4_), channel_id=1, source_target_pairs={{12,0},{0,4},{4,8},{8,12},{13,1},{1,5},{5,9},{9,13},{14,2},{2,6},{... | collective-permute-start | bytes 798728 | tf_op jit(solution)/shard_map/ppermute | solution.py:390
  35.5 25.9 %collective-permute-start.2 = (f32[520,128]{1,0:T(8,128)}, f32[520,128]{1,0:T(8,128)S(1)}, u32[]{:S(2)}, u32[]{:S(2)}) collective-permute-start(f32[520,128]{1,0:T(8,128)} %collective-permute-done.refs_5_), channel_id=1, source_target_pairs={{4,0},{8,4},{12,8},{0,12},{5,1},{9,5},{13,9},{1,13},{6,2},{10,6},{... | collective-permute-start | bytes 798728 | tf_op jit(solution)/shard_map/ppermute | solution.py:390
  46.2 15.2 %all-to-all-start.2 = ((f32[128,4,128]{2,1,0:T(4,128)}), f32[128,4,128]{2,1,0:T(4,128)S(1)}, u32[]{:S(2)}, u32[]{:S(2)}) async-start(f32[128,4,128]{2,1,0:T(4,128)} %bitcast.12), calls=%async_computation.2 | async-start | bytes 524288 | tf_op jit(solution)/shard_map/all_to_all | solution.py:382
  53.2 0.7 copy-start.1
  61.4 1.3 %copy-start.2 = (f32[520,128]{1,0:T(8,128)}, f32[520,128]{1,0:T(8,128)S(1)}, u32[]{:S(2)}) copy-start(f32[520,128]{1,0:T(8,128)S(1)} %collective-permute-done.2.refs_4_) | copy-start | bytes 798724
  62.7 14.7 %all-to-all-start.3 = ((f32[32,32,128]{2,1,0:T(8,128)}), f32[32,32,128]{2,1,0:T(8,128)S(1)}, u32[]{:S(2)}, u32[]{:S(2)}) async-start(f32[32,32,128]{2,1,0:T(8,128)} %bitcast.14), calls=%async_computation.3 | async-start | bytes 1048576 | tf_op jit(solution)/shard_map/all_to_all | solution.py:382
  66.7 5.5 %collective-permute-start.3 = (f32[64,128]{1,0:T(8,128)S(1)}, f32[64,128]{1,0:T(8,128)S(1)}, u32[]{:S(2)}, u32[]{:S(2)}) collective-permute-start(f32[64,128]{1,0:T(8,128)S(1)} %get-tuple-element.75), channel_id=1, source_target_pairs={{0,4},{4,8},{8,12},{12,0},{1,5},{5,9},{9,13},{13,1},{2,6},{6,10},{... | collective-permute-start | bytes 98312 | tf_op jit(solution)/shard_map/ppermute | solution.py:394
  67.1 5.1 %collective-permute-start.4 = (f32[64,128]{1,0:T(8,128)S(1)}, f32[64,128]{1,0:T(8,128)S(1)}, u32[]{:S(2)}, u32[]{:S(2)}) collective-permute-start(f32[64,128]{1,0:T(8,128)S(1)} %get-tuple-element.76), channel_id=1, source_target_pairs={{0,8},{4,12},{8,0},{12,4},{1,9},{5,13},{9,1},{13,5},{2,10},{6,14},... | collective-permute-start | bytes 98312 | tf_op jit(solution)/shard_map/ppermute | solution.py:394
  69.2 3.1 %collective-permute-start.5 = (f32[64,128]{1,0:T(8,128)S(1)}, f32[64,128]{1,0:T(8,128)S(1)}, u32[]{:S(2)}, u32[]{:S(2)}) collective-permute-start(f32[64,128]{1,0:T(8,128)S(1)} %get-tuple-element.77), channel_id=1, source_target_pairs={{0,12},{4,0},{8,4},{12,8},{1,13},{5,1},{9,5},{13,9},{2,14},{6,2},{... | collective-permute-start | bytes 98312 | tf_op jit(solution)/shard_map/ppermute | solution.py:394
  78.9 12.6 %all-to-all-start.4 = ((f32[96,2,128]{2,1,0:T(2,128)}), f32[96,2,128]{2,1,0:T(2,128)S(1)}, u32[]{:S(2)}, u32[]{:S(2)}) async-start(f32[96,2,128]{2,1,0:T(2,128)} %bitcast.16), calls=%async_computation.4 | async-start | bytes 196608 | tf_op jit(solution)/shard_map/all_to_all | solution.py:382
  84.2 15.3 %collective-permute-start.6 = (f32[256,128]{1,0:T(8,128)S(1)}, f32[256,128]{1,0:T(8,128)S(1)}, u32[]{:S(2)}, u32[]{:S(2)}) collective-permute-start(f32[256,128]{1,0:T(8,128)S(1)} %get-tuple-element.90), channel_id=1, source_target_pairs={{0,4},{4,8},{8,12},{12,0},{1,5},{5,9},{9,13},{13,1},{2,6},{6,10},{... | collective-permute-start | bytes 393224 | tf_op jit(solution)/shard_map/ppermute | solution.py:394
  84.6 14.9 %collective-permute-start.7 = (f32[256,128]{1,0:T(8,128)S(1)}, f32[256,128]{1,0:T(8,128)S(1)}, u32[]{:S(2)}, u32[]{:S(2)}) collective-permute-start(f32[256,128]{1,0:T(8,128)S(1)} %get-tuple-element.91), channel_id=1, source_target_pairs={{0,8},{4,12},{8,0},{12,4},{1,9},{5,13},{9,1},{13,5},{2,10},{6,14},... | collective-permute-start | bytes 393224 | tf_op jit(solution)/shard_map/ppermute | solution.py:394
  86.7 12.8 %collective-permute-start.8 = (f32[256,128]{1,0:T(8,128)S(1)}, f32[256,128]{1,0:T(8,128)S(1)}, u32[]{:S(2)}, u32[]{:S(2)}) collective-permute-start(f32[256,128]{1,0:T(8,128)S(1)} %get-tuple-element.92), channel_id=1, source_target_pairs={{0,12},{4,0},{8,4},{12,8},{1,13},{5,1},{9,5},{13,9},{2,14},{6,2},{... | collective-permute-start | bytes 393224 | tf_op jit(solution)/shard_map/ppermute | solution.py:394
  92.2 17.6 %all-to-all-start.5 = ((f32[384,2,128]{2,1,0:T(2,128)}), f32[384,2,128]{2,1,0:T(2,128)S(1)}, u32[]{:S(2)}, u32[]{:S(2)}) async-start(f32[384,2,128]{2,1,0:T(2,128)} %bitcast.20), calls=%async_computation.5 | async-start | bytes 786432 | tf_op jit(solution)/shard_map/all_to_all | solution.py:382

commit v6 on v5

--- a/solution.py
+++ b/solution.py
@@ -419,6 +419,7 @@
     sent, pack = call(
         first_kernel, [(8 * LANES, LANES), (cells + 8, LANES)], *inputs, far=len(inputs)
     )
+    next_pack, last_pack = fetch(pack, 1), fetch(pack, 3)
     sides = exchange(sent)
     sides, x_late, pack = lax.optimization_barrier((sides, x, pack))
     back, cg = call(
@@ -433,7 +434,7 @@
         far=8,
     )
     product = exchange(call(product_kernel, (4 * LANES, LANES), sides))
-    packs = [pack, fetch(pack, 1), fetch(pack, 3)]
+    packs = [pack, next_pack, last_pack]
     across = fetch(packs[1], 1)
     d_product = exchange(call(middle_kernel, (4 * LANES, LANES), product, back))
     update, d_norm, *extras = call(

time: 111 us -> 111 us (level)
  blocking collectives: 25 us -> 0 us
  starting transfers between devices: 33.9 us -> 46.6 us
  waiting for transfers between devices: 27.7 us -> 38.5 us
    all_to_all x1 -> x0, blocking collectives: 25 us -> none  [exchange(): return lax.all_to_all(x, axes, split_axis=0, concat_axis=0, tiled=True)]
    all_to_all x5 -> x6, waiting for transfers between devices: 27.6 us -> 38.4 us  [exchange(): return lax.all_to_all(x, axes, split_axis=0, concat_axis=0, tiled=True)]
    all_to_all x5 -> x6, starting transfers between devices: 22.9 us -> 33.6 us  [exchange(): return lax.all_to_all(x, axes, split_axis=0, concat_axis=0, tiled=True)]
    ppermute x3, starting transfers between devices: 3.7 us -> 5.53 us  [fetch(): lax.ppermute(x, LINE, [((n + turn) % MEMBERS, n) for n in range(MEMBERS)])]
  transfers between devices with their start and end apart: 14 -> 15, of which waited for: 6 -> 7; matrix products, arithmetic and copies ran while one was open for 0% -> 0% of each run, Pallas kernels for 15% -> 16%
where the time goes in v6:
time: 111 us; the launch traced here: 110 us
  starting transfers between devices  46.6 us (42%)
  waiting for transfers between devices  38.5 us (35%)
  Pallas kernels  23.5 us (21%)
    all_to_all x6, waiting for transfers between devices, exchange(): return lax.all_to_all(x, axes, split_axis=0, concat_axis=0, tiled=True)  38.4 us
    all_to_all x6, starting transfers between devices, exchange(): return lax.all_to_all(x, axes, split_axis=0, concat_axis=0, tiled=True)  33.6 us
    pallas_call x14, Pallas kernels, call(): pl.pallas_call(body if far else kernel, out_shape=shapes if many else sha...  23.5 us
    ppermute x6, starting transfers between devices, hand(): lax.ppermute(x, LINE, [(n, (n + turn) % MEMBERS) for n in range(MEMBERS)])  7.43 us
    ppermute x3, starting transfers between devices, fetch(): lax.ppermute(x, LINE, [((n + turn) % MEMBERS, n) for n in range(MEMBERS)])  5.53 us
  transfers between devices with their start and end apart: 15, of which 7 were waited for; matrix products, arithmetic and copies ran while one was open for 0% of the time, Pallas kernels for 16%

profile of v6, /device:TPU:1, one launch (start us, length us, event | category | flops | bytes accessed | tf_op | source)
XLA Modules:
  0.0 110.1 jit_solution(2408976718334228763)
XLA Ops:
  0.6 2.7 %shard_map.138 = (f32[1024,128]{1,0:T(8,128)}, f32[520,128]{1,0:T(8,128)S(1)}) custom-call(f32[512,128]{1,0:T(8,128)} %bitcast.30, s32[2,256]{1,0:T(2,128)} %refs_1_.3, f32[1,128]{1,0:T(1,128)} %bitcast.37, f32[1,128]{1,0:T(1,128)} %bitcast.44, f32[128,640]{1,0:T(8,128)} %refs_1_.4, f32[640]{0:T(1024)} %refs_5_.2), custom_call_target="tpu_custom_call" | custom-call | tf_op jit(solution)/shard_map/pallas_call | solution.py:365
  3.3 11.5 %all-to-all-start = ((f32[128,8,128]{2,1,0:T(8,128)}), f32[128,8,128]{2,1,0:T(8,128)S(1)}, u32[]{:S(2)}, u32[]{:S(2)}) async-start(f32[128,8,128]{2,1,0:T(8,128)} %bitcast.7), calls=%async_computation | async-start | bytes 1048576 | tf_op jit(solution)/shard_map/all_to_all | solution.py:382
  14.9 2.7 %collective-permute-start = (f32[520,128]{1,0:T(8,128)S(1)}, f32[520,128]{1,0:T(8,128)}, u32[]{:S(2)}, u32[]{:S(2)}) collective-permute-start(f32[520,128]{1,0:T(8,128)S(1)} %get-tuple-element.58.refs_4_), channel_id=1, source_target_pairs={{4,0},{8,4},{12,8},{0,12},{5,1},{9,5},{13,9},{1,13},{6,2},{10,6},{... | collective-permute-start | bytes 798728 | tf_op jit(solution)/shard_map/ppermute | solution.py:390
  17.6 11.0 %all-to-all-done = f32[128,8,128]{2,1,0:T(8,128)S(1)} async-done(((f32[128,8,128]{2,1,0:T(8,128)}), f32[128,8,128]{2,1,0:T(8,128)S(1)}, u32[]{:S(2)}, u32[]{:S(2)}) %all-to-all-start) | async-done | bytes 524320 | tf_op jit(solution)/shard_map/all_to_all | solution.py:382
  28.6 1.0 shard_map.139
  29.6 3.9 %all-to-all-start.1 = ((f32[128,4,128]{2,1,0:T(4,128)}), f32[128,4,128]{2,1,0:T(4,128)S(1)}, u32[]{:S(2)}, u32[]{:S(2)}) async-start(f32[128,4,128]{2,1,0:T(4,128)} %bitcast.9), calls=%async_computation.1 | async-start | bytes 524288 | tf_op jit(solution)/shard_map/all_to_all | solution.py:382
  33.5 1.5 %collective-permute-start.1 = (f32[520,128]{1,0:T(8,128)S(1)}, f32[520,128]{1,0:T(8,128)}, u32[]{:S(2)}, u32[]{:S(2)}) collective-permute-start(f32[520,128]{1,0:T(8,128)S(1)} %get-tuple-element.58.refs_4_), channel_id=1, source_target_pairs={{12,0},{0,4},{4,8},{8,12},{13,1},{1,5},{5,9},{9,13},{14,2},{2,6},{... | collective-permute-start | bytes 798728 | tf_op jit(solution)/shard_map/ppermute | solution.py:390
  35.0 1.4 %collective-permute-start.2 = (f32[520,128]{1,0:T(8,128)}, f32[520,128]{1,0:T(8,128)}, u32[]{:S(2)}, u32[]{:S(2)}) collective-permute-start(f32[520,128]{1,0:T(8,128)} %collective-permute-done.refs_5_), channel_id=1, source_target_pairs={{4,0},{8,4},{12,8},{0,12},{5,1},{9,5},{13,9},{1,13},{6,2},{10,6},{... | collective-permute-start | bytes 798728 | tf_op jit(solution)/shard_map/ppermute | solution.py:390
  36.3 2.3 %shard_map.140 = (f32[128,512]{1,0:T(8,128)S(1)}, f32[512,128]{1,0:T(8,128)S(1)}) custom-call(f32[512,128]{1,0:T(8,128)} %bitcast.31, f32[1,128]{1,0:T(1,128)} %bitcast.38, f32[1,128]{1,0:T(1,128)} %bitcast.45, f32[128,640]{1,0:T(8,128)} %refs_1_.4, f32[640]{0:T(1024)} %refs_5_.2, f32[512,128]{1,0:T(8,128)} %bitcast.34, f32[128,128]{1,0:T(8,128)} %refs_6_.3, ...), custom_call_target="tpu_custom_call" | custom-call | tf_op jit(solution)/shard_map/pallas_call | solution.py:365
  38.6 6.1 %all-to-all-done.1 = f32[128,4,128]{2,1,0:T(4,128)S(1)} async-done(((f32[128,4,128]{2,1,0:T(4,128)}), f32[128,4,128]{2,1,0:T(4,128)S(1)}, u32[]{:S(2)}, u32[]{:S(2)}) %all-to-all-start.1) | async-done | bytes 262176 | tf_op jit(solution)/shard_map/all_to_all | solution.py:382
  44.8 0.9 shard_map.142
  45.7 3.9 %all-to-all-start.2 = ((f32[128,4,128]{2,1,0:T(4,128)}), f32[128,4,128]{2,1,0:T(4,128)S(1)}, u32[]{:S(2)}, u32[]{:S(2)}) async-start(f32[128,4,128]{2,1,0:T(4,128)} %bitcast.12), calls=%async_computation.2 | async-start | bytes 524288 | tf_op jit(solution)/shard_map/all_to_all | solution.py:382
  49.6 2.4 %shard_map.143 = (bf16[2048,128]{1,0:T(8,128)(2,1)S(1)}, bf16[2048,128]{1,0:T(8,128)(2,1)S(1)}, f32[512,512]{1,0:T(8,128)S(1)}) custom-call(f32[1,128]{1,0:T(1,128)} %bitcast.39, f32[1,128]{1,0:T(1,128)} %bitcast.46, f32[128,640]{1,0:T(8,128)} %refs_1_.4, f32[640]{0:T(1024)} %refs_5_.2, f32[520,128]{1,0:T(8,128)} %copy-done, ...), custom_call_target="tpu_custom_call" | custom-call | tf_op jit(solution)/shard_map/pallas_call | solution.py:365
  52.0 3.1 %shard_map.141 = (f32[512,128]{1,0:T(8,128)}, f32[512,128]{1,0:T(8,128)S(1)}, f32[64,128]{1,0:T(8,128)S(1)}, f32[64,128]{1,0:T(8,128)S(1)}, f32[64,128]{1,0:T(8,128)S(1)}, /*index=5*/f32[64,128]{1,0:T(8,128)S(1)}) custom-call(f32[512,128]{1,0:T(8,128)} %bitcast.32, f32[1,128]{1,0:T(1,128)} %bitcast.40, f32[1,128]{1,0:T(1,128)} %bitcast.47, ...), custom_call_target="tpu_custom_call" | custom-call | tf_op jit(solution)/shard_map/pallas_call | solution.py:365
  55.8 5.1 %all-to-all-done.2 = f32[128,4,128]{2,1,0:T(4,128)S(1)} async-done(((f32[128,4,128]{2,1,0:T(4,128)}), f32[128,4,128]{2,1,0:T(4,128)S(1)}, u32[]{:S(2)}, u32[]{:S(2)}) %all-to-all-start.2) | async-done | bytes 262176 | tf_op jit(solution)/shard_map/all_to_all | solution.py:382
  60.9 1.3 %shard_map.144 = f32[1024,128]{1,0:T(8,128)} custom-call(f32[512,128]{1,0:T(8,128)S(1)} %bitcast.28, f32[1024,128]{1,0:T(8,128)S(1)} %bitcast.23), custom_call_target="tpu_custom_call" | custom-call | tf_op jit(solution)/shard_map/pallas_call | solution.py:365
  62.2 4.0 %all-to-all-start.3 = ((f32[32,32,128]{2,1,0:T(8,128)}), f32[32,32,128]{2,1,0:T(8,128)S(1)}, u32[]{:S(2)}, u32[]{:S(2)}) async-start(f32[32,32,128]{2,1,0:T(8,128)} %bitcast.14), calls=%async_computation.3 | async-start | bytes 1048576 | tf_op jit(solution)/shard_map/all_to_all | solution.py:382
  66.6 2.2 %collective-permute-start.4 = (f32[64,128]{1,0:T(8,128)S(1)}, f32[64,128]{1,0:T(8,128)S(1)}, u32[]{:S(2)}, u32[]{:S(2)}) collective-permute-start(f32[64,128]{1,0:T(8,128)S(1)} %get-tuple-element.76), channel_id=1, source_target_pairs={{0,8},{4,12},{8,0},{12,4},{1,9},{5,13},{9,1},{13,5},{2,10},{6,14},... | collective-permute-start | bytes 98312 | tf_op jit(solution)/shard_map/ppermute | solution.py:394
  68.7 1.1 %collective-permute-start.5 = (f32[64,128]{1,0:T(8,128)S(1)}, f32[64,128]{1,0:T(8,128)S(1)}, u32[]{:S(2)}, u32[]{:S(2)}) collective-permute-start(f32[64,128]{1,0:T(8,128)S(1)} %get-tuple-element.77), channel_id=1, source_target_pairs={{0,12},{4,0},{8,4},{12,8},{1,13},{5,1},{9,5},{13,9},{2,14},{6,2},{... | collective-permute-start | bytes 98312 | tf_op jit(solution)/shard_map/ppermute | solution.py:394
  69.9 1.9 %shard_map.145 = (bf16[2048,128]{1,0:T(8,128)(2,1)S(1)}, bf16[2048,128]{1,0:T(8,128)(2,1)S(1)}, f32[512,512]{1,0:T(8,128)S(1)}) custom-call(f32[1,128]{1,0:T(1,128)} %bitcast.41, f32[1,128]{1,0:T(1,128)} %bitcast.48, f32[128,640]{1,0:T(8,128)} %refs_1_.4, f32[640]{0:T(1024)} %refs_5_.2, ...), custom_call_target="tpu_custom_call", output_to_operand_aliasing={{0}: (5, {}), {1}: (6, {}), {2}: (7, {})} | custom-call | tf_op jit(solution)/shard_map/pallas_call | solution.py:365
  71.9 5.0 %all-to-all-done.3 = f32[32,32,128]{2,1,0:T(8,128)S(1)} async-done(((f32[32,32,128]{2,1,0:T(8,128)}), f32[32,32,128]{2,1,0:T(8,128)S(1)}, u32[]{:S(2)}, u32[]{:S(2)}) %all-to-all-start.3) | async-done | bytes 524320 | tf_op jit(solution)/shard_map/all_to_all | solution.py:382
  76.9 1.5 %shard_map.146 = f32[192,128]{1,0:T(8,128)} custom-call(f32[1024,128]{1,0:T(8,128)S(1)} %bitcast.24, f32[512,512]{1,0:T(8,128)S(1)} %get-tuple-element.71.factor_ref, bf16[2048,128]{1,0:T(8,128)(2,1)S(1)} %get-tuple-element.72.high_ref, bf16[2048,128]{1,0:T(8,128)(2,1)S(1)} %get-tuple-element.73.low_ref, f32[64,128]{1,0:T(8,128)S(1)} %get-tuple-element.74.refs_0_, ...), custom_call_target="tpu_custom_call" | custom-call | tf_op jit(solution)/shard_map/pallas_call | solution.py:365
  78.4 5.1 %all-to-all-start.4 = ((f32[96,2,128]{2,1,0:T(2,128)}), f32[96,2,128]{2,1,0:T(2,128)S(1)}, u32[]{:S(2)}, u32[]{:S(2)}) async-start(f32[96,2,128]{2,1,0:T(2,128)} %bitcast.16), calls=%async_computation.4 | async-start | bytes 196608 | tf_op jit(solution)/shard_map/all_to_all | solution.py:382
  84.0 2.2 %collective-permute-start.7 = (f32[256,128]{1,0:T(8,128)S(1)}, f32[256,128]{1,0:T(8,128)S(1)}, u32[]{:S(2)}, u32[]{:S(2)}) collective-permute-start(f32[256,128]{1,0:T(8,128)S(1)} %get-tuple-element.91), channel_id=1, source_target_pairs={{0,8},{4,12},{8,0},{12,4},{1,9},{5,13},{9,1},{13,5},{2,10},{6,14},... | collective-permute-start | bytes 393224 | tf_op jit(solution)/shard_map/ppermute | solution.py:394
  86.2 1.1 %collective-permute-start.8 = (f32[256,128]{1,0:T(8,128)S(1)}, f32[256,128]{1,0:T(8,128)S(1)}, u32[]{:S(2)}, u32[]{:S(2)}) collective-permute-start(f32[256,128]{1,0:T(8,128)S(1)} %get-tuple-element.92), channel_id=1, source_target_pairs={{0,12},{4,0},{8,4},{12,8},{1,13},{5,1},{9,5},{13,9},{2,14},{6,2},{... | collective-permute-start | bytes 393224 | tf_op jit(solution)/shard_map/ppermute | solution.py:394
  87.3 3.6 %all-to-all-done.4 = f32[96,2,128]{2,1,0:T(2,128)S(1)} async-done(((f32[96,2,128]{2,1,0:T(2,128)}), f32[96,2,128]{2,1,0:T(2,128)S(1)}, u32[]{:S(2)}, u32[]{:S(2)}) %all-to-all-start.4) | async-done | bytes 98336 | tf_op jit(solution)/shard_map/all_to_all | solution.py:382
  90.9 0.8 shard_map.150
  91.7 5.2 %all-to-all-start.5 = ((f32[384,2,128]{2,1,0:T(2,128)}), f32[384,2,128]{2,1,0:T(2,128)S(1)}, u32[]{:S(2)}, u32[]{:S(2)}) async-start(f32[384,2,128]{2,1,0:T(2,128)} %bitcast.20), calls=%async_computation.5 | async-start | bytes 786432 | tf_op jit(solution)/shard_map/all_to_all | solution.py:382
  96.9 2.0 %shard_map.147 = (f32[512,128]{1,0:T(8,128)S(1)}, f32[512,128]{1,0:T(8,128)S(1)}, f32[512,512]{1,0:T(8,128)S(1)}) custom-call(f32[512,128]{1,0:T(8,128)} %bitcast.33, s32[2,256]{1,0:T(2,128)} %refs_1_.3, f32[1,128]{1,0:T(1,128)} %bitcast.42, f32[1,128]{1,0:T(1,128)} %bitcast.49, f32[128,640]{1,0:T(8,128)} %refs_1_.4, f32[640]{0:T(1024)} %refs_5_.2), custom_call_target="tpu_custom_call" | custom-call | flops 10000000000 | bytes 10000000 | tf_op jit(solution)/shard_map/pallas_call | solution.py:365
  99.0 2.7 %shard_map.149 = f32[512,128]{1,0:T(8,128)} custom-call(f32[1,128]{1,0:T(1,128)} %bitcast.43, f32[128,640]{1,0:T(8,128)} %refs_1_.4, f32[512,128]{1,0:T(8,128)} %copy-done.1, f32[512,128]{1,0:T(8,128)S(1)} %get-tuple-element.85.refs_3_, f32[512,128]{1,0:T(8,128)S(1)} %get-tuple-element.86.refs_4_, f32[512,512]{1,0:T(8,128)S(1)} %get-tuple-element.87.refs_5_, ...), custom_call_target="tpu_custom_call" | custom-call | tf_op jit(solution)/shard_map/pallas_call | solution.py:365
  101.6 7.6 %all-to-all-done.5 = f32[384,2,128]{2,1,0:T(2,128)S(1)} async-done(((f32[384,2,128]{2,1,0:T(2,128)}), f32[384,2,128]{2,1,0:T(2,128)S(1)}, u32[]{:S(2)}, u32[]{:S(2)}) %all-to-all-start.5) | async-done | bytes 393248 | tf_op jit(solution)/shard_map/all_to_all | solution.py:382
  109.3 0.9 shard_map.151
  (20 shorter events, 1.8 us)
Async XLA Ops:
  3.3 30.2 %copy-start = (f32[520,128]{1,0:T(8,128)}, f32[520,128]{1,0:T(8,128)S(1)}, u32[]{:S(2)}) copy-start(f32[520,128]{1,0:T(8,128)S(1)} %get-tuple-element.58.refs_4_) | copy-start | bytes 798724
  3.3 25.2 %all-to-all-start = ((f32[128,8,128]{2,1,0:T(8,128)}), f32[128,8,128]{2,1,0:T(8,128)S(1)}, u32[]{:S(2)}, u32[]{:S(2)}) async-start(f32[128,8,128]{2,1,0:T(8,128)} %bitcast.7), calls=%async_computation | async-start | bytes 1048576 | tf_op jit(solution)/shard_map/all_to_all | solution.py:382
  14.9 20.1 %collective-permute-start = (f32[520,128]{1,0:T(8,128)S(1)}, f32[520,128]{1,0:T(8,128)}, u32[]{:S(2)}, u32[]{:S(2)}) collective-permute-start(f32[520,128]{1,0:T(8,128)S(1)} %get-tuple-element.58.refs_4_), channel_id=1, source_target_pairs={{4,0},{8,4},{12,8},{0,12},{5,1},{9,5},{13,9},{1,13},{6,2},{10,6},{... | collective-permute-start | bytes 798728 | tf_op jit(solution)/shard_map/ppermute | solution.py:390
  29.6 15.2 %all-to-all-start.1 = ((f32[128,4,128]{2,1,0:T(4,128)}), f32[128,4,128]{2,1,0:T(4,128)S(1)}, u32[]{:S(2)}, u32[]{:S(2)}) async-start(f32[128,4,128]{2,1,0:T(4,128)} %bitcast.9), calls=%async_computation.1 | async-start | bytes 524288 | tf_op jit(solution)/shard_map/all_to_all | solution.py:382
  33.5 16.1 %collective-permute-start.1 = (f32[520,128]{1,0:T(8,128)S(1)}, f32[520,128]{1,0:T(8,128)}, u32[]{:S(2)}, u32[]{:S(2)}) collective-permute-start(f32[520,128]{1,0:T(8,128)S(1)} %get-tuple-element.58.refs_4_), channel_id=1, source_target_pairs={{12,0},{0,4},{4,8},{8,12},{13,1},{1,5},{5,9},{9,13},{14,2},{2,6},{... | collective-permute-start | bytes 798728 | tf_op jit(solution)/shard_map/ppermute | solution.py:390
  35.0 20.8 %collective-permute-start.2 = (f32[520,128]{1,0:T(8,128)}, f32[520,128]{1,0:T(8,128)}, u32[]{:S(2)}, u32[]{:S(2)}) collective-permute-start(f32[520,128]{1,0:T(8,128)} %collective-permute-done.refs_5_), channel_id=1, source_target_pairs={{4,0},{8,4},{12,8},{0,12},{5,1},{9,5},{13,9},{1,13},{6,2},{10,6},{... | collective-permute-start | bytes 798728 | tf_op jit(solution)/shard_map/ppermute | solution.py:390
  38.6 7.0 %copy-start.2 = (f32[512,128]{1,0:T(8,128)}, f32[512,128]{1,0:T(8,128)S(1)}, u32[]{:S(2)}) copy-start(f32[512,128]{1,0:T(8,128)S(1)} %get-tuple-element.54.refs_11_) | copy-start | bytes 786436
  45.7 15.2 %all-to-all-start.2 = ((f32[128,4,128]{2,1,0:T(4,128)}), f32[128,4,128]{2,1,0:T(4,128)S(1)}, u32[]{:S(2)}, u32[]{:S(2)}) async-start(f32[128,4,128]{2,1,0:T(4,128)} %bitcast.12), calls=%async_computation.2 | async-start | bytes 524288 | tf_op jit(solution)/shard_map/all_to_all | solution.py:382
  49.6 2.4 %copy-start.3 = (f32[512,128]{1,0:T(8,128)S(1)}, f32[512,128]{1,0:T(8,128)}, u32[]{:S(2)}) copy-start(f32[512,128]{1,0:T(8,128)} %copy-done.2) | copy-start | bytes 786436
  55.1 0.7 copy-start.1
  62.2 14.7 %all-to-all-start.3 = ((f32[32,32,128]{2,1,0:T(8,128)}), f32[32,32,128]{2,1,0:T(8,128)S(1)}, u32[]{:S(2)}, u32[]{:S(2)}) async-start(f32[32,32,128]{2,1,0:T(8,128)} %bitcast.14), calls=%async_computation.3 | async-start | bytes 1048576 | tf_op jit(solution)/shard_map/all_to_all | solution.py:382
  66.1 5.6 %collective-permute-start.3 = (f32[64,128]{1,0:T(8,128)S(1)}, f32[64,128]{1,0:T(8,128)S(1)}, u32[]{:S(2)}, u32[]{:S(2)}) collective-permute-start(f32[64,128]{1,0:T(8,128)S(1)} %get-tuple-element.75), channel_id=1, source_target_pairs={{0,4},{4,8},{8,12},{12,0},{1,5},{5,9},{9,13},{13,1},{2,6},{6,10},{... | collective-permute-start | bytes 98312 | tf_op jit(solution)/shard_map/ppermute | solution.py:394
  66.6 5.2 %collective-permute-start.4 = (f32[64,128]{1,0:T(8,128)S(1)}, f32[64,128]{1,0:T(8,128)S(1)}, u32[]{:S(2)}, u32[]{:S(2)}) collective-permute-start(f32[64,128]{1,0:T(8,128)S(1)} %get-tuple-element.76), channel_id=1, source_target_pairs={{0,8},{4,12},{8,0},{12,4},{1,9},{5,13},{9,1},{13,5},{2,10},{6,14},... | collective-permute-start | bytes 98312 | tf_op jit(solution)/shard_map/ppermute | solution.py:394
  68.7 3.1 %collective-permute-start.5 = (f32[64,128]{1,0:T(8,128)S(1)}, f32[64,128]{1,0:T(8,128)S(1)}, u32[]{:S(2)}, u32[]{:S(2)}) collective-permute-start(f32[64,128]{1,0:T(8,128)S(1)} %get-tuple-element.77), channel_id=1, source_target_pairs={{0,12},{4,0},{8,4},{12,8},{1,13},{5,1},{9,5},{13,9},{2,14},{6,2},{... | collective-permute-start | bytes 98312 | tf_op jit(solution)/shard_map/ppermute | solution.py:394
  78.4 12.6 %all-to-all-start.4 = ((f32[96,2,128]{2,1,0:T(2,128)}), f32[96,2,128]{2,1,0:T(2,128)S(1)}, u32[]{:S(2)}, u32[]{:S(2)}) async-start(f32[96,2,128]{2,1,0:T(2,128)} %bitcast.16), calls=%async_computation.4 | async-start | bytes 196608 | tf_op jit(solution)/shard_map/all_to_all | solution.py:382
  83.6 15.3 %collective-permute-start.6 = (f32[256,128]{1,0:T(8,128)S(1)}, f32[256,128]{1,0:T(8,128)S(1)}, u32[]{:S(2)}, u32[]{:S(2)}) collective-permute-start(f32[256,128]{1,0:T(8,128)S(1)} %get-tuple-element.90), channel_id=1, source_target_pairs={{0,4},{4,8},{8,12},{12,0},{1,5},{5,9},{9,13},{13,1},{2,6},{6,10},{... | collective-permute-start | bytes 393224 | tf_op jit(solution)/shard_map/ppermute | solution.py:394
  84.0 14.9 %collective-permute-start.7 = (f32[256,128]{1,0:T(8,128)S(1)}, f32[256,128]{1,0:T(8,128)S(1)}, u32[]{:S(2)}, u32[]{:S(2)}) collective-permute-start(f32[256,128]{1,0:T(8,128)S(1)} %get-tuple-element.91), channel_id=1, source_target_pairs={{0,8},{4,12},{8,0},{12,4},{1,9},{5,13},{9,1},{13,5},{2,10},{6,14},... | collective-permute-start | bytes 393224 | tf_op jit(solution)/shard_map/ppermute | solution.py:394
  86.2 12.7 %collective-permute-start.8 = (f32[256,128]{1,0:T(8,128)S(1)}, f32[256,128]{1,0:T(8,128)S(1)}, u32[]{:S(2)}, u32[]{:S(2)}) collective-permute-start(f32[256,128]{1,0:T(8,128)S(1)} %get-tuple-element.92), channel_id=1, source_target_pairs={{0,12},{4,0},{8,4},{12,8},{1,13},{5,1},{9,5},{13,9},{2,14},{6,2},{... | collective-permute-start | bytes 393224 | tf_op jit(solution)/shard_map/ppermute | solution.py:394
  91.7 17.6 %all-to-all-start.5 = ((f32[384,2,128]{2,1,0:T(2,128)}), f32[384,2,128]{2,1,0:T(2,128)S(1)}, u32[]{:S(2)}, u32[]{:S(2)}) async-start(f32[384,2,128]{2,1,0:T(2,128)} %bitcast.20), calls=%async_computation.5 | async-start | bytes 786432 | tf_op jit(solution)/shard_map/all_to_all | solution.py:382

commit v7 on v6

--- a/solution.py
+++ b/solution.py
@@ -333,11 +333,20 @@
     out_ref[...] = jnp.broadcast_to(mine[None], (LANES // 4, 24, LANES)).reshape(out_ref.shape)
 
 
-def last_kernel(in_ref, win_ref, wout_ref):
+def last_kernel(in_ref, win_ref, wout_ref, win_held, wout_held, sems):
+    copies = [
+        pltpu.make_async_copy(win_held.at[:, block(p)], win_ref.at[:, block(p)], sems.at[p])
+        for p in range(5)
+    ] + [pltpu.make_async_copy(wout_held, wout_ref, sems.at[5])]
+    wout_held[...] = in_ref[every(4, 6), :]
+    copies[5].start()
+    win_held[:, block(4)] = in_ref[every(5, 6), :]
+    copies[4].start()
     for part in range(4):
-        win_ref[:, block(part)] = jnp.transpose(in_ref[every(part, 6), :])
-    wout_ref[...] = in_ref[every(4, 6), :]
-    win_ref[:, block(4)] = in_ref[every(5, 6), :]
+        win_held[:, block(part)] = jnp.transpose(in_ref[every(part, 6), :])
+        copies[part].start()
+    for copy in copies:
+        copy.wait()
 
 
 def call(kernel, outs, *given, args=(), scratch=(), far=0, work=0, aliases={}):
@@ -500,7 +509,15 @@
     whole = exchange_pairs(
         call(functools.partial(sum_kernel, length), (6 * LANES, LANES), terms)
     )
-    d_win, d_wout = call(last_kernel, [w_in.shape, w_out.shape], whole)
+    d_win, d_wout = pl.pallas_call(
+        last_kernel,
+        out_shape=[jax.ShapeDtypeStruct(w.shape, F32) for w in (w_in, w_out)],
+        in_specs=[pl.BlockSpec(memory_space=pltpu.VMEM)],
+        out_specs=[pl.BlockSpec(memory_space=pltpu.HBM)] * 2,
+        scratch_shapes=[pltpu.VMEM(w.shape, F32) for w in (w_in, w_out)]
+        + [pltpu.SemaphoreType.DMA((6,))],
+        compiler_params=pltpu.CompilerParams(vmem_limit_bytes=24 * 2**20),
+    )(whole)
     return (update.reshape(pair_rep.shape), grad_pair.reshape(pair_rep.shape), d_win, d_wout)
 
 

time: 111 us -> 111 us (level)
    pallas_call x14 -> x13, Pallas kernels: 23.5 us -> 22.6 us  [call(): pl.pallas_call(body if far else kernel, out_shape=shapes if many else sha...]
where the time goes in v7:
time: 111 us; the launch traced here: 110 us
  starting transfers between devices  46.6 us (42%)
  waiting for transfers between devices  38.5 us (35%)
  Pallas kernels  23.4 us (21%)
    all_to_all x6, waiting for transfers between devices, exchange(): return lax.all_to_all(x, axes, split_axis=0, concat_axis=0, tiled=True)  38.4 us
    all_to_all x6, starting transfers between devices, exchange(): return lax.all_to_all(x, axes, split_axis=0, concat_axis=0, tiled=True)  33.6 us
    pallas_call x13, Pallas kernels, call(): pl.pallas_call(body if far else kernel, out_shape=shapes if many else sha...  22.6 us
    ppermute x6, starting transfers between devices, hand(): lax.ppermute(x, LINE, [(n, (n + turn) % MEMBERS) for n in range(MEMBERS)])  7.43 us
    ppermute x3, starting transfers between devices, fetch(): lax.ppermute(x, LINE, [((n + turn) % MEMBERS, n) for n in range(MEMBERS)])  5.53 us
  transfers between devices with their start and end apart: 15, of which 7 were waited for; matrix products, arithmetic and copies ran while one was open for 0% of the time, Pallas kernels for 16%

profile of v7, /device:TPU:1, one launch (start us, length us, event | category | flops | bytes accessed | tf_op | source)
XLA Modules:
  0.0 110.1 jit_solution(1330176585751968642)
XLA Ops:
  0.6 2.7 %shard_map.138 = (f32[1024,128]{1,0:T(8,128)}, f32[520,128]{1,0:T(8,128)S(1)}) custom-call(f32[512,128]{1,0:T(8,128)} %bitcast.30, s32[2,256]{1,0:T(2,128)} %refs_1_.3, f32[1,128]{1,0:T(1,128)} %bitcast.37, f32[1,128]{1,0:T(1,128)} %bitcast.44, f32[128,640]{1,0:T(8,128)} %refs_1_.4, f32[640]{0:T(1024)} %refs_5_.2), custom_call_target="tpu_custom_call" | custom-call | tf_op jit(solution)/shard_map/pallas_call | solution.py:374
  3.3 11.5 %all-to-all-start = ((f32[128,8,128]{2,1,0:T(8,128)}), f32[128,8,128]{2,1,0:T(8,128)S(1)}, u32[]{:S(2)}, u32[]{:S(2)}) async-start(f32[128,8,128]{2,1,0:T(8,128)} %bitcast.7), calls=%async_computation | async-start | bytes 1048576 | tf_op jit(solution)/shard_map/all_to_all | solution.py:391
  14.9 2.7 %collective-permute-start = (f32[520,128]{1,0:T(8,128)S(1)}, f32[520,128]{1,0:T(8,128)}, u32[]{:S(2)}, u32[]{:S(2)}) collective-permute-start(f32[520,128]{1,0:T(8,128)S(1)} %get-tuple-element.58.refs_4_), channel_id=1, source_target_pairs={{4,0},{8,4},{12,8},{0,12},{5,1},{9,5},{13,9},{1,13},{6,2},{10,6},{... | collective-permute-start | bytes 798728 | tf_op jit(solution)/shard_map/ppermute | solution.py:399
  17.6 11.0 %all-to-all-done = f32[128,8,128]{2,1,0:T(8,128)S(1)} async-done(((f32[128,8,128]{2,1,0:T(8,128)}), f32[128,8,128]{2,1,0:T(8,128)S(1)}, u32[]{:S(2)}, u32[]{:S(2)}) %all-to-all-start) | async-done | bytes 524320 | tf_op jit(solution)/shard_map/all_to_all | solution.py:391
  28.6 1.0 shard_map.139
  29.6 3.9 %all-to-all-start.1 = ((f32[128,4,128]{2,1,0:T(4,128)}), f32[128,4,128]{2,1,0:T(4,128)S(1)}, u32[]{:S(2)}, u32[]{:S(2)}) async-start(f32[128,4,128]{2,1,0:T(4,128)} %bitcast.9), calls=%async_computation.1 | async-start | bytes 524288 | tf_op jit(solution)/shard_map/all_to_all | solution.py:391
  33.5 1.5 %collective-permute-start.1 = (f32[520,128]{1,0:T(8,128)S(1)}, f32[520,128]{1,0:T(8,128)}, u32[]{:S(2)}, u32[]{:S(2)}) collective-permute-start(f32[520,128]{1,0:T(8,128)S(1)} %get-tuple-element.58.refs_4_), channel_id=1, source_target_pairs={{12,0},{0,4},{4,8},{8,12},{13,1},{1,5},{5,9},{9,13},{14,2},{2,6},{... | collective-permute-start | bytes 798728 | tf_op jit(solution)/shard_map/ppermute | solution.py:399
  35.0 1.4 %collective-permute-start.2 = (f32[520,128]{1,0:T(8,128)}, f32[520,128]{1,0:T(8,128)}, u32[]{:S(2)}, u32[]{:S(2)}) collective-permute-start(f32[520,128]{1,0:T(8,128)} %collective-permute-done.refs_5_), channel_id=1, source_target_pairs={{4,0},{8,4},{12,8},{0,12},{5,1},{9,5},{13,9},{1,13},{6,2},{10,6},{... | collective-permute-start | bytes 798728 | tf_op jit(solution)/shard_map/ppermute | solution.py:399
  36.3 2.3 %shard_map.140 = (f32[128,512]{1,0:T(8,128)S(1)}, f32[512,128]{1,0:T(8,128)S(1)}) custom-call(f32[512,128]{1,0:T(8,128)} %bitcast.31, f32[1,128]{1,0:T(1,128)} %bitcast.38, f32[1,128]{1,0:T(1,128)} %bitcast.45, f32[128,640]{1,0:T(8,128)} %refs_1_.4, f32[640]{0:T(1024)} %refs_5_.2, f32[512,128]{1,0:T(8,128)} %bitcast.34, f32[128,128]{1,0:T(8,128)} %refs_6_.3, ...), custom_call_target="tpu_custom_call" | custom-call | tf_op jit(solution)/shard_map/pallas_call | solution.py:374
  38.6 6.1 %all-to-all-done.1 = f32[128,4,128]{2,1,0:T(4,128)S(1)} async-done(((f32[128,4,128]{2,1,0:T(4,128)}), f32[128,4,128]{2,1,0:T(4,128)S(1)}, u32[]{:S(2)}, u32[]{:S(2)}) %all-to-all-start.1) | async-done | bytes 262176 | tf_op jit(solution)/shard_map/all_to_all | solution.py:391
  44.8 0.9 shard_map.142
  45.7 3.9 %all-to-all-start.2 = ((f32[128,4,128]{2,1,0:T(4,128)}), f32[128,4,128]{2,1,0:T(4,128)S(1)}, u32[]{:S(2)}, u32[]{:S(2)}) async-start(f32[128,4,128]{2,1,0:T(4,128)} %bitcast.12), calls=%async_computation.2 | async-start | bytes 524288 | tf_op jit(solution)/shard_map/all_to_all | solution.py:391
  49.6 2.4 %shard_map.143 = (bf16[2048,128]{1,0:T(8,128)(2,1)S(1)}, bf16[2048,128]{1,0:T(8,128)(2,1)S(1)}, f32[512,512]{1,0:T(8,128)S(1)}) custom-call(f32[1,128]{1,0:T(1,128)} %bitcast.39, f32[1,128]{1,0:T(1,128)} %bitcast.46, f32[128,640]{1,0:T(8,128)} %refs_1_.4, f32[640]{0:T(1024)} %refs_5_.2, f32[520,128]{1,0:T(8,128)} %copy-done, ...), custom_call_target="tpu_custom_call" | custom-call | tf_op jit(solution)/shard_map/pallas_call | solution.py:374
  52.0 3.1 %shard_map.141 = (f32[512,128]{1,0:T(8,128)}, f32[512,128]{1,0:T(8,128)S(1)}, f32[64,128]{1,0:T(8,128)S(1)}, f32[64,128]{1,0:T(8,128)S(1)}, f32[64,128]{1,0:T(8,128)S(1)}, /*index=5*/f32[64,128]{1,0:T(8,128)S(1)}) custom-call(f32[512,128]{1,0:T(8,128)} %bitcast.32, f32[1,128]{1,0:T(1,128)} %bitcast.40, f32[1,128]{1,0:T(1,128)} %bitcast.47, ...), custom_call_target="tpu_custom_call" | custom-call | tf_op jit(solution)/shard_map/pallas_call | solution.py:374
  55.8 5.1 %all-to-all-done.2 = f32[128,4,128]{2,1,0:T(4,128)S(1)} async-done(((f32[128,4,128]{2,1,0:T(4,128)}), f32[128,4,128]{2,1,0:T(4,128)S(1)}, u32[]{:S(2)}, u32[]{:S(2)}) %all-to-all-start.2) | async-done | bytes 262176 | tf_op jit(solution)/shard_map/all_to_all | solution.py:391
  60.9 1.3 %shard_map.144 = f32[1024,128]{1,0:T(8,128)} custom-call(f32[512,128]{1,0:T(8,128)S(1)} %bitcast.28, f32[1024,128]{1,0:T(8,128)S(1)} %bitcast.23), custom_call_target="tpu_custom_call" | custom-call | tf_op jit(solution)/shard_map/pallas_call | solution.py:374
  62.2 4.0 %all-to-all-start.3 = ((f32[32,32,128]{2,1,0:T(8,128)}), f32[32,32,128]{2,1,0:T(8,128)S(1)}, u32[]{:S(2)}, u32[]{:S(2)}) async-start(f32[32,32,128]{2,1,0:T(8,128)} %bitcast.14), calls=%async_computation.3 | async-start | bytes 1048576 | tf_op jit(solution)/shard_map/all_to_all | solution.py:391
  66.6 2.2 %collective-permute-start.4 = (f32[64,128]{1,0:T(8,128)S(1)}, f32[64,128]{1,0:T(8,128)S(1)}, u32[]{:S(2)}, u32[]{:S(2)}) collective-permute-start(f32[64,128]{1,0:T(8,128)S(1)} %get-tuple-element.76), channel_id=1, source_target_pairs={{0,8},{4,12},{8,0},{12,4},{1,9},{5,13},{9,1},{13,5},{2,10},{6,14},... | collective-permute-start | bytes 98312 | tf_op jit(solution)/shard_map/ppermute | solution.py:403
  68.7 1.1 %collective-permute-start.5 = (f32[64,128]{1,0:T(8,128)S(1)}, f32[64,128]{1,0:T(8,128)S(1)}, u32[]{:S(2)}, u32[]{:S(2)}) collective-permute-start(f32[64,128]{1,0:T(8,128)S(1)} %get-tuple-element.77), channel_id=1, source_target_pairs={{0,12},{4,0},{8,4},{12,8},{1,13},{5,1},{9,5},{13,9},{2,14},{6,2},{... | collective-permute-start | bytes 98312 | tf_op jit(solution)/shard_map/ppermute | solution.py:403
  69.9 1.9 %shard_map.145 = (bf16[2048,128]{1,0:T(8,128)(2,1)S(1)}, bf16[2048,128]{1,0:T(8,128)(2,1)S(1)}, f32[512,512]{1,0:T(8,128)S(1)}) custom-call(f32[1,128]{1,0:T(1,128)} %bitcast.41, f32[1,128]{1,0:T(1,128)} %bitcast.48, f32[128,640]{1,0:T(8,128)} %refs_1_.4, f32[640]{0:T(1024)} %refs_5_.2, ...), custom_call_target="tpu_custom_call", output_to_operand_aliasing={{0}: (5, {}), {1}: (6, {}), {2}: (7, {})} | custom-call | tf_op jit(solution)/shard_map/pallas_call | solution.py:374
  71.9 5.0 %all-to-all-done.3 = f32[32,32,128]{2,1,0:T(8,128)S(1)} async-done(((f32[32,32,128]{2,1,0:T(8,128)}), f32[32,32,128]{2,1,0:T(8,128)S(1)}, u32[]{:S(2)}, u32[]{:S(2)}) %all-to-all-start.3) | async-done | bytes 524320 | tf_op jit(solution)/shard_map/all_to_all | solution.py:391
  76.9 1.5 %shard_map.146 = f32[192,128]{1,0:T(8,128)} custom-call(f32[1024,128]{1,0:T(8,128)S(1)} %bitcast.24, f32[512,512]{1,0:T(8,128)S(1)} %get-tuple-element.71.factor_ref, bf16[2048,128]{1,0:T(8,128)(2,1)S(1)} %get-tuple-element.72.high_ref, bf16[2048,128]{1,0:T(8,128)(2,1)S(1)} %get-tuple-element.73.low_ref, f32[64,128]{1,0:T(8,128)S(1)} %get-tuple-element.74.refs_0_, ...), custom_call_target="tpu_custom_call" | custom-call | tf_op jit(solution)/shard_map/pallas_call | solution.py:374
  78.4 5.1 %all-to-all-start.4 = ((f32[96,2,128]{2,1,0:T(2,128)}), f32[96,2,128]{2,1,0:T(2,128)S(1)}, u32[]{:S(2)}, u32[]{:S(2)}) async-start(f32[96,2,128]{2,1,0:T(2,128)} %bitcast.16), calls=%async_computation.4 | async-start | bytes 196608 | tf_op jit(solution)/shard_map/all_to_all | solution.py:391
  84.0 2.2 %collective-permute-start.7 = (f32[256,128]{1,0:T(8,128)S(1)}, f32[256,128]{1,0:T(8,128)S(1)}, u32[]{:S(2)}, u32[]{:S(2)}) collective-permute-start(f32[256,128]{1,0:T(8,128)S(1)} %get-tuple-element.91), channel_id=1, source_target_pairs={{0,8},{4,12},{8,0},{12,4},{1,9},{5,13},{9,1},{13,5},{2,10},{6,14},... | collective-permute-start | bytes 393224 | tf_op jit(solution)/shard_map/ppermute | solution.py:403
  86.2 1.1 %collective-permute-start.8 = (f32[256,128]{1,0:T(8,128)S(1)}, f32[256,128]{1,0:T(8,128)S(1)}, u32[]{:S(2)}, u32[]{:S(2)}) collective-permute-start(f32[256,128]{1,0:T(8,128)S(1)} %get-tuple-element.92), channel_id=1, source_target_pairs={{0,12},{4,0},{8,4},{12,8},{1,13},{5,1},{9,5},{13,9},{2,14},{6,2},{... | collective-permute-start | bytes 393224 | tf_op jit(solution)/shard_map/ppermute | solution.py:403
  87.3 3.6 %all-to-all-done.4 = f32[96,2,128]{2,1,0:T(2,128)S(1)} async-done(((f32[96,2,128]{2,1,0:T(2,128)}), f32[96,2,128]{2,1,0:T(2,128)S(1)}, u32[]{:S(2)}, u32[]{:S(2)}) %all-to-all-start.4) | async-done | bytes 98336 | tf_op jit(solution)/shard_map/all_to_all | solution.py:391
  90.9 0.8 shard_map.150
  91.7 5.2 %all-to-all-start.5 = ((f32[384,2,128]{2,1,0:T(2,128)}), f32[384,2,128]{2,1,0:T(2,128)S(1)}, u32[]{:S(2)}, u32[]{:S(2)}) async-start(f32[384,2,128]{2,1,0:T(2,128)} %bitcast.20), calls=%async_computation.5 | async-start | bytes 786432 | tf_op jit(solution)/shard_map/all_to_all | solution.py:391
  96.9 2.0 %shard_map.147 = (f32[512,128]{1,0:T(8,128)S(1)}, f32[512,128]{1,0:T(8,128)S(1)}, f32[512,512]{1,0:T(8,128)S(1)}) custom-call(f32[512,128]{1,0:T(8,128)} %bitcast.33, s32[2,256]{1,0:T(2,128)} %refs_1_.3, f32[1,128]{1,0:T(1,128)} %bitcast.42, f32[1,128]{1,0:T(1,128)} %bitcast.49, f32[128,640]{1,0:T(8,128)} %refs_1_.4, f32[640]{0:T(1024)} %refs_5_.2), custom_call_target="tpu_custom_call" | custom-call | flops 10000000000 | bytes 10000000 | tf_op jit(solution)/shard_map/pallas_call | solution.py:374
  99.0 2.7 %shard_map.149 = f32[512,128]{1,0:T(8,128)} custom-call(f32[1,128]{1,0:T(1,128)} %bitcast.43, f32[128,640]{1,0:T(8,128)} %refs_1_.4, f32[512,128]{1,0:T(8,128)} %copy-done.1, f32[512,128]{1,0:T(8,128)S(1)} %get-tuple-element.85.refs_3_, f32[512,128]{1,0:T(8,128)S(1)} %get-tuple-element.86.refs_4_, f32[512,512]{1,0:T(8,128)S(1)} %get-tuple-element.87.refs_5_, ...), custom_call_target="tpu_custom_call" | custom-call | tf_op jit(solution)/shard_map/pallas_call | solution.py:374
  101.6 7.6 %all-to-all-done.5 = f32[384,2,128]{2,1,0:T(2,128)S(1)} async-done(((f32[384,2,128]{2,1,0:T(2,128)}), f32[384,2,128]{2,1,0:T(2,128)S(1)}, u32[]{:S(2)}, u32[]{:S(2)}) %all-to-all-start.5) | async-done | bytes 393248 | tf_op jit(solution)/shard_map/all_to_all | solution.py:391
  109.3 0.8 shard_map.151
  (20 shorter events, 1.8 us)
Async XLA Ops:
  3.3 30.2 %copy-start = (f32[520,128]{1,0:T(8,128)}, f32[520,128]{1,0:T(8,128)S(1)}, u32[]{:S(2)}) copy-start(f32[520,128]{1,0:T(8,128)S(1)} %get-tuple-element.58.refs_4_) | copy-start | bytes 798724
  3.3 25.2 %all-to-all-start = ((f32[128,8,128]{2,1,0:T(8,128)}), f32[128,8,128]{2,1,0:T(8,128)S(1)}, u32[]{:S(2)}, u32[]{:S(2)}) async-start(f32[128,8,128]{2,1,0:T(8,128)} %bitcast.7), calls=%async_computation | async-start | bytes 1048576 | tf_op jit(solution)/shard_map/all_to_all | solution.py:391
  14.9 20.1 %collective-permute-start = (f32[520,128]{1,0:T(8,128)S(1)}, f32[520,128]{1,0:T(8,128)}, u32[]{:S(2)}, u32[]{:S(2)}) collective-permute-start(f32[520,128]{1,0:T(8,128)S(1)} %get-tuple-element.58.refs_4_), channel_id=1, source_target_pairs={{4,0},{8,4},{12,8},{0,12},{5,1},{9,5},{13,9},{1,13},{6,2},{10,6},{... | collective-permute-start | bytes 798728 | tf_op jit(solution)/shard_map/ppermute | solution.py:399
  29.6 15.2 %all-to-all-start.1 = ((f32[128,4,128]{2,1,0:T(4,128)}), f32[128,4,128]{2,1,0:T(4,128)S(1)}, u32[]{:S(2)}, u32[]{:S(2)}) async-start(f32[128,4,128]{2,1,0:T(4,128)} %bitcast.9), calls=%async_computation.1 | async-start | bytes 524288 | tf_op jit(solution)/shard_map/all_to_all | solution.py:391
  33.5 16.1 %collective-permute-start.1 = (f32[520,128]{1,0:T(8,128)S(1)}, f32[520,128]{1,0:T(8,128)}, u32[]{:S(2)}, u32[]{:S(2)}) collective-permute-start(f32[520,128]{1,0:T(8,128)S(1)} %get-tuple-element.58.refs_4_), channel_id=1, source_target_pairs={{12,0},{0,4},{4,8},{8,12},{13,1},{1,5},{5,9},{9,13},{14,2},{2,6},{... | collective-permute-start | bytes 798728 | tf_op jit(solution)/shard_map/ppermute | solution.py:399
  35.0 20.8 %collective-permute-start.2 = (f32[520,128]{1,0:T(8,128)}, f32[520,128]{1,0:T(8,128)}, u32[]{:S(2)}, u32[]{:S(2)}) collective-permute-start(f32[520,128]{1,0:T(8,128)} %collective-permute-done.refs_5_), channel_id=1, source_target_pairs={{4,0},{8,4},{12,8},{0,12},{5,1},{9,5},{13,9},{1,13},{6,2},{10,6},{... | collective-permute-start | bytes 798728 | tf_op jit(solution)/shard_map/ppermute | solution.py:399
  38.6 7.0 %copy-start.2 = (f32[512,128]{1,0:T(8,128)}, f32[512,128]{1,0:T(8,128)S(1)}, u32[]{:S(2)}) copy-start(f32[512,128]{1,0:T(8,128)S(1)} %get-tuple-element.54.refs_11_) | copy-start | bytes 786436
  45.7 15.2 %all-to-all-start.2 = ((f32[128,4,128]{2,1,0:T(4,128)}), f32[128,4,128]{2,1,0:T(4,128)S(1)}, u32[]{:S(2)}, u32[]{:S(2)}) async-start(f32[128,4,128]{2,1,0:T(4,128)} %bitcast.12), calls=%async_computation.2 | async-start | bytes 524288 | tf_op jit(solution)/shard_map/all_to_all | solution.py:391
  49.6 2.4 %copy-start.3 = (f32[512,128]{1,0:T(8,128)S(1)}, f32[512,128]{1,0:T(8,128)}, u32[]{:S(2)}) copy-start(f32[512,128]{1,0:T(8,128)} %copy-done.2) | copy-start | bytes 786436
  55.1 0.7 copy-start.1
  62.2 14.7 %all-to-all-start.3 = ((f32[32,32,128]{2,1,0:T(8,128)}), f32[32,32,128]{2,1,0:T(8,128)S(1)}, u32[]{:S(2)}, u32[]{:S(2)}) async-start(f32[32,32,128]{2,1,0:T(8,128)} %bitcast.14), calls=%async_computation.3 | async-start | bytes 1048576 | tf_op jit(solution)/shard_map/all_to_all | solution.py:391
  66.1 5.6 %collective-permute-start.3 = (f32[64,128]{1,0:T(8,128)S(1)}, f32[64,128]{1,0:T(8,128)S(1)}, u32[]{:S(2)}, u32[]{:S(2)}) collective-permute-start(f32[64,128]{1,0:T(8,128)S(1)} %get-tuple-element.75), channel_id=1, source_target_pairs={{0,4},{4,8},{8,12},{12,0},{1,5},{5,9},{9,13},{13,1},{2,6},{6,10},{... | collective-permute-start | bytes 98312 | tf_op jit(solution)/shard_map/ppermute | solution.py:403
  66.6 5.2 %collective-permute-start.4 = (f32[64,128]{1,0:T(8,128)S(1)}, f32[64,128]{1,0:T(8,128)S(1)}, u32[]{:S(2)}, u32[]{:S(2)}) collective-permute-start(f32[64,128]{1,0:T(8,128)S(1)} %get-tuple-element.76), channel_id=1, source_target_pairs={{0,8},{4,12},{8,0},{12,4},{1,9},{5,13},{9,1},{13,5},{2,10},{6,14},... | collective-permute-start | bytes 98312 | tf_op jit(solution)/shard_map/ppermute | solution.py:403
  68.7 3.1 %collective-permute-start.5 = (f32[64,128]{1,0:T(8,128)S(1)}, f32[64,128]{1,0:T(8,128)S(1)}, u32[]{:S(2)}, u32[]{:S(2)}) collective-permute-start(f32[64,128]{1,0:T(8,128)S(1)} %get-tuple-element.77), channel_id=1, source_target_pairs={{0,12},{4,0},{8,4},{12,8},{1,13},{5,1},{9,5},{13,9},{2,14},{6,2},{... | collective-permute-start | bytes 98312 | tf_op jit(solution)/shard_map/ppermute | solution.py:403
  78.4 12.6 %all-to-all-start.4 = ((f32[96,2,128]{2,1,0:T(2,128)}), f32[96,2,128]{2,1,0:T(2,128)S(1)}, u32[]{:S(2)}, u32[]{:S(2)}) async-start(f32[96,2,128]{2,1,0:T(2,128)} %bitcast.16), calls=%async_computation.4 | async-start | bytes 196608 | tf_op jit(solution)/shard_map/all_to_all | solution.py:391
  83.6 15.3 %collective-permute-start.6 = (f32[256,128]{1,0:T(8,128)S(1)}, f32[256,128]{1,0:T(8,128)S(1)}, u32[]{:S(2)}, u32[]{:S(2)}) collective-permute-start(f32[256,128]{1,0:T(8,128)S(1)} %get-tuple-element.90), channel_id=1, source_target_pairs={{0,4},{4,8},{8,12},{12,0},{1,5},{5,9},{9,13},{13,1},{2,6},{6,10},{... | collective-permute-start | bytes 393224 | tf_op jit(solution)/shard_map/ppermute | solution.py:403
  84.0 14.9 %collective-permute-start.7 = (f32[256,128]{1,0:T(8,128)S(1)}, f32[256,128]{1,0:T(8,128)S(1)}, u32[]{:S(2)}, u32[]{:S(2)}) collective-permute-start(f32[256,128]{1,0:T(8,128)S(1)} %get-tuple-element.91), channel_id=1, source_target_pairs={{0,8},{4,12},{8,0},{12,4},{1,9},{5,13},{9,1},{13,5},{2,10},{6,14},... | collective-permute-start | bytes 393224 | tf_op jit(solution)/shard_map/ppermute | solution.py:403
  86.2 12.7 %collective-permute-start.8 = (f32[256,128]{1,0:T(8,128)S(1)}, f32[256,128]{1,0:T(8,128)S(1)}, u32[]{:S(2)}, u32[]{:S(2)}) collective-permute-start(f32[256,128]{1,0:T(8,128)S(1)} %get-tuple-element.92), channel_id=1, source_target_pairs={{0,12},{4,0},{8,4},{12,8},{1,13},{5,1},{9,5},{13,9},{2,14},{6,2},{... | collective-permute-start | bytes 393224 | tf_op jit(solution)/shard_map/ppermute | solution.py:403
  91.7 17.6 %all-to-all-start.5 = ((f32[384,2,128]{2,1,0:T(2,128)}), f32[384,2,128]{2,1,0:T(2,128)S(1)}, u32[]{:S(2)}, u32[]{:S(2)}) async-start(f32[384,2,128]{2,1,0:T(2,128)} %bitcast.20), calls=%async_computation.5 | async-start | bytes 786432 | tf_op jit(solution)/shard_map/all_to_all | solution.py:391
